TPU v7x, 256 devices: a whole 4x4x8 slice. The times are simulated.
256 devices in a mesh: gx: 8 (over x_lo, y), gy: 8 (over z), gz: 4 (over x_hi, core).
Axes of the slice: x: 4 (x_hi: 2, x_lo: 2; x = x_hi * 2 + x_lo), y: 4, z: 8, core: 2. Of those that a mesh axis runs over, the one named last changes fastest.
Arguments:
- checkpoint_store: bfloat16 [32, 9, 1, 64, 1024], P('gz', None, None, 'gy', 'gx'), may hold values from -6 to 6
- holder_peer: int32 [8, 8, 4, 8], P('gx', 'gy'), may hold values from 0 to 3, as said below
- holder_slot: int32 [8, 8, 4, 8], P('gx', 'gy'), may hold values from 0 to 7, as said below
- adjoint_state: float32 [9, 32, 64, 1024], P(None, 'gz', 'gy', 'gx'), may hold values from -6 to 6
- lame_lambda: float32 [32, 64, 1024], P('gz', 'gy', 'gx'), may hold values from 0.1 to 0.3
- lame_mu: float32 [32, 64, 1024], P('gz', 'gy', 'gx'), may hold values from 0.05 to 0.15
- buoyancy: float32 [32, 64, 1024], P('gz', 'gy', 'gx'), may hold values from 0.25 to 0.5
- source_cell: int32 [4, 8, 8, 4], P('gz', 'gy', 'gx'), may hold values from 0 to 8191
- wavelet: float32 [64], replicated, may hold values from -6 to 6
- receiver_cell: int32 [4, 8, 8, 64], P('gz', 'gy', 'gx'), may hold values from 0 to 8191
- traces: float32 [4, 8, 8, 64, 64], P('gz', 'gy', 'gx'), may hold values from -6 to 6
- plan: int32 [2], replicated, may hold values from 0 to 63
Outputs:
- adjoint_final: float32 [9, 32, 64, 1024], P(None, 'gz', 'gy', 'gx')
- image_lambda: float32 [32, 64, 1024], P('gz', 'gy', 'gx')
- image_mu: float32 [32, 64, 1024], P('gz', 'gy', 'gx')
Inputs may be any that keep to these rules, and one draw needn't show every extreme that they name: `holder_peer`: within each group of bricks sharing x and y bricks, every holder's 8 slots hold exactly one piece each; for every brick one holder supplies exactly 5 of its pieces and each other holder exactly one. `holder_slot`: slots of one holder are distinct over the pieces it holds.
All inputs are finite; a program needn't handle non-finite values.
Results may differ from a plain program's by a relative error of at most 0.0003.
Values may be sent and summed in bfloat16 or wider, within the bound.
A program may use at most 128 MiB of HBM per device.

v0:
```python
import jax
import jax.numpy as jnp
from jax import lax
from jax.sharding import PartitionSpec as P

STEPS = 2


along_z = 0
along_y = 1
along_x = 2


def padded_2(cells, sides, width):
    for axis, dim in sides:
        count = lax.axis_size(axis)
        ends = count - 1
        head = lax.slice_in_dim(cells, 0, width, axis=dim)
        tail = lax.slice_in_dim(cells, cells.shape[dim] - width, cells.shape[dim], axis=dim)
        cells = jnp.concatenate(
            [
                lax.ppermute(tail, axis, [(i, (i + 1) % count) for i in range(ends)]),
                cells,
                lax.ppermute(head, axis, [((i + 1) % count, i) for i in range(ends)]),
            ],
            axis=dim,
        )
    return cells


def shifted(padded, which_axis, offset):
    extents = padded.shape[-3:]
    starts = [1, 1, 1]
    starts[which_axis] = 1 + offset
    return padded[
        ...,
        starts[0] : starts[0] + extents[0] - 2,
        starts[1] : starts[1] + extents[1] - 2,
        starts[2] : starts[2] + extents[2] - 2,
    ]


def ahead(padded, which_axis):
    return shifted(padded, which_axis, 1) - shifted(padded, which_axis, 0)


def behind(padded, which_axis):
    return shifted(padded, which_axis, 0) - shifted(padded, which_axis, -1)


def velocity_rates(stress_pad, buoyancy):
    rate_x = buoyancy * (
        ahead(stress_pad[0], along_x)
        + behind(stress_pad[3], along_y)
        + behind(stress_pad[4], along_z)
    )
    rate_y = buoyancy * (
        behind(stress_pad[3], along_x)
        + ahead(stress_pad[1], along_y)
        + behind(stress_pad[5], along_z)
    )
    rate_z = buoyancy * (
        behind(stress_pad[4], along_x)
        + behind(stress_pad[5], along_y)
        + ahead(stress_pad[2], along_z)
    )
    return jnp.stack([rate_x, rate_y, rate_z])


def stress_rates(velocity_pad, lame_lambda, lame_mu):
    strain_xx = behind(velocity_pad[0], along_x)
    strain_yy = behind(velocity_pad[1], along_y)
    strain_zz = behind(velocity_pad[2], along_z)
    dilation = strain_xx + strain_yy + strain_zz
    rate_xx = lame_lambda * dilation + 2.0 * lame_mu * strain_xx
    rate_yy = lame_lambda * dilation + 2.0 * lame_mu * strain_yy
    rate_zz = lame_lambda * dilation + 2.0 * lame_mu * strain_zz
    rate_xy = lame_mu * (ahead(velocity_pad[0], along_y) + ahead(velocity_pad[1], along_x))
    rate_xz = lame_mu * (ahead(velocity_pad[0], along_z) + ahead(velocity_pad[2], along_x))
    rate_yz = lame_mu * (ahead(velocity_pad[1], along_z) + ahead(velocity_pad[2], along_y))
    return jnp.stack([rate_xx, rate_yy, rate_zz, rate_xy, rate_xz, rate_yz])


def imaging_terms(forward_stress, adjoint_stress):
    pressure_fwd = forward_stress[0] + forward_stress[1] + forward_stress[2]
    pressure_adj = adjoint_stress[0] + adjoint_stress[1] + adjoint_stress[2]
    term_lambda = pressure_fwd * pressure_adj
    term_mu = (
        forward_stress[0] * adjoint_stress[0]
        + forward_stress[1] * adjoint_stress[1]
        + forward_stress[2] * adjoint_stress[2]
        + 2.0
        * (
            forward_stress[3] * adjoint_stress[3]
            + forward_stress[4] * adjoint_stress[4]
            + forward_stress[5] * adjoint_stress[5]
        )
    )
    return (term_lambda, term_mu)


def stress_rim(stress):
    return padded_2(stress, (("gx", 3), ("gy", 2), ("gz", 1)), 1)


def velocity_rim(velocity):
    return padded_2(velocity, (("gx", 3), ("gy", 2), ("gz", 1)), 1)


def inject(stress, cells, values):
    normal = stress[:3]
    flat = normal.reshape(3, -1).at[:, cells].add(values).reshape(normal.shape)
    return jnp.concatenate([flat, stress[3:]], axis=0)


def restore(checkpoint_store, holder_peer, holder_slot):
    pieces = holder_peer.shape[-1]
    layers = checkpoint_store.shape[2]
    peer_table = holder_peer[0, 0]
    slot_table = holder_slot[0, 0]
    position = lax.axis_index("gz")
    my_peers = lax.dynamic_index_in_dim(peer_table, position, 0, keepdims=False)
    my_slots = lax.dynamic_index_in_dim(slot_table, position, 0, keepdims=False)
    everything = lax.all_gather(checkpoint_store, "gz", axis=0, tiled=True)
    rows = everything[my_peers * pieces + my_slots]
    restored = jnp.transpose(rows, (1, 0, 2, 3, 4)).reshape((9, pieces * layers) + rows.shape[-2:])
    return restored.astype(jnp.float32)


def on_device(
    checkpoint_store,
    holder_peer,
    holder_slot,
    adjoint_state,
    lame_lambda,
    lame_mu,
    buoyancy,
    source_cell,
    wavelet,
    receiver_cell,
    traces,
    plan,
):
    source_flat = source_cell.reshape(-1)
    receiver_flat = receiver_cell.reshape(-1)
    trace_rows = traces.reshape(traces.shape[-2], traces.shape[-1])
    state = restore(checkpoint_store, holder_peer, holder_slot)
    adjoint = adjoint_state
    snapshots = [state[3:]]
    injected = {}
    for step_now in range(STEPS):
        velocity = state[:3] + velocity_rates(stress_rim(state[3:]), buoyancy)
        stress = state[3:] + stress_rates(velocity_rim(velocity), lame_lambda, lame_mu)
        stress = inject(stress, source_flat, wavelet[plan[step_now]])
        state = jnp.concatenate([velocity, stress], axis=0)
        snapshots.append(stress)
    for step_now in reversed(range(STEPS)):
        stress = inject(adjoint[3:], receiver_flat, trace_rows[plan[step_now]])
        injected[step_now] = stress
        stress = stress - stress_rates(velocity_rim(adjoint[:3]), lame_lambda, lame_mu)
        velocity = adjoint[:3] - velocity_rates(stress_rim(stress), buoyancy)
        adjoint = jnp.concatenate([velocity, stress], axis=0)
    image_lambda = jnp.zeros(lame_mu.shape, jnp.float32)
    image_mu = jnp.zeros(lame_mu.shape, jnp.float32)
    for step_now in reversed(range(STEPS)):
        term_lambda, term_mu = imaging_terms(snapshots[step_now + 1], injected[step_now])
        image_lambda = image_lambda + term_lambda
        image_mu = image_mu + term_mu
    return (adjoint, image_lambda, image_mu)


def solution(mesh):
    return jax.shard_map(
        on_device,
        mesh=mesh,
        in_specs=(
            P("gz", None, None, "gy", "gx"),
            P("gx", "gy", None, None),
            P("gx", "gy", None, None),
            P(None, "gz", "gy", "gx"),
            P("gz", "gy", "gx"),
            P("gz", "gy", "gx"),
            P("gz", "gy", "gx"),
            P("gz", "gy", "gx", None),
            P(),
            P("gz", "gy", "gx", None),
            P("gz", "gy", "gx", None, None),
            P(),
        ),
        out_specs=(P(None, "gz", "gy", "gx"), P("gz", "gy", "gx"), P("gz", "gy", "gx")),
        check_vma=False,
    )
```

profile of v0, /device:TPU:131, one launch (start us, length us, event | category | flops | bytes accessed | tf_op | source)
XLA Modules:
  0.0 287.1 jit_solution(10211413250516954154)
XLA Ops:
  9.8 9.5 %all_gather.3 = bf16[32,9,1,8,128]{4,3,2,1,0:T(8,128)(2,1)S(1)} all-gather(bf16[8,9,1,8,128]{4,3,2,1,0:T(8,128)(2,1)} %param.12), channel_id=1, replica_groups=mesh['gx'=8,'gy'=8,'gz'=4] {'gz'}, dimensions={0}, use_global_device_ids=true | all-gather | bytes 737280 | tf_op jit(solution)/shard_map/all_gather | solution.py:124
  22.0 5.5 %collective-permute-start.25 = (f32[6,8,8,1]{3,2,0,1:T(8,128)S(1)}, f32[6,8,8,1]{3,2,0,1:T(8,128)S(1)}, u32[]{:S(2)}, u32[]{:S(2)}) collective-permute-start(f32[6,8,8,1]{3,2,0,1:T(8,128)S(1)} %get-tuple-element.79), channel_id=1, source_target_pairs={{32,0},{64,32},{96,64},{128,96},{160,128},{192,160},{224,192},{33,... | collective-permute-start | bytes 4616 | tf_op jit(solution)/shard_map/ppermute | solution.py:24
  45.3 5.1 %scatter_custom_fusion = f32[3,8192]{0,1:T(8,128)} fusion(f32[3,8192]{0,1:T(8,128)} %bitcast.236, s32[64]{0:T(128)S(1)} %fusion.111, f32[64]{0:T(128)S(1)} %get-tuple-element.128), kind=kCustom, calls=%fused_computation.342 | custom fusion | flops 192 | bytes 98816 | tf_op jit(solution)/shard_map/scatter-add | solution.py:112
  54.0 4.9 %collective-permute-start.28 = (f32[6,1,10,130]{3,2,1,0:T(8,128)S(1)}, f32[6,1,10,130]{3,2,1,0:T(8,128)S(1)}, u32[]{:S(2)}, u32[]{:S(2)}) collective-permute-start(f32[6,1,10,130]{3,2,1,0:T(8,128)S(1)} %get-tuple-element.40), channel_id=1, source_target_pairs={{0,1},{1,2},{2,3},{4,5},{5,6},{6,7},{8,9},{9,10},{10,11},{12,13},{... | collective-permute-start | bytes 93608 | tf_op jit(solution)/shard_map/ppermute | solution.py:22
  63.0 4.6 %collective-permute-start.3 = (f32[3,8,1,130]{3,2,1,0:T(1,128)S(1)}, f32[3,8,1,130]{3,2,1,0:T(1,128)S(1)}, u32[]{:S(2)}, u32[]{:S(2)}) collective-permute-start(f32[3,8,1,130]{3,2,1,0:T(1,128)S(1)} %get-tuple-element.86), channel_id=1, source_target_pairs={{4,0},{8,4},{12,8},{16,12},{20,16},{24,20},{28,24},{5,1},{9,5},{13... | collective-permute-start | bytes 37448 | tf_op jit(solution)/shard_map/ppermute | solution.py:24
  70.4 5.5 %collective-permute-start.31 = (f32[3,8,8,1]{3,2,1,0:T(8,128)S(1)}, f32[3,8,8,1]{3,2,1,0:T(8,128)S(1)}, u32[]{:S(2)}, u32[]{:S(2)}) collective-permute-start(f32[3,8,8,1]{3,2,1,0:T(8,128)S(1)} %get-tuple-element.116), channel_id=1, source_target_pairs={{32,0},{64,32},{96,64},{128,96},{160,128},{192,160},{224,192},{33,... | collective-permute-start | bytes 2312 | tf_op jit(solution)/shard_map/ppermute | solution.py:24
  76.0 6.3 %collective-permute-start.4 = (f32[3,1,10,130]{3,2,1,0:T(8,128)S(1)}, f32[3,1,10,130]{3,2,1,0:T(8,128)S(1)}, u32[]{:S(2)}, u32[]{:S(2)}) collective-permute-start(f32[3,1,10,130]{3,2,1,0:T(8,128)S(1)} %get-tuple-element.72), channel_id=1, source_target_pairs={{0,1},{1,2},{2,3},{4,5},{5,6},{6,7},{8,9},{9,10},{10,11},{12,13},{... | collective-permute-start | bytes 46808 | tf_op jit(solution)/shard_map/ppermute | solution.py:22
  92.0 6.3 %collective-permute-start.34 = (f32[3,1,10,130]{3,2,1,0:T(8,128)S(1)}, f32[3,1,10,130]{3,2,1,0:T(8,128)S(1)}, u32[]{:S(2)}, u32[]{:S(2)}) collective-permute-start(f32[3,1,10,130]{3,2,1,0:T(8,128)S(1)} %get-tuple-element.68), channel_id=1, source_target_pairs={{0,1},{1,2},{2,3},{4,5},{5,6},{6,7},{8,9},{9,10},{10,11},{12,13},{... | collective-permute-start | bytes 46808 | tf_op jit(solution)/shard_map/ppermute | solution.py:22
  100.2 4.9 %collective-permute-done.35 = f32[3,1,10,130]{3,2,1,0:T(8,128)S(1)} collective-permute-done((f32[3,1,10,130]{3,2,1,0:T(8,128)S(1)}, f32[3,1,10,130]{3,2,1,0:T(8,128)S(1)}, u32[]{:S(2)}, u32[]{:S(2)}) %collective-permute-start.35) | collective-permute-done | bytes 15632 | tf_op jit(solution)/shard_map/ppermute | solution.py:24
  108.7 5.5 %collective-permute-start.7 = (f32[6,8,8,1]{3,2,1,0:T(8,128)S(1)}, f32[6,8,8,1]{3,2,1,0:T(8,128)S(1)}, u32[]{:S(2)}, u32[]{:S(2)}) collective-permute-start(f32[6,8,8,1]{3,2,1,0:T(8,128)S(1)} %get-tuple-element.110), channel_id=1, source_target_pairs={{32,0},{64,32},{96,64},{128,96},{160,128},{192,160},{224,192},{33,... | collective-permute-start | bytes 4616 | tf_op jit(solution)/shard_map/ppermute | solution.py:24
  116.9 5.4 %scatter_custom_fusion.2 = f32[3,8192]{0,1:T(8,128)} fusion(f32[3,8192]{0,1:T(8,128)} %bitcast.238, s32[4]{0:T(128)S(1)} %fusion.113, f32[]{:T(128)} %bitcast.77), kind=kCustom, calls=%fused_computation.351 | custom fusion | flops 12 | bytes 98816 | tf_op jit(solution)/shard_map/scatter-add | solution.py:112
  128.1 5.2 %scatter_custom_fusion.1 = f32[3,8192]{0,1:T(8,128)} fusion(f32[3,8192]{0,1:T(8,128)} %bitcast.234, s32[64]{0:T(128)S(1)} %fusion.111, f32[64]{0:T(128)S(1)} %get-tuple-element.127), kind=kCustom, calls=%fused_computation.340 | custom fusion | flops 192 | bytes 98816 | tf_op jit(solution)/shard_map/scatter-add | solution.py:112
  138.2 5.5 %collective-permute-start.37 = (f32[6,8,8,1]{3,2,1,0:T(8,128)S(1)}, f32[6,8,8,1]{3,2,1,0:T(8,128)S(1)}, u32[]{:S(2)}, u32[]{:S(2)}) collective-permute-start(f32[6,8,8,1]{3,2,1,0:T(8,128)S(1)} %get-tuple-element.93), channel_id=1, source_target_pairs={{32,0},{64,32},{96,64},{128,96},{160,128},{192,160},{224,192},{33,... | collective-permute-start | bytes 4616 | tf_op jit(solution)/shard_map/ppermute | solution.py:24
  146.0 5.1 %collective-permute-start.9 = (f32[6,8,1,130]{3,2,1,0:T(1,128)S(1)}, f32[6,8,1,130]{3,2,1,0:T(1,128)S(1)}, u32[]{:S(2)}, u32[]{:S(2)}) collective-permute-start(f32[6,8,1,130]{3,2,1,0:T(1,128)S(1)} %get-tuple-element.53), channel_id=1, source_target_pairs={{4,0},{8,4},{12,8},{16,12},{20,16},{24,20},{28,24},{5,1},{9,5},{13... | collective-permute-start | bytes 74888 | tf_op jit(solution)/shard_map/ppermute | solution.py:24
  164.1 5.1 %collective-permute-start.40 = (f32[6,1,10,130]{3,2,1,0:T(8,128)S(1)}, f32[6,1,10,130]{3,2,1,0:T(8,128)S(1)}, u32[]{:S(2)}, u32[]{:S(2)}) collective-permute-start(f32[6,1,10,130]{3,2,1,0:T(8,128)S(1)} %get-tuple-element.38), channel_id=1, source_target_pairs={{0,1},{1,2},{2,3},{4,5},{5,6},{6,7},{8,9},{9,10},{10,11},{12,13},{... | collective-permute-start | bytes 93608 | tf_op jit(solution)/shard_map/ppermute | solution.py:22
  174.0 5.5 %collective-permute-start.13 = (f32[3,8,8,1]{3,2,1,0:T(8,128)S(1)}, f32[3,8,8,1]{3,2,1,0:T(8,128)S(1)}, u32[]{:S(2)}, u32[]{:S(2)}) collective-permute-start(f32[3,8,8,1]{3,2,1,0:T(8,128)S(1)} %get-tuple-element.118), channel_id=1, source_target_pairs={{32,0},{64,32},{96,64},{128,96},{160,128},{192,160},{224,192},{33,... | collective-permute-start | bytes 2312 | tf_op jit(solution)/shard_map/ppermute | solution.py:24
  182.2 5.5 %collective-permute-start.43 = (f32[3,8,8,1]{3,2,0,1:T(8,128)S(1)}, f32[3,8,8,1]{3,2,0,1:T(8,128)S(1)}, u32[]{:S(2)}, u32[]{:S(2)}) collective-permute-start(f32[3,8,8,1]{3,2,0,1:T(8,128)S(1)} %get-tuple-element.114), channel_id=1, source_target_pairs={{32,0},{64,32},{96,64},{128,96},{160,128},{192,160},{224,192},{33,... | collective-permute-start | bytes 2312 | tf_op jit(solution)/shard_map/ppermute | solution.py:24
  201.5 7.4 %collective-permute-start.16 = (f32[3,1,10,130]{3,2,1,0:T(8,128)S(1)}, f32[3,1,10,130]{3,2,1,0:T(8,128)S(1)}, u32[]{:S(2)}, u32[]{:S(2)}) collective-permute-start(f32[3,1,10,130]{3,2,1,0:T(8,128)S(1)} %get-tuple-element.70), channel_id=1, source_target_pairs={{0,1},{1,2},{2,3},{4,5},{5,6},{6,7},{8,9},{9,10},{10,11},{12,13},{... | collective-permute-start | bytes 46808 | tf_op jit(solution)/shard_map/ppermute | solution.py:22
  210.9 5.1 %collective-permute-start.46 = (f32[3,1,10,130]{3,2,0,1:T(8,128)S(1)}, f32[3,1,10,130]{3,2,0,1:T(8,128)S(1)}, u32[]{:S(2)}, u32[]{:S(2)}) collective-permute-start(f32[3,1,10,130]{3,2,0,1:T(8,128)S(1)} %get-tuple-element.66), channel_id=1, source_target_pairs={{0,1},{1,2},{2,3},{4,5},{5,6},{6,7},{8,9},{9,10},{10,11},{12,13},{... | collective-permute-start | bytes 46808 | tf_op jit(solution)/shard_map/ppermute | solution.py:22
  218.3 4.7 %collective-permute-done.47 = f32[3,1,10,130]{3,2,0,1:T(8,128)S(1)} collective-permute-done((f32[3,1,10,130]{3,2,0,1:T(8,128)S(1)}, f32[3,1,10,130]{3,2,0,1:T(8,128)S(1)}, u32[]{:S(2)}, u32[]{:S(2)}) %collective-permute-start.47) | collective-permute-done | bytes 15632 | tf_op jit(solution)/shard_map/ppermute | solution.py:24
  226.5 5.5 %collective-permute-start.19 = (f32[6,8,8,1]{3,2,1,0:T(8,128)S(1)}, f32[6,8,8,1]{3,2,1,0:T(8,128)S(1)}, u32[]{:S(2)}, u32[]{:S(2)}) collective-permute-start(f32[6,8,8,1]{3,2,1,0:T(8,128)S(1)} %get-tuple-element.103), channel_id=1, source_target_pairs={{32,0},{64,32},{96,64},{128,96},{160,128},{192,160},{224,192},{33,... | collective-permute-start | bytes 4616 | tf_op jit(solution)/shard_map/ppermute | solution.py:24
  234.6 5.4 %scatter_custom_fusion.3 = f32[3,8192]{0,1:T(8,128)} fusion(f32[3,8192]{0,1:T(8,128)} %bitcast.240, s32[4]{0:T(128)S(1)} %fusion.113, f32[]{:T(128)} %bitcast.98), kind=kCustom, calls=%fused_computation.349 | custom fusion | flops 12 | bytes 98816 | tf_op jit(solution)/shard_map/scatter-add | solution.py:112
  246.9 28.2 %add_reduce_fusion.1 = (f32[8192]{0:T(1024)S(1)}, f32[8192]{0:T(1024)}, f32[8192]{0:T(1024)S(1)}) fusion(f32[3,8192]{0,1:T(8,128)} %scatter_custom_fusion, f32[3,8192]{0,1:T(8,128)} %scatter_custom_fusion.3, f32[3,8192]{0,1:T(8,128)} %scatter_custom_fusion.1, f32[3,8192]{0,1:T(8,128)} %scatter_custom_fusion.2), kind=kLoop, calls=%fused_computation.6 | loop fusion | flops 172032 | bytes 491520 | tf_op jit(solution)/shard_map/add | solution.py:89
  280.8 4.9 %collective-permute-done.23 = f32[6,1,10,130]{3,2,1,0:T(8,128)S(1)} collective-permute-done((f32[6,1,10,130]{3,2,1,0:T(8,128)S(1)}, f32[6,1,10,130]{3,2,1,0:T(8,128)S(1)}, u32[]{:S(2)}, u32[]{:S(2)}) %collective-permute-start.23) | collective-permute-done | bytes 31232 | tf_op jit(solution)/shard_map/ppermute | solution.py:24
  (182 shorter events, 125.0 us)
Async XLA Ops:
  1.7 59.2 %collective-permute-start = (f32[3,8,8,1]{3,2,1,0:T(8,128)S(1)}, f32[3,8,8,1]{3,2,1,0:T(8,128)S(1)}, u32[]{:S(2)}, u32[]{:S(2)}) collective-permute-start(f32[3,8,8,1]{3,2,1,0:T(8,128)S(1)} %get-tuple-element.87), channel_id=1, source_target_pairs={{0,32},{32,64},{64,96},{96,128},{128,160},{160,192},{192,224},{1,3... | collective-permute-start | bytes 2312 | tf_op jit(solution)/shard_map/ppermute | solution.py:22
  4.9 56.0 %collective-permute-start.1 = (f32[3,8,8,1]{3,2,1,0:T(8,128)S(1)}, f32[3,8,8,1]{3,2,1,0:T(8,128)S(1)}, u32[]{:S(2)}, u32[]{:S(2)}) collective-permute-start(f32[3,8,8,1]{3,2,1,0:T(8,128)S(1)} %get-tuple-element.88), channel_id=1, source_target_pairs={{32,0},{64,32},{96,64},{128,96},{160,128},{192,160},{224,192},{33,... | collective-permute-start | bytes 2312 | tf_op jit(solution)/shard_map/ppermute | solution.py:24
  20.0 15.0 %collective-permute-start.24 = (f32[6,8,8,1]{3,2,0,1:T(8,128)S(1)}, f32[6,8,8,1]{3,2,0,1:T(8,128)S(1)}, u32[]{:S(2)}, u32[]{:S(2)}) collective-permute-start(f32[6,8,8,1]{3,2,0,1:T(8,128)S(1)} %get-tuple-element.78), channel_id=1, source_target_pairs={{0,32},{32,64},{64,96},{96,128},{128,160},{160,192},{192,224},{1,3... | collective-permute-start | bytes 4616 | tf_op jit(solution)/shard_map/ppermute | solution.py:22
  35.4 18.4 %collective-permute-start.26 = (f32[6,8,1,130]{3,2,1,0:T(1,128)S(1)}, f32[6,8,1,130]{3,2,1,0:T(1,128)S(1)}, u32[]{:S(2)}, u32[]{:S(2)}) collective-permute-start(f32[6,8,1,130]{3,2,1,0:T(1,128)S(1)} %get-tuple-element.48), channel_id=1, source_target_pairs={{0,4},{4,8},{8,12},{12,16},{16,20},{20,24},{24,28},{1,5},{5,9},{9,... | collective-permute-start | bytes 74888 | tf_op jit(solution)/shard_map/ppermute | solution.py:22
  38.0 15.8 %collective-permute-start.27 = (f32[6,8,1,130]{3,2,1,0:T(1,128)S(1)}, f32[6,8,1,130]{3,2,1,0:T(1,128)S(1)}, u32[]{:S(2)}, u32[]{:S(2)}) collective-permute-start(f32[6,8,1,130]{3,2,1,0:T(1,128)S(1)} %get-tuple-element.49), channel_id=1, source_target_pairs={{4,0},{8,4},{12,8},{16,12},{20,16},{24,20},{28,24},{5,1},{9,5},{13... | collective-permute-start | bytes 74888 | tf_op jit(solution)/shard_map/ppermute | solution.py:24
  54.0 13.6 %collective-permute-start.28 = (f32[6,1,10,130]{3,2,1,0:T(8,128)S(1)}, f32[6,1,10,130]{3,2,1,0:T(8,128)S(1)}, u32[]{:S(2)}, u32[]{:S(2)}) collective-permute-start(f32[6,1,10,130]{3,2,1,0:T(8,128)S(1)} %get-tuple-element.40), channel_id=1, source_target_pairs={{0,1},{1,2},{2,3},{4,5},{5,6},{6,7},{8,9},{9,10},{10,11},{12,13},{... | collective-permute-start | bytes 93608 | tf_op jit(solution)/shard_map/ppermute | solution.py:22
  61.1 14.8 %collective-permute-start.2 = (f32[3,8,1,130]{3,2,1,0:T(1,128)S(1)}, f32[3,8,1,130]{3,2,1,0:T(1,128)S(1)}, u32[]{:S(2)}, u32[]{:S(2)}) collective-permute-start(f32[3,8,1,130]{3,2,1,0:T(1,128)S(1)} %get-tuple-element.85), channel_id=1, source_target_pairs={{0,4},{4,8},{8,12},{12,16},{16,20},{20,24},{24,28},{1,5},{5,9},{9,... | collective-permute-start | bytes 37448 | tf_op jit(solution)/shard_map/ppermute | solution.py:22
  68.4 15.7 %collective-permute-start.30 = (f32[3,8,8,1]{3,2,1,0:T(8,128)S(1)}, f32[3,8,8,1]{3,2,1,0:T(8,128)S(1)}, u32[]{:S(2)}, u32[]{:S(2)}) collective-permute-start(f32[3,8,8,1]{3,2,1,0:T(8,128)S(1)} %get-tuple-element.115), channel_id=1, source_target_pairs={{0,32},{32,64},{64,96},{96,128},{128,160},{160,192},{192,224},{1,3... | collective-permute-start | bytes 2312 | tf_op jit(solution)/shard_map/ppermute | solution.py:22
  70.4 13.8 %collective-permute-start.31 = (f32[3,8,8,1]{3,2,1,0:T(8,128)S(1)}, f32[3,8,8,1]{3,2,1,0:T(8,128)S(1)}, u32[]{:S(2)}, u32[]{:S(2)}) collective-permute-start(f32[3,8,8,1]{3,2,1,0:T(8,128)S(1)} %get-tuple-element.116), channel_id=1, source_target_pairs={{32,0},{64,32},{96,64},{128,96},{160,128},{192,160},{224,192},{33,... | collective-permute-start | bytes 2312 | tf_op jit(solution)/shard_map/ppermute | solution.py:24
  76.0 15.0 %collective-permute-start.4 = (f32[3,1,10,130]{3,2,1,0:T(8,128)S(1)}, f32[3,1,10,130]{3,2,1,0:T(8,128)S(1)}, u32[]{:S(2)}, u32[]{:S(2)}) collective-permute-start(f32[3,1,10,130]{3,2,1,0:T(8,128)S(1)} %get-tuple-element.72), channel_id=1, source_target_pairs={{0,1},{1,2},{2,3},{4,5},{5,6},{6,7},{8,9},{9,10},{10,11},{12,13},{... | collective-permute-start | bytes 46808 | tf_op jit(solution)/shard_map/ppermute | solution.py:22
  106.8 36.8 %collective-permute-start.6 = (f32[6,8,8,1]{3,2,1,0:T(8,128)S(1)}, f32[6,8,8,1]{3,2,1,0:T(8,128)S(1)}, u32[]{:S(2)}, u32[]{:S(2)}) collective-permute-start(f32[6,8,8,1]{3,2,1,0:T(8,128)S(1)} %get-tuple-element.109), channel_id=1, source_target_pairs={{0,32},{32,64},{64,96},{96,128},{128,160},{160,192},{192,224},{1,3... | collective-permute-start | bytes 4616 | tf_op jit(solution)/shard_map/ppermute | solution.py:22
  108.7 34.9 %collective-permute-start.7 = (f32[6,8,8,1]{3,2,1,0:T(8,128)S(1)}, f32[6,8,8,1]{3,2,1,0:T(8,128)S(1)}, u32[]{:S(2)}, u32[]{:S(2)}) collective-permute-start(f32[6,8,8,1]{3,2,1,0:T(8,128)S(1)} %get-tuple-element.110), channel_id=1, source_target_pairs={{32,0},{64,32},{96,64},{128,96},{160,128},{192,160},{224,192},{33,... | collective-permute-start | bytes 4616 | tf_op jit(solution)/shard_map/ppermute | solution.py:24
  136.1 15.0 %collective-permute-start.36 = (f32[6,8,8,1]{3,2,1,0:T(8,128)S(1)}, f32[6,8,8,1]{3,2,1,0:T(8,128)S(1)}, u32[]{:S(2)}, u32[]{:S(2)}) collective-permute-start(f32[6,8,8,1]{3,2,1,0:T(8,128)S(1)} %get-tuple-element.92), channel_id=1, source_target_pairs={{0,32},{32,64},{64,96},{96,128},{128,160},{160,192},{192,224},{1,3... | collective-permute-start | bytes 4616 | tf_op jit(solution)/shard_map/ppermute | solution.py:22
  144.0 14.0 %collective-permute-start.8 = (f32[6,8,1,130]{3,2,1,0:T(1,128)S(1)}, f32[6,8,1,130]{3,2,1,0:T(1,128)S(1)}, u32[]{:S(2)}, u32[]{:S(2)}) collective-permute-start(f32[6,8,1,130]{3,2,1,0:T(1,128)S(1)} %get-tuple-element.52), channel_id=1, source_target_pairs={{0,4},{4,8},{8,12},{12,16},{16,20},{20,24},{24,28},{1,5},{5,9},{9,... | collective-permute-start | bytes 74888 | tf_op jit(solution)/shard_map/ppermute | solution.py:22
  164.1 15.3 %collective-permute-start.40 = (f32[6,1,10,130]{3,2,1,0:T(8,128)S(1)}, f32[6,1,10,130]{3,2,1,0:T(8,128)S(1)}, u32[]{:S(2)}, u32[]{:S(2)}) collective-permute-start(f32[6,1,10,130]{3,2,1,0:T(8,128)S(1)} %get-tuple-element.38), channel_id=1, source_target_pairs={{0,1},{1,2},{2,3},{4,5},{5,6},{6,7},{8,9},{9,10},{10,11},{12,13},{... | collective-permute-start | bytes 93608 | tf_op jit(solution)/shard_map/ppermute | solution.py:22
  172.0 15.6 %collective-permute-start.12 = (f32[3,8,8,1]{3,2,1,0:T(8,128)S(1)}, f32[3,8,8,1]{3,2,1,0:T(8,128)S(1)}, u32[]{:S(2)}, u32[]{:S(2)}) collective-permute-start(f32[3,8,8,1]{3,2,1,0:T(8,128)S(1)} %get-tuple-element.117), channel_id=1, source_target_pairs={{0,32},{32,64},{64,96},{96,128},{128,160},{160,192},{192,224},{1,3... | collective-permute-start | bytes 2312 | tf_op jit(solution)/shard_map/ppermute | solution.py:22
  174.0 13.7 %collective-permute-start.13 = (f32[3,8,8,1]{3,2,1,0:T(8,128)S(1)}, f32[3,8,8,1]{3,2,1,0:T(8,128)S(1)}, u32[]{:S(2)}, u32[]{:S(2)}) collective-permute-start(f32[3,8,8,1]{3,2,1,0:T(8,128)S(1)} %get-tuple-element.118), channel_id=1, source_target_pairs={{32,0},{64,32},{96,64},{128,96},{160,128},{192,160},{224,192},{33,... | collective-permute-start | bytes 2312 | tf_op jit(solution)/shard_map/ppermute | solution.py:24
  180.2 14.2 %collective-permute-start.42 = (f32[3,8,8,1]{3,2,0,1:T(8,128)S(1)}, f32[3,8,8,1]{3,2,0,1:T(8,128)S(1)}, u32[]{:S(2)}, u32[]{:S(2)}) collective-permute-start(f32[3,8,8,1]{3,2,0,1:T(8,128)S(1)} %get-tuple-element.113), channel_id=1, source_target_pairs={{0,32},{32,64},{64,96},{96,128},{128,160},{160,192},{192,224},{1,3... | collective-permute-start | bytes 2312 | tf_op jit(solution)/shard_map/ppermute | solution.py:22
  194.7 16.1 %collective-permute-start.44 = (f32[3,8,1,130]{3,2,0,1:T(1,128)S(1)}, f32[3,8,1,130]{3,2,0,1:T(1,128)S(1)}, u32[]{:S(2)}, u32[]{:S(2)}) collective-permute-start(f32[3,8,1,130]{3,2,0,1:T(1,128)S(1)} %get-tuple-element.74), channel_id=1, source_target_pairs={{0,4},{4,8},{8,12},{12,16},{16,20},{20,24},{24,28},{1,5},{5,9},{9,... | collective-permute-start | bytes 37448 | tf_op jit(solution)/shard_map/ppermute | solution.py:22
  196.8 14.0 %collective-permute-start.45 = (f32[3,8,1,130]{3,2,0,1:T(1,128)S(1)}, f32[3,8,1,130]{3,2,0,1:T(1,128)S(1)}, u32[]{:S(2)}, u32[]{:S(2)}) collective-permute-start(f32[3,8,1,130]{3,2,0,1:T(1,128)S(1)} %get-tuple-element.75), channel_id=1, source_target_pairs={{4,0},{8,4},{12,8},{16,12},{20,16},{24,20},{28,24},{5,1},{9,5},{13... | collective-permute-start | bytes 37448 | tf_op jit(solution)/shard_map/ppermute | solution.py:24
  201.5 16.5 %collective-permute-start.16 = (f32[3,1,10,130]{3,2,1,0:T(8,128)S(1)}, f32[3,1,10,130]{3,2,1,0:T(8,128)S(1)}, u32[]{:S(2)}, u32[]{:S(2)}) collective-permute-start(f32[3,1,10,130]{3,2,1,0:T(8,128)S(1)} %get-tuple-element.70), channel_id=1, source_target_pairs={{0,1},{1,2},{2,3},{4,5},{5,6},{6,7},{8,9},{9,10},{10,11},{12,13},{... | collective-permute-start | bytes 46808 | tf_op jit(solution)/shard_map/ppermute | solution.py:22
  224.6 15.5 %collective-permute-start.18 = (f32[6,8,8,1]{3,2,1,0:T(8,128)S(1)}, f32[6,8,8,1]{3,2,1,0:T(8,128)S(1)}, u32[]{:S(2)}, u32[]{:S(2)}) collective-permute-start(f32[6,8,8,1]{3,2,1,0:T(8,128)S(1)} %get-tuple-element.102), channel_id=1, source_target_pairs={{0,32},{32,64},{64,96},{96,128},{128,160},{160,192},{192,224},{1,3... | collective-permute-start | bytes 4616 | tf_op jit(solution)/shard_map/ppermute | solution.py:22
  240.4 34.7 %collective-permute-start.20 = (f32[6,8,1,130]{3,2,1,0:T(1,128)S(1)}, f32[6,8,1,130]{3,2,1,0:T(1,128)S(1)}, u32[]{:S(2)}, u32[]{:S(2)}) collective-permute-start(f32[6,8,1,130]{3,2,1,0:T(1,128)S(1)} %get-tuple-element.50), channel_id=1, source_target_pairs={{0,4},{4,8},{8,12},{12,16},{16,20},{20,24},{24,28},{1,5},{5,9},{9,... | collective-permute-start | bytes 74888 | tf_op jit(solution)/shard_map/ppermute | solution.py:22
  242.3 32.8 %collective-permute-start.21 = (f32[6,8,1,130]{3,2,1,0:T(1,128)S(1)}, f32[6,8,1,130]{3,2,1,0:T(1,128)S(1)}, u32[]{:S(2)}, u32[]{:S(2)}) collective-permute-start(f32[6,8,1,130]{3,2,1,0:T(1,128)S(1)} %get-tuple-element.51), channel_id=1, source_target_pairs={{4,0},{8,4},{12,8},{16,12},{20,16},{24,20},{28,24},{5,1},{9,5},{13... | collective-permute-start | bytes 74888 | tf_op jit(solution)/shard_map/ppermute | solution.py:24
  (29 other events, 374.8 us)
where the time goes:
time: 289 us; the launch traced here: 287 us
  starting transfers between devices  169 us (58%)
  other arithmetic  61.7 us (21%)
  local copies, waits for them, and re-layouts  25.7 us (9%)
  waiting for transfers between devices  15.3 us (5%)
  blocking collectives  9.47 us (3%)
  between operations  5.73 us (2%)
    ppermute x24, starting transfers between devices, padded_2(): lax.ppermute(head, axis, [((i + 1) % count, i) for i in range(ends)])  94.3 us
    ppermute x24, starting transfers between devices, padded_2(): lax.ppermute(tail, axis, [(i, (i + 1) % count) for i in range(ends)])  75.1 us
    add x1, other arithmetic, imaging_terms(): forward_stress[0] * adjoint_stress[0]  28.2 us
    scatter-add x4, other arithmetic, inject(): flat = normal.reshape(3, -1).at[:, cells].add(values).reshape(normal.shape)  21 us
    ppermute x24, waiting for transfers between devices, padded_2(): lax.ppermute(head, axis, [((i + 1) % count, i) for i in range(ends)])  15.2 us
    reshape x5, local copies, waits for them, and re-layouts, inject(): flat = normal.reshape(3, -1).at[:, cells].add(values).reshape(normal.shape)  13.9 us
    all_gather x1, blocking collectives, restore(): everything = lax.all_gather(checkpoint_store, 'gz', axis=0, tiled=True)  9.47 us
    slice x5, local copies, waits for them, and re-layouts, inject(): normal = stress[:3]  6.46 us
  transfers between devices with their start and end apart: 48, of which 4 were waited for; matrix products, arithmetic and copies ran while one was open for 28% of the time, Pallas kernels for 0%

commit v1 on v0

v1 whole, which is shorter than its diff:
```python
import functools

import jax
import jax.numpy as jnp
from jax import lax
from jax.experimental import pallas as pl
from jax.experimental.pallas import tpu as pltpu
from jax.sharding import PartitionSpec as P

MESH = pl.DeviceIdType.MESH
STEPS = 2

ADJ, FWD = 0, 4


def iota3(dim):
    return lax.broadcasted_iota(jnp.int32, (8, 8, 128), dim)


def pack_columns(fields, lane):
    lanes = lax.broadcasted_iota(jnp.int32, (8, 128), 1)
    packed = jnp.zeros((8, 128), jnp.float32)
    for number, field in enumerate(fields):
        for z in range(8):
            at = number * 8 + z
            moved = pltpu.roll(field[z], (at - lane) % 128, 1)
            packed = jnp.where(lanes == at, moved, packed)
    return packed


def unpack_columns(packed, number, lane):
    return jnp.stack([pltpu.roll(packed, (lane - number * 8 - z) % 128, 1) for z in range(8)])


class Halo:
    def __init__(self, xl, xr, yl, yr, zl, zr):
        self.xl, self.xr, self.yl, self.yr, self.zl, self.zr = xl, xr, yl, yr, zl, zr

    def behind_x(self, f, i):
        before = jnp.where(iota3(2) == 0, unpack_columns(self.xl, i, 0), pltpu.roll(f, 1, 2))
        return f - before

    def ahead_x(self, f, i):
        after = jnp.where(iota3(2) == 127, unpack_columns(self.xr, i, 127), pltpu.roll(f, 127, 2))
        return after - f

    def behind_y(self, f, i):
        face = jnp.broadcast_to(self.yl[i], (8, 8, 128))
        return f - jnp.where(iota3(1) == 0, face, pltpu.roll(f, 1, 1))

    def ahead_y(self, f, i):
        face = jnp.broadcast_to(self.yr[i], (8, 8, 128))
        return jnp.where(iota3(1) == 7, face, pltpu.roll(f, 7, 1)) - f

    def behind_z(self, f, i):
        return f - jnp.concatenate([self.zl[i][None], f[:7]], axis=0)

    def ahead_z(self, f, i):
        return jnp.concatenate([f[1:], self.zr[i][None]], axis=0) - f


def kernel(
    sizes,
    store,
    hpeer,
    hslot,
    adj_in,
    lam_in,
    mu_in,
    buoy_in,
    src_in,
    wav_in,
    rec_in,
    tr_in,
    plan_in,
    adj_out,
    il_out,
    im_out,
    lam,
    mu,
    buoy,
    rec,
    traces,
    t_peer,
    t_slot,
    t_src,
    t_wav,
    t_plan,
    gath_s,
    gath_v,
    fv,
    fs,
    av,
    as_,
    a1,
    a0,
    s_xl,
    s_xr,
    s_yl,
    s_yr,
    s_zl,
    s_zr,
    r_xl,
    r_xr,
    r_yl,
    r_yr,
    r_zl,
    r_zr,
    in_sem,
    send_sem,
    recv_sem,
    rs_send,
    rs_recv,
):
    ngx, ngy, ngz = sizes
    gx, gy, gz = lax.axis_index("gx"), lax.axis_index("gy"), lax.axis_index("gz")
    partner = gz + 1 - 2 * lax.rem(gz, 2)
    cross = lax.rem(gz + 2, 4)

    def local(src, dst, n):
        return pltpu.make_async_copy(src, dst, in_sem.at[n])

    loads = dict(
        av=local(adj_in.at[pl.ds(0, 3)], av, 0),
        as_=local(adj_in.at[pl.ds(3, 6)], as_, 1),
        lam=local(lam_in, lam, 2),
        mu=local(mu_in, mu, 3),
        buoy=local(buoy_in, buoy, 4),
        rec=local(rec_in.at[0, 0], rec, 5),
        traces=local(tr_in.at[0, 0, 0], traces, 6),
        plan=local(plan_in, t_plan, 7),
        wav=local(wav_in, t_wav, 8),
        src=local(src_in.at[0, 0, 0], t_src, 9),
        peer=local(hpeer.at[0, 0], t_peer, 10),
        slot=local(hslot.at[0, 0], t_slot, 11),
        own_s=local(store.at[:, pl.ds(3, 6), 0], gath_s.at[pl.ds(gz * 8, 8)], 12),
        own_v=local(store.at[:, pl.ds(0, 3), 0], gath_v.at[pl.ds(gz * 8, 8)], 13),
    )
    for copy in loads.values():
        copy.start()

    barrier = pltpu.get_barrier_semaphore()

    def at(**axes):
        return dict(axes)

    def greet(where):
        pl.semaphore_signal(barrier, inc=1, device_id=where, device_id_type=MESH)

    greeted = 3
    for axis, index, count in (("gx", gx, ngx), ("gy", gy, ngy)):
        for step, exists in ((-1, index > 0), (1, index < count - 1)):

            @pl.when(exists)
            def _():
                greet({axis: index + step})

            greeted = greeted + exists.astype(jnp.int32)
    for d in (1, 2, 3):
        greet({"gz": lax.rem(gz + d, 4)})

    for exists, ref in (
        (gx > 0, r_xl),
        (gx < ngx - 1, r_xr),
        (gy > 0, r_yl),
        (gy < ngy - 1, r_yr),
        (gz > 0, r_zl),
        (gz < ngz - 1, r_zr),
    ):

        @pl.when(jnp.logical_not(exists))
        def _():
            ref[...] = jnp.zeros(ref.shape, jnp.float32)

    pl.semaphore_wait(barrier, greeted)

    def remote(src, dst, n, where):
        return pltpu.make_async_remote_copy(
            src_ref=src,
            dst_ref=dst,
            send_sem=rs_send.at[n],
            recv_sem=rs_recv.at[n],
            device_id={"gz": where},
            device_id_type=MESH,
        )

    mine, theirs = pl.ds(gz * 8, 8), pl.ds(cross * 8, 8)
    st_s, st_v = store.at[:, pl.ds(3, 6), 0], store.at[:, pl.ds(0, 3), 0]
    cross_s = remote(st_s, gath_s.at[mine], 0, cross)
    cross_v = remote(st_v, gath_v.at[mine], 1, cross)
    pair_s = remote(st_s, gath_s.at[mine], 2, partner)
    pair_v = remote(st_v, gath_v.at[mine], 3, partner)
    relay_s = remote(gath_s.at[theirs], gath_s.at[theirs], 4, partner)
    relay_v = remote(gath_v.at[theirs], gath_v.at[theirs], 5, partner)
    cross_s.start()
    cross_v.start()
    pair_s.start()
    pair_v.start()

    ends = (
        ("gx", gx, 1, ngx, s_xr, r_xl),
        ("gx", gx, -1, ngx, s_xl, r_xr),
        ("gy", gy, 1, ngy, s_yr, r_yl),
        ("gy", gy, -1, ngy, s_yl, r_yr),
        ("gz", gz, 1, ngz, s_zr, r_zl),
        ("gz", gz, -1, ngz, s_zl, r_zr),
    )

    def face(r, d, fields):
        axis, index, step, count, source, target = ends[d]
        if axis == "gx":
            src, dst = source.at[r], target.at[r]
        else:
            src, dst = source.at[r, pl.ds(0, fields)], target.at[r, pl.ds(0, fields)]
        copy = pltpu.make_async_remote_copy(
            src_ref=src,
            dst_ref=dst,
            send_sem=send_sem.at[r, d],
            recv_sem=recv_sem.at[r, d],
            device_id={axis: index + step},
            device_id_type=MESH,
        )
        goes = index < count - 1 if step > 0 else index > 0
        comes = index > 0 if step > 0 else index < count - 1
        return copy, goes, comes

    STRESS, VELOCITY = (2, 1, 2, 1, 2, 1), (1, 2, 1, 2, 1, 2)

    def send_faces(r, up, down, counts):
        (xu, yu, zu), (xd, yd, zd) = up, down
        for i, f in enumerate(zu):
            s_zr[r, i] = f[7]
        for i, f in enumerate(zd):
            s_zl[r, i] = f[0]
        for d in (4, 5):
            start(r, d, counts)
        for i, f in enumerate(yu):
            s_yr[r, i] = f[:, 7:8, :]
        for i, f in enumerate(yd):
            s_yl[r, i] = f[:, 0:1, :]
        for d in (2, 3):
            start(r, d, counts)
        s_xr[r] = pack_columns(xu, 127)
        s_xl[r] = pack_columns(xd, 0)
        for d in (0, 1):
            start(r, d, counts)

    def start(r, d, counts):
        copy, goes, _ = face(r, d, counts[d])

        @pl.when(goes)
        def _():
            copy.start()

    def send_stress(r, s):
        send_faces(r, ((s[3], s[4]), (s[3], s[5]), (s[4], s[5])), ((s[0],), (s[1],), (s[2],)), STRESS)

    def send_velocity(r, v):
        send_faces(r, ((v[0],), (v[1],), (v[2],)), ((v[1], v[2]), (v[0], v[2]), (v[0], v[1])), VELOCITY)

    def receive(r, counts):
        for d in range(6):
            copy, _, comes = face(r, d, counts[d])

            @pl.when(comes)
            def _():
                copy.wait_recv()

        return Halo(r_xl[r], r_xr[r], r_yl[r], r_yr[r], r_zl[r], r_zr[r])

    def velocity_rates(s, h):
        b = buoy[...]
        rx = b * (h.ahead_x(s[0], 0) + h.behind_y(s[3], 0) + h.behind_z(s[4], 0))
        ry = b * (h.behind_x(s[3], 0) + h.ahead_y(s[1], 0) + h.behind_z(s[5], 1))
        rz = b * (h.behind_x(s[4], 1) + h.behind_y(s[5], 1) + h.ahead_z(s[2], 0))
        return rx, ry, rz

    def stress_rates(v, h):
        exx, eyy, ezz = h.behind_x(v[0], 0), h.behind_y(v[1], 0), h.behind_z(v[2], 0)
        m = mu[...]
        spread = lam[...] * (exx + eyy + ezz)
        twice = 2.0 * m
        return (
            spread + twice * exx,
            spread + twice * eyy,
            spread + twice * ezz,
            m * (h.ahead_y(v[0], 0) + h.ahead_x(v[1], 0)),
            m * (h.ahead_z(v[0], 0) + h.ahead_x(v[2], 1)),
            m * (h.ahead_z(v[1], 1) + h.ahead_y(v[2], 1)),
        )

    loads["av"].wait()
    send_velocity(ADJ, [av[i] for i in range(3)])

    for name in ("rec", "traces", "plan", "as_", "lam", "mu", "buoy"):
        loads[name].wait()
    cells = rec[0]
    row_of, x_of = lax.shift_right_logical(cells, 7), lax.bitwise_and(cells, 127)
    rows = lax.broadcasted_iota(jnp.int32, (64, 64), 0)
    hit = rows == jnp.broadcast_to(row_of, (64, 64))
    samples = [jnp.broadcast_to(traces[pl.ds(t_plan[k], 1), :], (64, 64)) for k in range(STEPS)]
    left = jnp.concatenate([jnp.where(hit, samples[k], 0.0) for k in range(STEPS)], axis=0)
    columns = lax.broadcasted_iota(jnp.int32, (128, 64), 0)
    right = jnp.where(columns == jnp.broadcast_to(x_of, (128, 64)), 1.0, 0.0)
    spread = lax.dot_general(
        left, right, (((1,), (1,)), ((), ())), precision=lax.Precision.HIGHEST, preferred_element_type=jnp.float32
    )
    spread = spread.reshape(STEPS, 8, 8, 128)
    for i in range(3):
        a1[i] = as_[i] + spread[1]
        a0[i] = spread[0]
    for i in range(3, 6):
        a1[i] = as_[i]

    h = receive(ADJ, VELOCITY)
    rates = stress_rates([av[i] for i in range(3)], h)
    for i in range(6):
        as_[i] = a1[i] - rates[i]
    send_stress(ADJ + 1, [as_[i] for i in range(6)])

    cross_s.wait_recv()
    relay_s.start()
    cross_v.wait_recv()
    relay_v.start()

    h = receive(ADJ + 1, STRESS)
    rates = velocity_rates([as_[i] for i in range(6)], h)
    for i in range(3):
        av[i] = av[i] - rates[i]
    send_velocity(ADJ + 2, [av[i] for i in range(3)])
    for i in range(3):
        a0[i] = a0[i] + as_[i]
    for i in range(3, 6):
        a0[i] = as_[i]

    for name in ("peer", "slot", "own_s", "own_v", "wav", "src"):
        loads[name].wait()
    pair_s.wait_recv()
    relay_s.wait_recv()
    where_is = [t_peer[gz, p] * 8 + t_slot[gz, p] for p in range(8)]
    for p in range(8):
        fs[:, p] = gath_s[where_is[p]].astype(jnp.float32)
    send_stress(FWD, [fs[i] for i in range(6)])

    h = receive(ADJ + 2, VELOCITY)
    rates = stress_rates([av[i] for i in range(3)], h)
    for i in range(6):
        as_[i] = a0[i] - rates[i]
    send_stress(ADJ + 3, [as_[i] for i in range(6)])

    pair_v.wait_recv()
    relay_v.wait_recv()
    for p in range(8):
        fv[:, p] = gath_v[where_is[p]].astype(jnp.float32)
    flat = iota3(0) * 1024 + iota3(1) * 128 + iota3(2)
    hits = jnp.zeros((8, 8, 128), jnp.float32)
    for j in range(t_src.shape[0]):
        hits = hits + jnp.where(flat == t_src[j], 1.0, 0.0)

    h = receive(FWD, STRESS)
    rates = velocity_rates([fs[i] for i in range(6)], h)
    for i in range(3):
        fv[i] = fv[i] + rates[i]
    send_velocity(FWD + 1, [fv[i] for i in range(3)])

    h = receive(ADJ + 3, STRESS)
    rates = velocity_rates([as_[i] for i in range(6)], h)
    for i in range(3):
        adj_out[i] = av[i] - rates[i]
    for i in range(6):
        adj_out[3 + i] = as_[i]

    h = receive(FWD + 1, VELOCITY)
    rates = stress_rates([fv[i] for i in range(3)], h)
    pulse = hits * t_wav[t_plan[0]]
    for i in range(3):
        fs[i] = fs[i] + rates[i] + pulse
    for i in range(3, 6):
        fs[i] = fs[i] + rates[i]
    send_stress(FWD + 2, [fs[i] for i in range(6)])

    def image(s, a):
        by_lambda = (s[0] + s[1] + s[2]) * (a[0] + a[1] + a[2])
        by_mu = s[0] * a[0] + s[1] * a[1] + s[2] * a[2] + 2.0 * (s[3] * a[3] + s[4] * a[4] + s[5] * a[5])
        return by_lambda, by_mu

    by_lambda, by_mu = image(fs, a0)
    il_out[...] = by_lambda
    im_out[...] = by_mu

    h = receive(FWD + 2, STRESS)
    rates = velocity_rates([fs[i] for i in range(6)], h)
    for i in range(3):
        fv[i] = fv[i] + rates[i]
    send_velocity(FWD + 3, [fv[i] for i in range(3)])

    h = receive(FWD + 3, VELOCITY)
    rates = stress_rates([fv[i] for i in range(3)], h)
    pulse = hits * t_wav[t_plan[1]]
    last = [fs[i] + rates[i] + pulse for i in range(3)] + [fs[i] + rates[i] for i in range(3, 6)]
    by_lambda, by_mu = image(last, a1)
    il_out[...] += by_lambda
    im_out[...] += by_mu

    for copy in (cross_s, cross_v, pair_s, pair_v, relay_s, relay_v):
        copy.wait_send()
    for r in range(8):
        counts = VELOCITY if r in (0, 2, 5, 7) else STRESS
        for d in range(6):
            copy, goes, _ = face(r, d, counts[d])

            @pl.when(goes)
            def _():
                copy.wait_send()


def solution(mesh):
    sizes = (mesh.shape["gx"], mesh.shape["gy"], mesh.shape["gz"])
    f32, i32, bf16 = jnp.float32, jnp.int32, jnp.bfloat16
    brick = (8, 8, 128)

    def on_device(*args):
        nt, nrec = args[10].shape[-2:]
        nsrc = args[7].shape[-1]
        vmem = pltpu.VMEM
        scratch = [
            vmem(brick, f32),
            vmem(brick, f32),
            vmem(brick, f32),
            vmem((1, nrec), i32),
            vmem((nt, nrec), f32),
            pltpu.SMEM((4, 8), i32),
            pltpu.SMEM((4, 8), i32),
            pltpu.SMEM((nsrc,), i32),
            pltpu.SMEM((nt,), f32),
            pltpu.SMEM((STEPS,), i32),
            vmem((32, 6, 8, 128), bf16),
            vmem((32, 3, 8, 128), bf16),
            vmem((3,) + brick, f32),
            vmem((6,) + brick, f32),
            vmem((3,) + brick, f32),
            vmem((6,) + brick, f32),
            vmem((6,) + brick, f32),
            vmem((6,) + brick, f32),
        ]
        for _ in range(2):
            scratch += [vmem((8, 8, 128), f32)] * 2 + [vmem((8, 2, 8, 1, 128), f32)] * 2 + [vmem((8, 2, 8, 128), f32)] * 2
        dma = pltpu.SemaphoreType.DMA
        scratch += [dma((14,)), dma((8, 6)), dma((8, 6)), dma((6,)), dma((6,))]
        return pl.pallas_call(
            functools.partial(kernel, sizes),
            out_shape=(
                jax.ShapeDtypeStruct((9,) + brick, f32),
                jax.ShapeDtypeStruct(brick, f32),
                jax.ShapeDtypeStruct(brick, f32),
            ),
            in_specs=[pl.BlockSpec(memory_space=pl.ANY)] * 12,
            out_specs=(pl.BlockSpec(memory_space=pltpu.VMEM),) * 3,
            scratch_shapes=scratch,
            compiler_params=pltpu.CompilerParams(collective_id=0, has_side_effects=True),
            name="window",
        )(*args)

    return jax.shard_map(
        on_device,
        mesh=mesh,
        in_specs=(
            P("gz", None, None, "gy", "gx"),
            P("gx", "gy", None, None),
            P("gx", "gy", None, None),
            P(None, "gz", "gy", "gx"),
            P("gz", "gy", "gx"),
            P("gz", "gy", "gx"),
            P("gz", "gy", "gx"),
            P("gz", "gy", "gx", None),
            P(),
            P("gz", "gy", "gx", None),
            P("gz", "gy", "gx", None, None),
            P(),
        ),
        out_specs=(P(None, "gz", "gy", "gx"), P("gz", "gy", "gx"), P("gz", "gy", "gx")),
        check_vma=False,
    )
```

time: 289 us -> 37.1 us (0.13)
  the two profiles are of different devices: /device:TPU:131 before, /device:TPU:34 now
where the time goes in v1:
time: 37.1 us; the launch traced here: 36.7 us
  Pallas kernels  32.9 us (89%)
  local copies, waits for them, and re-layouts  3.09 us (8%)
  between operations  0.65 us (2%)
    pallas_call x1, Pallas kernels, on_device(): pl.pallas_call(functools.partial(kernel, sizes), out_shape=(jax.ShapeDtyp...  32.9 us
    unnamed x7, local copies, waits for them, and re-layouts  3.09 us

profile of v1, /device:TPU:34, one launch (start us, length us, event | category | flops | bytes accessed | tf_op | source)
XLA Modules:
  0.0 36.7 jit_solution(17786691127091341454)
XLA Ops:
  0.6 32.9 %window.1 = (f32[9,8,8,128]{3,2,1,0:T(8,128)}, f32[8,8,128]{2,1,0:T(8,128)}, f32[8,8,128]{2,1,0:T(8,128)}) custom-call(bf16[8,9,1,8,128]{4,3,2,1,0:T(8,128)(2,1)} %store.1, s32[1,1,4,8]{3,2,1,0:T(4,128)} %hpeer.1, s32[1,1,4,8]{3,2,1,0:T(4,128)} %hslot.1, f32[9,8,8,128]{3,2,1,0:T(8,128)} %adj_in.1, f32[8,8,128]{2,1,0:T(8,128)} %lam_in.1, f32[8,8,128]{2,1,0:T(8,128)} %mu_in.1, ...), custom_call_target="tpu_custom_call" | custom-call | tf_op jit(solution)/shard_map/window/pallas_call | solution.py:450
  33.6 0.0 copy-start.1
  33.6 1.7 %copy.18 = f32[9,8,8,128]{3,2,1,0:T(8,128)} copy(f32[9,8,8,128]{3,2,1,0:T(8,128)} %get-tuple-element.6) | data formatting | bytes 589824
  35.3 0.0 copy-done.1
  35.3 0.0 copy-start
  35.3 0.6 %copy.19 = f32[8,8,128]{2,1,0:T(8,128)} copy(f32[8,8,128]{2,1,0:T(8,128)S(1)} %copy-done.1) | data formatting | bytes 65536
  35.9 0.2 copy-done
  36.0 0.6 %copy.20 = f32[8,8,128]{2,1,0:T(8,128)} copy(f32[8,8,128]{2,1,0:T(8,128)S(1)} %copy-done) | data formatting | bytes 65536
Async XLA Ops:
  33.6 1.7 %copy-start.1 = (f32[8,8,128]{2,1,0:T(8,128)S(1)}, f32[8,8,128]{2,1,0:T(8,128)}, u32[]{:S(2)}) copy-start(f32[8,8,128]{2,1,0:T(8,128)} %get-tuple-element.7) | copy-start | bytes 98308
  35.3 0.8 %copy-start = (f32[8,8,128]{2,1,0:T(8,128)S(1)}, f32[8,8,128]{2,1,0:T(8,128)}, u32[]{:S(2)}) copy-start(f32[8,8,128]{2,1,0:T(8,128)} %get-tuple-element.8) | copy-start | bytes 98308

commit v2 on v1

--- a/solution.py
+++ b/solution.py
@@ -323,16 +323,6 @@
     cross_v.wait_recv()
     relay_v.start()
 
-    h = receive(ADJ + 1, STRESS)
-    rates = velocity_rates([as_[i] for i in range(6)], h)
-    for i in range(3):
-        av[i] = av[i] - rates[i]
-    send_velocity(ADJ + 2, [av[i] for i in range(3)])
-    for i in range(3):
-        a0[i] = a0[i] + as_[i]
-    for i in range(3, 6):
-        a0[i] = as_[i]
-
     for name in ("peer", "slot", "own_s", "own_v", "wav", "src"):
         loads[name].wait()
     pair_s.wait_recv()
@@ -342,11 +332,15 @@
         fs[:, p] = gath_s[where_is[p]].astype(jnp.float32)
     send_stress(FWD, [fs[i] for i in range(6)])
 
-    h = receive(ADJ + 2, VELOCITY)
-    rates = stress_rates([av[i] for i in range(3)], h)
-    for i in range(6):
-        as_[i] = a0[i] - rates[i]
-    send_stress(ADJ + 3, [as_[i] for i in range(6)])
+    h = receive(ADJ + 1, STRESS)
+    rates = velocity_rates([as_[i] for i in range(6)], h)
+    for i in range(3):
+        av[i] = av[i] - rates[i]
+    send_velocity(ADJ + 2, [av[i] for i in range(3)])
+    for i in range(3):
+        a0[i] = a0[i] + as_[i]
+    for i in range(3, 6):
+        a0[i] = as_[i]
 
     pair_v.wait_recv()
     relay_v.wait_recv()
@@ -363,12 +357,11 @@
         fv[i] = fv[i] + rates[i]
     send_velocity(FWD + 1, [fv[i] for i in range(3)])
 
-    h = receive(ADJ + 3, STRESS)
-    rates = velocity_rates([as_[i] for i in range(6)], h)
-    for i in range(3):
-        adj_out[i] = av[i] - rates[i]
+    h = receive(ADJ + 2, VELOCITY)
+    rates = stress_rates([av[i] for i in range(3)], h)
     for i in range(6):
-        adj_out[3 + i] = as_[i]
+        as_[i] = a0[i] - rates[i]
+    send_stress(ADJ + 3, [as_[i] for i in range(6)])
 
     h = receive(FWD + 1, VELOCITY)
     rates = stress_rates([fv[i] for i in range(3)], h)
@@ -378,6 +371,13 @@
     for i in range(3, 6):
         fs[i] = fs[i] + rates[i]
     send_stress(FWD + 2, [fs[i] for i in range(6)])
+
+    h = receive(ADJ + 3, STRESS)
+    rates = velocity_rates([as_[i] for i in range(6)], h)
+    for i in range(3):
+        adj_out[i] = av[i] - rates[i]
+    for i in range(6):
+        adj_out[3 + i] = as_[i]
 
     def image(s, a):
         by_lambda = (s[0] + s[1] + s[2]) * (a[0] + a[1] + a[2])
@@ -412,6 +412,17 @@
             @pl.when(goes)
             def _():
                 copy.wait_send()
+
+
+def write_out(adj, il, im, adj_out, il_out, im_out, sem):
+    copies = [
+        pltpu.make_async_copy(src, dst, sem.at[n])
+        for n, (src, dst) in enumerate(((adj, adj_out), (il, il_out), (im, im_out)))
+    ]
+    for copy in copies:
+        copy.start()
+    for copy in copies:
+        copy.wait()
 
 
 def solution(mesh):
@@ -447,19 +458,27 @@
             scratch += [vmem((8, 8, 128), f32)] * 2 + [vmem((8, 2, 8, 1, 128), f32)] * 2 + [vmem((8, 2, 8, 128), f32)] * 2
         dma = pltpu.SemaphoreType.DMA
         scratch += [dma((14,)), dma((8, 6)), dma((8, 6)), dma((6,)), dma((6,))]
-        return pl.pallas_call(
+        shapes = ((9,) + brick, brick, brick)
+        results = pl.pallas_call(
             functools.partial(kernel, sizes),
-            out_shape=(
-                jax.ShapeDtypeStruct((9,) + brick, f32),
-                jax.ShapeDtypeStruct(brick, f32),
-                jax.ShapeDtypeStruct(brick, f32),
-            ),
+            out_shape=tuple(pltpu.VMEM(shape, f32) for shape in shapes),
             in_specs=[pl.BlockSpec(memory_space=pl.ANY)] * 12,
             out_specs=(pl.BlockSpec(memory_space=pltpu.VMEM),) * 3,
             scratch_shapes=scratch,
-            compiler_params=pltpu.CompilerParams(collective_id=0, has_side_effects=True),
+            compiler_params=pltpu.CompilerParams(
+                collective_id=0, has_side_effects=True, vmem_limit_bytes=16 << 20
+            ),
             name="window",
         )(*args)
+        return pl.pallas_call(
+            write_out,
+            out_shape=tuple(jax.ShapeDtypeStruct(shape, f32) for shape in shapes),
+            in_specs=[pl.BlockSpec(memory_space=pltpu.VMEM)] * 3,
+            out_specs=(pl.BlockSpec(memory_space=pl.ANY),) * 3,
+            scratch_shapes=[pltpu.SemaphoreType.DMA((3,))],
+            compiler_params=pltpu.CompilerParams(vmem_limit_bytes=16 << 20),
+            name="write_out",
+        )(*results)
 
     return jax.shard_map(
         on_device,

time: 37.1 us -> 39.6 us (1.067)
  the two profiles are of different devices: /device:TPU:34 before, /device:TPU:66 now
where the time goes in v2:
time: 39.6 us; the launch traced here: 39.1 us
  Pallas kernels  29.5 us (74%)
  local copies, waits for them, and re-layouts  8.87 us (22%)
  between operations  0.66 us (2%)
    pallas_call x1, Pallas kernels, on_device(): pl.pallas_call(functools.partial(kernel, sizes), out_shape=tuple((pltpu.V...  28.8 us
    unnamed x24, local copies, waits for them, and re-layouts  8.87 us

profile of v2, /device:TPU:66, one launch (start us, length us, event | category | flops | bytes accessed | tf_op | source)
XLA Modules:
  0.0 39.1 jit_solution(2777352432151096924)
XLA Ops:
  0.6 0.0 copy-start
  0.6 1.0 %copy-done = f32[9,8,8,128]{3,2,1,0:T(8,128)S(1)} copy-done((f32[9,8,8,128]{3,2,1,0:T(8,128)S(1)}, f32[9,8,8,128]{3,2,1,0:T(8,128)}, u32[]{:S(2)}) %copy-start) | copy-done | bytes 294936
  1.6 0.0 copy-start.1
  1.6 0.9 %copy-done.1 = bf16[8,9,1,8,128]{4,3,2,1,0:T(8,128)(2,1)S(1)} copy-done((bf16[8,9,1,8,128]{4,3,2,1,0:T(8,128)(2,1)S(1)}, bf16[8,9,1,8,128]{4,3,2,1,0:T(8,128)(2,1)}, u32[]{:S(2)}) %copy-start.1) | copy-done | bytes 147480
  2.5 0.0 copy-start.2
  2.5 0.8 %copy-done.2 = f32[8,8,128]{2,1,0:T(8,128)S(1)} copy-done((f32[8,8,128]{2,1,0:T(8,128)S(1)}, f32[8,8,128]{2,1,0:T(8,128)}, u32[]{:S(2)}) %copy-start.2) | copy-done | bytes 32792
  3.3 0.0 copy-start.3
  3.3 0.8 %copy-done.3 = f32[8,8,128]{2,1,0:T(8,128)S(1)} copy-done((f32[8,8,128]{2,1,0:T(8,128)S(1)}, f32[8,8,128]{2,1,0:T(8,128)}, u32[]{:S(2)}) %copy-start.3) | copy-done | bytes 32792
  4.0 0.0 copy-start.4
  4.0 0.8 %copy-done.4 = f32[8,8,128]{2,1,0:T(8,128)S(1)} copy-done((f32[8,8,128]{2,1,0:T(8,128)S(1)}, f32[8,8,128]{2,1,0:T(8,128)}, u32[]{:S(2)}) %copy-start.4) | copy-done | bytes 32792
  4.8 0.0 copy-start.5
  4.8 0.8 %copy-done.5 = f32[1,1,1,64,64]{4,3,2,1,0:T(8,128)S(1)} copy-done((f32[1,1,1,64,64]{4,3,2,1,0:T(8,128)S(1)}, f32[1,1,1,64,64]{4,3,2,1,0:T(8,128)}, u32[]{:S(2)}) %copy-start.5) | copy-done | bytes 16408
  5.5 0.0 copy-start.6
  5.5 0.7 %copy-done.6 = s32[1,1,4,8]{3,2,1,0:T(4,128)S(1)} copy-done((s32[1,1,4,8]{3,2,1,0:T(4,128)S(1)}, s32[1,1,4,8]{3,2,1,0:T(4,128)}, u32[]{:S(2)}) %copy-start.6) | copy-done | bytes 152
  6.2 0.0 copy-start.7
  6.2 0.7 %copy-done.7 = s32[1,1,4,8]{3,2,1,0:T(4,128)S(1)} copy-done((s32[1,1,4,8]{3,2,1,0:T(4,128)S(1)}, s32[1,1,4,8]{3,2,1,0:T(4,128)}, u32[]{:S(2)}) %copy-start.7) | copy-done | bytes 152
  6.9 0.0 copy-start.8
  6.9 0.7 %copy-done.8 = s32[1,1,1,4]{3,2,1,0:T(1,128)S(1)} copy-done((s32[1,1,1,4]{3,2,1,0:T(1,128)S(1)}, s32[1,1,1,4]{3,2,1,0:T(1,128)}, u32[]{:S(2)}) %copy-start.8) | copy-done | bytes 40
  7.6 0.0 copy-start.9
  7.6 0.7 %copy-done.9 = f32[64]{0:T(128)S(1)} copy-done((f32[64]{0:T(128)S(1)}, f32[64]{0:T(128)}, u32[]{:S(2)}) %copy-start.9) | copy-done | bytes 280
  8.2 0.7 %copy-done.10 = s32[1,1,1,64]{3,2,1,0:T(1,128)S(1)} copy-done((s32[1,1,1,64]{3,2,1,0:T(1,128)S(1)}, s32[1,1,1,64]{3,2,1,0:T(1,128)}, u32[]{:S(2)}) %copy-start.10) | copy-done | bytes 280
  8.9 0.7 %copy-done.11 = s32[2]{0:T(128)S(1)} copy-done((s32[2]{0:T(128)S(1)}, s32[2]{0:T(128)}, u32[]{:S(2)}) %copy-start.11) | copy-done | bytes 32
  9.5 28.8 %window.1 = (f32[9,8,8,128]{3,2,1,0:T(8,128)S(1)}, f32[8,8,128]{2,1,0:T(8,128)S(1)}, f32[8,8,128]{2,1,0:T(8,128)S(1)}) custom-call(bf16[8,9,1,8,128]{4,3,2,1,0:T(8,128)(2,1)S(1)} %copy-done.1, s32[1,1,4,8]{3,2,1,0:T(4,128)S(1)} %copy-done.6, s32[1,1,4,8]{3,2,1,0:T(4,128)S(1)} %copy-done.7, f32[9,8,8,128]{3,2,1,0:T(8,128)S(1)} %copy-done, ...), custom_call_target="tpu_custom_call" | custom-call | tf_op jit(solution)/shard_map/window/pallas_call | solution.py:462
  38.3 0.8 %write_out.1 = (f32[9,8,8,128]{3,2,1,0:T(8,128)}, f32[8,8,128]{2,1,0:T(8,128)}, f32[8,8,128]{2,1,0:T(8,128)}) custom-call(f32[9,8,8,128]{3,2,1,0:T(8,128)S(1)} %get-tuple-element.6.adj, f32[8,8,128]{2,1,0:T(8,128)S(1)} %get-tuple-element.7.il, f32[8,8,128]{2,1,0:T(8,128)S(1)} %get-tuple-element.8.im), custom_call_target="tpu_custom_call" | custom-call | tf_op jit(solution)/shard_map/write_out/pallas_call | solution.py:473
  (2 shorter events, 0.0 us)
Async XLA Ops:
  0.6 1.0 %copy-start = (f32[9,8,8,128]{3,2,1,0:T(8,128)S(1)}, f32[9,8,8,128]{3,2,1,0:T(8,128)}, u32[]{:S(2)}) copy-start(f32[9,8,8,128]{3,2,1,0:T(8,128)} %adj_in.1) | copy-start | bytes 884740
  1.6 0.9 %copy-start.1 = (bf16[8,9,1,8,128]{4,3,2,1,0:T(8,128)(2,1)S(1)}, bf16[8,9,1,8,128]{4,3,2,1,0:T(8,128)(2,1)}, u32[]{:S(2)}) copy-start(bf16[8,9,1,8,128]{4,3,2,1,0:T(8,128)(2,1)} %store.1) | copy-start | bytes 442372
  2.5 0.8 %copy-start.2 = (f32[8,8,128]{2,1,0:T(8,128)S(1)}, f32[8,8,128]{2,1,0:T(8,128)}, u32[]{:S(2)}) copy-start(f32[8,8,128]{2,1,0:T(8,128)} %lam_in.1) | copy-start | bytes 98308
  3.3 0.8 %copy-start.3 = (f32[8,8,128]{2,1,0:T(8,128)S(1)}, f32[8,8,128]{2,1,0:T(8,128)}, u32[]{:S(2)}) copy-start(f32[8,8,128]{2,1,0:T(8,128)} %mu_in.1) | copy-start | bytes 98308
  4.0 0.8 %copy-start.4 = (f32[8,8,128]{2,1,0:T(8,128)S(1)}, f32[8,8,128]{2,1,0:T(8,128)}, u32[]{:S(2)}) copy-start(f32[8,8,128]{2,1,0:T(8,128)} %buoy_in.1) | copy-start | bytes 98308
  4.8 0.8 %copy-start.5 = (f32[1,1,1,64,64]{4,3,2,1,0:T(8,128)S(1)}, f32[1,1,1,64,64]{4,3,2,1,0:T(8,128)}, u32[]{:S(2)}) copy-start(f32[1,1,1,64,64]{4,3,2,1,0:T(8,128)} %tr_in.1) | copy-start | bytes 49156
  5.5 0.7 %copy-start.6 = (s32[1,1,4,8]{3,2,1,0:T(4,128)S(1)}, s32[1,1,4,8]{3,2,1,0:T(4,128)}, u32[]{:S(2)}) copy-start(s32[1,1,4,8]{3,2,1,0:T(4,128)} %hpeer.1) | copy-start | bytes 388
  6.2 0.7 %copy-start.7 = (s32[1,1,4,8]{3,2,1,0:T(4,128)S(1)}, s32[1,1,4,8]{3,2,1,0:T(4,128)}, u32[]{:S(2)}) copy-start(s32[1,1,4,8]{3,2,1,0:T(4,128)} %hslot.1) | copy-start | bytes 388
  6.9 0.7 %copy-start.8 = (s32[1,1,1,4]{3,2,1,0:T(1,128)S(1)}, s32[1,1,1,4]{3,2,1,0:T(1,128)}, u32[]{:S(2)}) copy-start(s32[1,1,1,4]{3,2,1,0:T(1,128)} %src_in.1) | copy-start | bytes 52
  7.6 0.7 %copy-start.9 = (f32[64]{0:T(128)S(1)}, f32[64]{0:T(128)}, u32[]{:S(2)}) copy-start(f32[64]{0:T(128)} %wav_in.1) | copy-start | bytes 772
  8.2 0.7 %copy-start.10 = (s32[1,1,1,64]{3,2,1,0:T(1,128)S(1)}, s32[1,1,1,64]{3,2,1,0:T(1,128)}, u32[]{:S(2)}) copy-start(s32[1,1,1,64]{3,2,1,0:T(1,128)} %rec_in.1) | copy-start | bytes 772
  8.9 0.7 %copy-start.11 = (s32[2]{0:T(128)S(1)}, s32[2]{0:T(128)}, u32[]{:S(2)}) copy-start(s32[2]{0:T(128)} %plan_in.1) | copy-start | bytes 28

commit v3 on v2

--- a/solution.py
+++ b/solution.py
@@ -117,6 +117,23 @@
     partner = gz + 1 - 2 * lax.rem(gz, 2)
     cross = lax.rem(gz + 2, 4)
 
+    barrier = pltpu.get_barrier_semaphore()
+
+    def greet(where):
+        pl.semaphore_signal(barrier, inc=1, device_id=where, device_id_type=MESH)
+
+    greeted = 3
+    for axis, index, count in (("gx", gx, ngx), ("gy", gy, ngy)):
+        for step, exists in ((-1, index > 0), (1, index < count - 1)):
+
+            @pl.when(exists)
+            def _():
+                greet({axis: index + step})
+
+            greeted = greeted + exists.astype(jnp.int32)
+    for d in (1, 2, 3):
+        greet({"gz": lax.rem(gz + d, 4)})
+
     def local(src, dst, n):
         return pltpu.make_async_copy(src, dst, in_sem.at[n])
 
@@ -138,26 +155,6 @@
     )
     for copy in loads.values():
         copy.start()
-
-    barrier = pltpu.get_barrier_semaphore()
-
-    def at(**axes):
-        return dict(axes)
-
-    def greet(where):
-        pl.semaphore_signal(barrier, inc=1, device_id=where, device_id_type=MESH)
-
-    greeted = 3
-    for axis, index, count in (("gx", gx, ngx), ("gy", gy, ngy)):
-        for step, exists in ((-1, index > 0), (1, index < count - 1)):
-
-            @pl.when(exists)
-            def _():
-                greet({axis: index + step})
-
-            greeted = greeted + exists.astype(jnp.int32)
-    for d in (1, 2, 3):
-        greet({"gz": lax.rem(gz + d, 4)})
 
     for exists, ref in (
         (gx > 0, r_xl),
@@ -466,7 +463,7 @@
             out_specs=(pl.BlockSpec(memory_space=pltpu.VMEM),) * 3,
             scratch_shapes=scratch,
             compiler_params=pltpu.CompilerParams(
-                collective_id=0, has_side_effects=True, vmem_limit_bytes=16 << 20
+                collective_id=0, has_side_effects=True
             ),
             name="window",
         )(*args)

time: 39.6 us -> 30.1 us (0.76); the launches traced: 39.1 us -> 30 us
  local copies, waits for them, and re-layouts: 8.87 us -> 0 us
    unnamed x24 -> x0, local copies, waits for them, and re-layouts: 8.87 us -> none
where the time goes in v3:
time: 30.1 us; the launch traced here: 30 us
  Pallas kernels  29.3 us (97%)
  between operations  0.64 us (2%)
    pallas_call x1, Pallas kernels, on_device(): pl.pallas_call(functools.partial(kernel, sizes), out_shape=tuple((pltpu.V...  28.6 us
    pallas_call x1, Pallas kernels, on_device(): pl.pallas_call(write_out, out_shape=tuple((jax.ShapeDtypeStruct(shape, f3...  0.75 us

profile of v3, /device:TPU:66, one launch (start us, length us, event | category | flops | bytes accessed | tf_op | source)
XLA Modules:
  0.0 30.0 jit_solution(16279921192162582398)
XLA Ops:
  0.6 28.6 %window.1 = (f32[9,8,8,128]{3,2,1,0:T(8,128)S(1)}, f32[8,8,128]{2,1,0:T(8,128)S(1)}, f32[8,8,128]{2,1,0:T(8,128)S(1)}) custom-call(bf16[8,9,1,8,128]{4,3,2,1,0:T(8,128)(2,1)} %store.1, s32[1,1,4,8]{3,2,1,0:T(4,128)} %hpeer.1, s32[1,1,4,8]{3,2,1,0:T(4,128)} %hslot.1, f32[9,8,8,128]{3,2,1,0:T(8,128)} %adj_in.1, f32[8,8,128]{2,1,0:T(8,128)} %lam_in.1, ...), custom_call_target="tpu_custom_call" | custom-call | tf_op jit(solution)/shard_map/window/pallas_call | solution.py:459
  29.2 0.8 %write_out.1 = (f32[9,8,8,128]{3,2,1,0:T(8,128)}, f32[8,8,128]{2,1,0:T(8,128)}, f32[8,8,128]{2,1,0:T(8,128)}) custom-call(f32[9,8,8,128]{3,2,1,0:T(8,128)S(1)} %get-tuple-element.6.adj, f32[8,8,128]{2,1,0:T(8,128)S(1)} %get-tuple-element.7.il, f32[8,8,128]{2,1,0:T(8,128)S(1)} %get-tuple-element.8.im), custom_call_target="tpu_custom_call" | custom-call | tf_op jit(solution)/shard_map/write_out/pallas_call | solution.py:470

commit v4 on v3

v4 whole, which is shorter than its diff:
```python
import functools

import jax
import jax.numpy as jnp
from jax import lax
from jax.experimental import pallas as pl
from jax.experimental.pallas import tpu as pltpu
from jax.sharding import PartitionSpec as P

MESH = pl.DeviceIdType.MESH
STEPS = 2

GREETED = ((1, 0, 0), (-1, 0, 0), (0, 1, 0), (0, -1, 0))


def iota3(dim):
    return lax.broadcasted_iota(jnp.int32, (8, 8, 128), dim)


def iota2(dim):
    return lax.broadcasted_iota(jnp.int32, (8, 128), dim)


def pack_columns(fields, lane):
    lanes = iota2(1)
    packed = jnp.zeros((8, 128), jnp.float32)
    for number, field in enumerate(fields):
        for z in range(8):
            at = number * 8 + z
            moved = pltpu.roll(field[z], (at - lane) % 128, 1)
            packed = jnp.where(lanes == at, moved, packed)
    return packed


def unpack_columns(packed, number, lane):
    return jnp.stack([pltpu.roll(packed, (lane - number * 8 - z) % 128, 1) for z in range(8)])


def behind_x(f, face):
    return f - jnp.where(iota3(2) == 0, face, pltpu.roll(f, 1, 2))


def ahead_x(f, face):
    return jnp.where(iota3(2) == 127, face, pltpu.roll(f, 127, 2)) - f


def behind_y(f, face):
    return f - jnp.where(iota3(1) == 0, jnp.broadcast_to(face, (8, 8, 128)), pltpu.roll(f, 1, 1))


def ahead_y(f, face):
    return jnp.where(iota3(1) == 7, jnp.broadcast_to(face, (8, 8, 128)), pltpu.roll(f, 7, 1)) - f


def behind_z(f, face):
    return f - jnp.concatenate([face[None], f[:7]], axis=0)


def ahead_z(f, face):
    return jnp.concatenate([f[1:], face[None]], axis=0) - f


def velocity_rates(s, b, h):
    rx = b * (ahead_x(s[0], h["xr", 0]) + behind_y(s[3], h["yl", 3]) + behind_z(s[4], h["zl", 4]))
    ry = b * (behind_x(s[3], h["xl", 3]) + ahead_y(s[1], h["yr", 1]) + behind_z(s[5], h["zl", 5]))
    rz = b * (behind_x(s[4], h["xl", 4]) + behind_y(s[5], h["yl", 5]) + ahead_z(s[2], h["zr", 2]))
    return rx, ry, rz


def stress_rates(v, lam, mu, h):
    exx, eyy, ezz = behind_x(v[0], h["xl", 0]), behind_y(v[1], h["yl", 1]), behind_z(v[2], h["zl", 2])
    spread = lam * (exx + eyy + ezz)
    twice = 2.0 * mu
    return (
        spread + twice * exx,
        spread + twice * eyy,
        spread + twice * ezz,
        mu * (ahead_y(v[0], h["yr", 0]) + ahead_x(v[1], h["xr", 1])),
        mu * (ahead_z(v[0], h["zr", 0]) + ahead_x(v[2], h["xr", 2])),
        mu * (ahead_z(v[1], h["zr", 1]) + ahead_y(v[2], h["yr", 2])),
    )


class Zeros:
    def __getitem__(self, key):
        side = key[0]
        shape = (8, 1, 128) if side[0] == "y" else (8, 128)
        return jnp.zeros((8, 8, 128) if side[0] == "x" else shape, jnp.float32)


def kernel(
    sizes,
    store,
    hpeer,
    hslot,
    adj_in,
    lam_in,
    mu_in,
    buoy_in,
    src_in,
    wav_in,
    rec_in,
    tr_in,
    plan_in,
    adj_out,
    il_out,
    im_out,
    params,
    rec,
    traces,
    t_peer,
    t_slot,
    t_src,
    t_wav,
    t_plan,
    gath_s,
    gath_v,
    fv,
    fs,
    adj,
    a1,
    a0,
    bx,
    hits,
    s_xl,
    s_xr,
    s_yl,
    s_yr,
    s_zl,
    s_zr,
    r_xl,
    r_xr,
    r_yl,
    r_yr,
    r_zl,
    r_zr,
    f_xl,
    f_xr,
    f_yl,
    f_yr,
    f_zl,
    f_zr,
    g_xl,
    g_xr,
    g_yl,
    g_yr,
    g_zl,
    g_zr,
    exy_mm,
    exy_pp,
    exy_pm,
    exy_mp,
    exz_mm,
    exz_pp,
    exz_pm,
    exz_mp,
    eyz_mm,
    eyz_pp,
    eyz_pm,
    eyz_mp,
    in_sem,
    send_sem,
    recv_sem,
    fsend_sem,
    frecv_sem,
    rs_send,
    rs_recv,
):
    count = dict(zip(("gx", "gy", "gz"), sizes))
    index = {axis: lax.axis_index(axis) for axis in ("gx", "gy", "gz")}
    gz = index["gz"]
    partner = gz + 1 - 2 * lax.rem(gz, 2)
    cross = lax.rem(gz + 2, 4)

    def exists(step):
        found = None
        for axis, d in zip(("gx", "gy", "gz"), step):
            if d:
                here = index[axis] < count[axis] - 1 if d > 0 else index[axis] > 0
                found = here if found is None else jnp.logical_and(found, here)
        return found

    def at(step):
        return {axis: index[axis] + d for axis, d in zip(("gx", "gy", "gz"), step) if d}

    barrier = pltpu.get_barrier_semaphore()

    def greet(where):
        pl.semaphore_signal(barrier, inc=1, device_id=where, device_id_type=MESH)

    greeted = 3
    for step in GREETED:

        @pl.when(exists(step))
        def _():
            greet(at(step))

        greeted = greeted + exists(step).astype(jnp.int32)
    for d in (1, 2, 3):
        greet({"gz": lax.rem(gz + d, 4)})

    def local(src, dst, n):
        return pltpu.make_async_copy(src, dst, in_sem.at[n])

    loads = dict(
        adj=local(adj_in, adj, 0),
        lam=local(lam_in, params.at[0], 1),
        mu=local(mu_in, params.at[1], 1),
        buoy=local(buoy_in, params.at[2], 1),
        rec=local(rec_in.at[0, 0], rec, 2),
        traces=local(tr_in.at[0, 0, 0], traces, 3),
        plan=local(plan_in, t_plan, 4),
        wav=local(wav_in, t_wav, 5),
        src=local(src_in.at[0, 0, 0], t_src, 6),
        peer=local(hpeer.at[0, 0], t_peer, 7),
        slot=local(hslot.at[0, 0], t_slot, 8),
        own_s=local(store.at[:, pl.ds(3, 6), 0], gath_s.at[pl.ds(gz * 8, 8)], 9),
        own_v=local(store.at[:, pl.ds(0, 3), 0], gath_v.at[pl.ds(gz * 8, 8)], 10),
    )
    for copy in loads.values():
        copy.start()

    def edges(e):
        return (
            (exy_mm, (1, 1, 0), f_yr.at[e, pl.ds(0, 1)]),
            (exy_pp, (-1, -1, 0), f_yl.at[e, pl.ds(2, 2)]),
            (exy_pm, (-1, 1, 0), f_yr.at[e, pl.ds(1, 1)]),
            (exy_mp, (1, -1, 0), f_yl.at[e, pl.ds(4, 1)]),
            (exz_mm, (1, 0, 1), f_zr.at[e, pl.ds(0, 1)]),
            (exz_pp, (-1, 0, -1), f_zl.at[e, pl.ds(2, 2)]),
            (exz_pm, (-1, 0, 1), f_zr.at[e, pl.ds(1, 1)]),
            (exz_mp, (1, 0, -1), f_zl.at[e, pl.ds(6, 1)]),
            (eyz_mm, (0, 1, 1), f_zr.at[e, pl.ds(1, 1)]),
            (eyz_pp, (0, -1, -1), f_zl.at[e, pl.ds(4, 2)]),
            (eyz_pm, (0, -1, 1), f_zr.at[e, pl.ds(0, 1)]),
            (eyz_mp, (0, 1, -1), f_zl.at[e, pl.ds(6, 1)]),
        )

    def back(step):
        return tuple(-d for d in step)

    for step, refs in (
        ((-1, 0, 0), (r_xl, g_xl)),
        ((1, 0, 0), (r_xr, g_xr)),
        ((0, -1, 0), (r_yl, g_yl)),
        ((0, 1, 0), (r_yr, g_yr)),
        ((0, 0, -1), (r_zl, g_zl)),
        ((0, 0, 1), (r_zr, g_zr)),
        *((back(step), (ref,)) for ref, step, _ in edges(0)),
    ):

        @pl.when(jnp.logical_not(exists(step)))
        def _():
            for ref in refs:
                ref[...] = jnp.zeros(ref.shape, jnp.float32)

    pl.semaphore_wait(barrier, greeted)

    def remote(src, dst, n, where):
        return pltpu.make_async_remote_copy(
            src_ref=src,
            dst_ref=dst,
            send_sem=rs_send.at[n],
            recv_sem=rs_recv.at[n],
            device_id={"gz": where},
            device_id_type=MESH,
        )

    mine, theirs = pl.ds(gz * 8, 8), pl.ds(cross * 8, 8)
    st_s, st_v = store.at[:, pl.ds(3, 6), 0], store.at[:, pl.ds(0, 3), 0]
    cross_s = remote(st_s, gath_s.at[mine], 0, cross)
    cross_v = remote(st_v, gath_v.at[mine], 1, cross)
    pair_s = remote(st_s, gath_s.at[mine], 2, partner)
    pair_v = remote(st_v, gath_v.at[mine], 3, partner)
    relay_s = remote(gath_s.at[theirs], gath_s.at[theirs], 4, partner)
    relay_v = remote(gath_v.at[theirs], gath_v.at[theirs], 5, partner)
    cross_s.start()
    cross_v.start()
    pair_s.start()
    pair_v.start()

    lam, mu, buoy = params.at[0], params.at[1], params.at[2]
    av, as_ = [adj.at[i] for i in range(3)], [adj.at[3 + i] for i in range(6)]

    ends = (
        ((1, 0, 0), s_xr, r_xl),
        ((-1, 0, 0), s_xl, r_xr),
        ((0, 1, 0), s_yr, r_yl),
        ((0, -1, 0), s_yl, r_yr),
        ((0, 0, 1), s_zr, r_zl),
        ((0, 0, -1), s_zl, r_zr),
    )

    def face(r, d, fields):
        step, source, target = ends[d]
        if d < 2:
            src, dst = source.at[r], target.at[r]
        else:
            src, dst = source.at[r, pl.ds(0, fields)], target.at[r, pl.ds(0, fields)]
        copy = pltpu.make_async_remote_copy(
            src_ref=src,
            dst_ref=dst,
            send_sem=send_sem.at[d],
            recv_sem=recv_sem.at[r % 2, d],
            device_id=at(step),
            device_id_type=MESH,
        )
        return copy, exists(step), exists(back(step))

    COUNTS = ((2, 3), (2, 1), (1, 2), (2, 1))

    def sent(r):
        for d in range(6):
            copy, goes, _ = face(r, d, COUNTS[r][d % 2])

            @pl.when(goes)
            def _():
                copy.wait_send()

    def send_faces(r, up, down):
        (xu, yu, zu), (xd, yd, zd) = up, down
        if r > 0:
            sent(r - 1)

        def start(d):
            copy, goes, _ = face(r, d, COUNTS[r][d % 2])

            @pl.when(goes)
            def _():
                copy.start()

        s_xr[r] = pack_columns(xu, 127)
        s_xl[r] = pack_columns(xd, 0)
        start(0)
        start(1)
        for i, f in enumerate(zu):
            s_zr[r, i] = f[7]
        for i, f in enumerate(zd):
            s_zl[r, i] = f[0]
        start(4)
        start(5)
        for i, f in enumerate(yu):
            s_yr[r, i] = f[:, 7:8, :]
        for i, f in enumerate(yd):
            s_yl[r, i] = f[:, 0:1, :]
        start(2)
        start(3)

    def send_stress(r, s):
        send_faces(r, ((s[3], s[4]), (s[3], s[5]), (s[4], s[5])), ((s[0],), (s[1],), (s[2],)))

    def send_velocity(r, v, more=()):
        send_faces(
            r,
            ((v[0], *more), (v[1], *more), (v[2], *more)),
            ((v[1], v[2], *more), (v[0], v[2], *more), (v[0], v[1], *more)),
        )

    def receive(r):
        for d in range(6):
            copy, _, comes = face(r, d, COUNTS[r][d % 2])

            @pl.when(comes)
            def _():
                copy.wait_recv()

    def stress_faces(r):
        xl, xr = r_xl[r], r_xr[r]
        return {
            ("xr", 0): unpack_columns(xr, 0, 127),
            ("xl", 3): unpack_columns(xl, 0, 0),
            ("xl", 4): unpack_columns(xl, 1, 0),
            ("yl", 3): r_yl[r, 0],
            ("yl", 5): r_yl[r, 1],
            ("yr", 1): r_yr[r, 0],
            ("zl", 4): r_zl[r, 0],
            ("zl", 5): r_zl[r, 1],
            ("zr", 2): r_zr[r, 0],
        }

    def velocity_faces(r):
        xl, xr = r_xl[r], r_xr[r]
        return {
            ("xl", 0): unpack_columns(xl, 0, 0),
            ("xr", 1): unpack_columns(xr, 0, 127),
            ("xr", 2): unpack_columns(xr, 1, 127),
            ("yl", 1): r_yl[r, 0],
            ("yr", 0): r_yr[r, 0],
            ("yr", 2): r_yr[r, 1],
            ("zl", 2): r_zl[r, 0],
            ("zr", 0): r_zr[r, 0],
            ("zr", 1): r_zr[r, 1],
        }

    fends = (
        (g_xl, (1, 0, 0), f_xr),
        (g_xr, (-1, 0, 0), f_xl),
        (g_yl, (0, 1, 0), f_yr),
        (g_yr, (0, -1, 0), f_yl),
        (g_zl, (0, 0, 1), f_zr),
        (g_zr, (0, 0, -1), f_zl),
    )

    def message(e, n):
        if n < 6:
            target, step, source = fends[n]
            src = source.at[e] if n < 2 else source.at[e, pl.ds(0, 3)]
        else:
            target, step, src = edges(e)[n - 6]
        copy = pltpu.make_async_remote_copy(
            src_ref=src,
            dst_ref=target.at[e],
            send_sem=fsend_sem.at[n],
            recv_sem=frecv_sem.at[e, n],
            device_id=at(step),
            device_id_type=MESH,
        )
        return copy, exists(step), exists(back(step))

    def forward_start(e, n):
        copy, goes, _ = message(e, n)

        @pl.when(goes)
        def _():
            copy.start()

    def forward_sent(e):
        for n in range(18):
            copy, goes, _ = message(e, n)

            @pl.when(goes)
            def _():
                copy.wait_send()

    def forward_receive(e):
        for n in range(18):
            copy, _, comes = message(e, n)

            @pl.when(comes)
            def _():
                copy.wait_recv()

    def forward_edges(e):
        if e > 0:
            forward_sent(e - 1)
        f_yr[e, 0] = fs[3, :, 7:8, :]
        f_yr[e, 1] = fs[5, :, 7:8, :]
        for i, f in ((2, 1), (3, 0), (4, 4)):
            f_yl[e, i] = fs[f, :, 0:1, :]
        for n in (6, 7, 8, 9):
            forward_start(e, n)
        f_zr[e, 0] = fs[4, 7]
        f_zr[e, 1] = fs[5, 7]
        for i, f in ((2, 2), (3, 0), (4, 2), (5, 1), (6, 3)):
            f_zl[e, i] = fs[f, 0]
        for n in range(10, 18):
            forward_start(e, n)

    def forward_faces(e):
        rates = velocity_rates([fs[i] for i in range(6)], buoy[...], Zeros())
        for i in range(3):
            fv[i] = fv[i] + rates[i]
        f_xr[e] = pack_columns((fs[3], fs[4], fv[0]), 127)
        f_xl[e] = pack_columns((fs[0], fv[1], fv[2]), 0)
        forward_start(e, 0)
        forward_start(e, 1)
        f_zr[e, 2] = fv[2, 7]
        f_zl[e, 0] = fv[0, 0]
        f_zl[e, 1] = fv[1, 0]
        forward_start(e, 4)
        forward_start(e, 5)
        f_yr[e, 2] = fv[1, :, 7:8, :]
        f_yl[e, 0] = fv[0, :, 0:1, :]
        f_yl[e, 1] = fv[2, :, 0:1, :]
        forward_start(e, 2)
        forward_start(e, 3)

    def forward_step(e):
        xl, xr = g_xl[e], g_xr[e]
        lane3, row3 = iota3(2), iota3(1)
        lane2, row2 = iota2(1), iota2(0)
        z1 = lax.broadcasted_iota(jnp.int32, (8, 1, 128), 0)
        lane1 = lax.broadcasted_iota(jnp.int32, (8, 1, 128), 2)

        def layer(at_z, tile, like):
            return jnp.where(iota3(0) == at_z, tile[None], 0.0) if like == 3 else jnp.where(z1 == at_z, tile, 0.0)

        def first_lane(f, axis):
            return pltpu.roll(f, 1, axis)

        def last_lane(f, axis):
            return pltpu.roll(f, 127, axis)

        mm, pp = first_lane(exy_mm[e, 0], 2), (last_lane(exy_pp[e, 0], 2), last_lane(exy_pp[e, 1], 2))
        pm, mp = last_lane(exy_pm[e, 0], 2), first_lane(exy_mp[e, 0], 2)
        zmm, zpp = first_lane(exz_mm[e, 0], 1), (last_lane(exz_pp[e, 0], 1), last_lane(exz_pp[e, 1], 1))
        zpm, zmp = last_lane(exz_pm[e, 0], 1), first_lane(exz_mp[e, 0], 1)
        all3 = (8, 8, 128)
        nothing = jnp.zeros(all3, jnp.float32)

        def row(at_y, face):
            return jnp.where(row3 == at_y, jnp.broadcast_to(face, all3), nothing)

        b = buoy[...]
        h = {}
        h["xl", 0] = unpack_columns(xl, 2, 0) + bx[0] * (fs[0] - row(0, mm) - layer(0, zmm, 3))
        h["xr", 1] = unpack_columns(xr, 1, 127) + bx[1] * (row(7, pp[0]) - fs[3] - layer(0, zpm, 3))
        h["xr", 2] = unpack_columns(xr, 2, 127) + bx[1] * (layer(7, zpp[0], 3) - fs[4] - row(0, pm))

        def y_layer(at_z, tile, at_y):
            return jnp.where(z1 == at_z, jnp.broadcast_to(tile[at_y : at_y + 1, :][None], (8, 1, 128)), 0.0)

        bym, byp = r_yl[0, 1], r_yr[0, 2]
        h["yl", 1] = g_yl[e, 2] + bym * (
            fs[1, :, 0:1, :] - jnp.where(lane1 == 0, mm, 0.0) - y_layer(0, eyz_mm[e, 0], 7)
        )
        h["yr", 0] = g_yr[e, 0] + byp * (
            jnp.where(lane1 == 127, pp[1], 0.0) - fs[3, :, 7:8, :] - y_layer(0, eyz_pm[e, 0], 0)
        )
        h["yr", 2] = g_yr[e, 1] + byp * (
            y_layer(7, eyz_pp[e, 0], 0) - fs[5, :, 7:8, :] - jnp.where(lane1 == 0, mp, 0.0)
        )

        def y_edge(tile, at_y, from_y):
            return jnp.where(row2 == at_y, jnp.broadcast_to(tile[from_y : from_y + 1, :], (8, 128)), 0.0)

        bzm, bzp = r_zl[0, 1], r_zr[0, 2]
        h["zl", 2] = g_zl[e, 2] + bzm * (fs[2, 0] - jnp.where(lane2 == 0, zmm, 0.0) - y_edge(eyz_mm[e, 0], 0, 7))
        h["zr", 0] = g_zr[e, 0] + bzp * (
            jnp.where(lane2 == 127, zpp[1], 0.0) - fs[4, 7] - y_edge(eyz_mp[e, 0], 0, 7)
        )
        h["zr", 1] = g_zr[e, 1] + bzp * (
            y_edge(eyz_pp[e, 1], 7, 0) - fs[5, 7] - jnp.where(lane2 == 0, zmp, 0.0)
        )

        fv[0] = fv[0] + b * (jnp.where(lane3 == 127, unpack_columns(xr, 0, 127), 0.0) - row(0, g_yl[e, 0]))
        fv[1] = fv[1] + b * (row(7, g_yr[e, 2]) - jnp.where(lane3 == 0, unpack_columns(xl, 0, 0), 0.0))
        fv[2] = fv[2] - b * (jnp.where(lane3 == 0, unpack_columns(xl, 1, 0), 0.0) + row(0, g_yl[e, 1]))
        fv[0, 0] = fv[0, 0] - buoy[0] * g_zl[e, 0]
        fv[1, 0] = fv[1, 0] - buoy[0] * g_zl[e, 1]
        fv[2, 7] = fv[2, 7] + buoy[7] * g_zr[e, 2]
        return stress_rates([fv[i] for i in range(3)], lam[...], mu[...], h)

    loads["adj"].wait()
    pltpu.make_async_copy(params, params, in_sem.at[1]).wait()
    send_velocity(0, [f[...] for f in av], (buoy[...],))

    for name in ("rec", "traces", "plan"):
        loads[name].wait()
    cells = rec[0]
    row_of, x_of = lax.shift_right_logical(cells, 7), lax.bitwise_and(cells, 127)
    rows = lax.broadcasted_iota(jnp.int32, (64, 64), 0)
    hit = rows == jnp.broadcast_to(row_of, (64, 64))
    samples = [jnp.broadcast_to(traces[pl.ds(t_plan[k], 1), :], (64, 64)) for k in range(STEPS)]
    left = jnp.concatenate([jnp.where(hit, samples[k], 0.0) for k in range(STEPS)], axis=0)
    columns = lax.broadcasted_iota(jnp.int32, (128, 64), 0)
    right = jnp.where(columns == jnp.broadcast_to(x_of, (128, 64)), 1.0, 0.0)
    spread = lax.dot_general(
        left, right, (((1,), (1,)), ((), ())), precision=lax.Precision.HIGHEST, preferred_element_type=jnp.float32
    )
    spread = spread.reshape(STEPS, 8, 8, 128)
    for i in range(3):
        a1[i] = as_[i][...] + spread[1]
        a0[i] = spread[0]
    for i in range(3, 6):
        a1[i] = as_[i][...]

    for name in ("wav", "src"):
        loads[name].wait()
    flat = iota3(0) * 1024 + iota3(1) * 128 + iota3(2)
    counted = jnp.zeros((8, 8, 128), jnp.float32)
    for j in range(t_src.shape[0]):
        counted = counted + jnp.where(flat == t_src[j], 1.0, 0.0)
    hits[...] = counted

    receive(0)
    rates = stress_rates([f[...] for f in av], lam[...], mu[...], velocity_faces(0))
    for i in range(6):
        as_[i][...] = a1[i] - rates[i]
    send_stress(1, [f[...] for f in as_])
    bx[0] = unpack_columns(r_xl[0], 1, 0)
    bx[1] = unpack_columns(r_xr[0], 2, 127)

    cross_s.wait_recv()
    relay_s.start()
    cross_v.wait_recv()
    relay_v.start()

    for name in ("peer", "slot", "own_s", "own_v"):
        loads[name].wait()
    pair_s.wait_recv()
    relay_s.wait_recv()
    where_is = [t_peer[gz, p] * 8 + t_slot[gz, p] for p in range(8)]
    for p in range(8):
        fs[:, p] = gath_s[where_is[p]].astype(jnp.float32)
    forward_edges(0)
    pair_v.wait_recv()
    relay_v.wait_recv()
    for p in range(8):
        fv[:, p] = gath_v[where_is[p]].astype(jnp.float32)
    forward_faces(0)

    receive(1)
    rates = velocity_rates([f[...] for f in as_], buoy[...], stress_faces(1))
    for i in range(3):
        av[i][...] = av[i][...] - rates[i]
    send_velocity(2, [f[...] for f in av])
    for i in range(3):
        a0[i] = a0[i] + as_[i][...]
    for i in range(3, 6):
        a0[i] = as_[i][...]

    receive(2)
    rates = stress_rates([f[...] for f in av], lam[...], mu[...], velocity_faces(2))
    for i in range(6):
        as_[i][...] = a0[i] - rates[i]
    send_stress(3, [f[...] for f in as_])

    forward_receive(0)
    rates = forward_step(0)
    pulse = hits[...] * t_wav[t_plan[0]]
    for i in range(3):
        fs[i] = fs[i] + rates[i] + pulse
    for i in range(3, 6):
        fs[i] = fs[i] + rates[i]
    forward_edges(1)
    forward_faces(1)

    def image(s, a):
        by_lambda = (s[0] + s[1] + s[2]) * (a[0] + a[1] + a[2])
        by_mu = s[0] * a[0] + s[1] * a[1] + s[2] * a[2] + 2.0 * (s[3] * a[3] + s[4] * a[4] + s[5] * a[5])
        return by_lambda, by_mu

    by_lambda, by_mu = image(fs, a0)
    il_out[...] = by_lambda
    im_out[...] = by_mu

    receive(3)
    rates = velocity_rates([f[...] for f in as_], buoy[...], stress_faces(3))
    for i in range(3):
        adj_out[i] = av[i][...] - rates[i]
    for i in range(6):
        adj_out[3 + i] = as_[i][...]
    sent(3)
    for copy in (cross_s, cross_v, pair_s, pair_v, relay_s, relay_v):
        copy.wait_send()

    forward_receive(1)
    rates = forward_step(1)
    pulse = hits[...] * t_wav[t_plan[1]]
    last = [fs[i] + rates[i] + pulse for i in range(3)] + [fs[i] + rates[i] for i in range(3, 6)]
    by_lambda, by_mu = image(last, a1)
    il_out[...] += by_lambda
    im_out[...] += by_mu
    forward_sent(1)


def write_out(adj, il, im, adj_out, il_out, im_out, sem):
    copies = [
        pltpu.make_async_copy(src, dst, sem.at[n])
        for n, (src, dst) in enumerate(((adj, adj_out), (il, il_out), (im, im_out)))
    ]
    for copy in copies:
        copy.start()
    for copy in copies:
        copy.wait()


def solution(mesh):
    sizes = (mesh.shape["gx"], mesh.shape["gy"], mesh.shape["gz"])
    f32, i32, bf16 = jnp.float32, jnp.int32, jnp.bfloat16
    brick = (8, 8, 128)

    def on_device(*args):
        nt, nrec = args[10].shape[-2:]
        nsrc = args[7].shape[-1]
        vmem = pltpu.VMEM
        scratch = [
            vmem((3,) + brick, f32),
            vmem((1, nrec), i32),
            vmem((nt, nrec), f32),
            pltpu.SMEM((4, 8), i32),
            pltpu.SMEM((4, 8), i32),
            pltpu.SMEM((nsrc,), i32),
            pltpu.SMEM((nt,), f32),
            pltpu.SMEM((STEPS,), i32),
            vmem((32, 6, 8, 128), bf16),
            vmem((32, 3, 8, 128), bf16),
            vmem((3,) + brick, f32),
            vmem((6,) + brick, f32),
            vmem((9,) + brick, f32),
            vmem((6,) + brick, f32),
            vmem((6,) + brick, f32),
            vmem((2,) + brick, f32),
            vmem(brick, f32),
        ]
        row, tile = (8, 1, 128), (8, 128)
        for _ in range(2):
            scratch += [vmem((4,) + tile, f32)] * 2 + [vmem((4, 3) + row, f32)] * 2 + [vmem((4, 3) + tile, f32)] * 2
        for down_y, down_z in ((5, 7), (3, 3)):
            received = down_y == 3
            scratch += [vmem((2,) + tile, f32)] * 2
            scratch += [vmem((2, 3 if received else 5) + row, f32), vmem((2, 3) + row, f32)]
            scratch += [vmem((2, 3 if received else 7) + tile, f32), vmem((2, 3) + tile, f32)]
        for shape in (row, tile, tile):
            scratch += [vmem((2, fields) + shape, f32) for fields in (1, 2, 1, 1)]
        dma = pltpu.SemaphoreType.DMA
        scratch += [dma((11,)), dma((6,)), dma((2, 6)), dma((18,)), dma((2, 18)), dma((6,)), dma((6,))]
        shapes = ((9,) + brick, brick, brick)
        results = pl.pallas_call(
            functools.partial(kernel, sizes),
            out_shape=tuple(pltpu.VMEM(shape, f32) for shape in shapes),
            in_specs=[pl.BlockSpec(memory_space=pl.ANY)] * 12,
            out_specs=(pl.BlockSpec(memory_space=pltpu.VMEM),) * 3,
            scratch_shapes=scratch,
            compiler_params=pltpu.CompilerParams(
                collective_id=0, has_side_effects=True
            ),
            name="window",
        )(*args)
        return pl.pallas_call(
            write_out,
            out_shape=tuple(jax.ShapeDtypeStruct(shape, f32) for shape in shapes),
            in_specs=[pl.BlockSpec(memory_space=pltpu.VMEM)] * 3,
            out_specs=(pl.BlockSpec(memory_space=pl.ANY),) * 3,
            scratch_shapes=[pltpu.SemaphoreType.DMA((3,))],
            compiler_params=pltpu.CompilerParams(vmem_limit_bytes=16 << 20),
            name="write_out",
        )(*results)

    return jax.shard_map(
        on_device,
        mesh=mesh,
        in_specs=(
            P("gz", None, None, "gy", "gx"),
            P("gx", "gy", None, None),
            P("gx", "gy", None, None),
            P(None, "gz", "gy", "gx"),
            P("gz", "gy", "gx"),
            P("gz", "gy", "gx"),
            P("gz", "gy", "gx"),
            P("gz", "gy", "gx", None),
            P(),
            P("gz", "gy", "gx", None),
            P("gz", "gy", "gx", None, None),
            P(),
        ),
        out_specs=(P(None, "gz", "gy", "gx"), P("gz", "gy", "gx"), P("gz", "gy", "gx")),
        check_vma=False,
    )
```

time: 30.1 us -> 27.9 us (0.927)
  Pallas kernels: 29.3 us -> 27.1 us
    pallas_call x1, Pallas kernels: 28.6 us -> 26.4 us  [on_device(): pl.pallas_call(functools.partial(kernel, sizes), out_shape=tuple((pltpu.V...]
where the time goes in v4:
time: 27.9 us; the launch traced here: 27.8 us
  Pallas kernels  27.1 us (97%)
  between operations  0.64 us (2%)
    pallas_call x1, Pallas kernels, on_device(): pl.pallas_call(functools.partial(kernel, sizes), out_shape=tuple((pltpu.V...  26.4 us
    pallas_call x1, Pallas kernels, on_device(): pl.pallas_call(write_out, out_shape=tuple((jax.ShapeDtypeStruct(shape, f3...  0.75 us

profile of v4, /device:TPU:66, one launch (start us, length us, event | category | flops | bytes accessed | tf_op | source)
XLA Modules:
  0.0 27.8 jit_solution(9767011195120403853)
XLA Ops:
  0.6 26.4 %window.1 = (f32[9,8,8,128]{3,2,1,0:T(8,128)S(1)}, f32[8,8,128]{2,1,0:T(8,128)S(1)}, f32[8,8,128]{2,1,0:T(8,128)S(1)}) custom-call(bf16[8,9,1,8,128]{4,3,2,1,0:T(8,128)(2,1)} %store.1, s32[1,1,4,8]{3,2,1,0:T(4,128)} %hpeer.1, s32[1,1,4,8]{3,2,1,0:T(4,128)} %hslot.1, f32[9,8,8,128]{3,2,1,0:T(8,128)} %adj_in.1, f32[8,8,128]{2,1,0:T(8,128)} %lam_in.1, ...), custom_call_target="tpu_custom_call" | custom-call | tf_op jit(solution)/shard_map/window/pallas_call | solution.py:710
  27.0 0.8 %write_out.1 = (f32[9,8,8,128]{3,2,1,0:T(8,128)}, f32[8,8,128]{2,1,0:T(8,128)}, f32[8,8,128]{2,1,0:T(8,128)}) custom-call(f32[9,8,8,128]{3,2,1,0:T(8,128)S(1)} %get-tuple-element.6.adj, f32[8,8,128]{2,1,0:T(8,128)S(1)} %get-tuple-element.7.il, f32[8,8,128]{2,1,0:T(8,128)S(1)} %get-tuple-element.8.im), custom_call_target="tpu_custom_call" | custom-call | tf_op jit(solution)/shard_map/write_out/pallas_call | solution.py:721

commit v5 on v4

--- a/solution.py
+++ b/solution.py
@@ -267,7 +267,9 @@
         )
 
     mine, theirs = pl.ds(gz * 8, 8), pl.ds(cross * 8, 8)
-    st_s, st_v = store.at[:, pl.ds(3, 6), 0], store.at[:, pl.ds(0, 3), 0]
+    st_s, st_v = gath_s.at[mine], gath_v.at[mine]
+    loads["own_s"].wait()
+    loads["own_v"].wait()
     cross_s = remote(st_s, gath_s.at[mine], 0, cross)
     cross_v = remote(st_v, gath_v.at[mine], 1, cross)
     pair_s = remote(st_s, gath_s.at[mine], 2, partner)
@@ -275,7 +277,6 @@
     relay_s = remote(gath_s.at[theirs], gath_s.at[theirs], 4, partner)
     relay_v = remote(gath_v.at[theirs], gath_v.at[theirs], 5, partner)
     cross_s.start()
-    cross_v.start()
     pair_s.start()
     pair_v.start()
 
@@ -573,6 +574,9 @@
         counted = counted + jnp.where(flat == t_src[j], 1.0, 0.0)
     hits[...] = counted
 
+    cross_s.wait_send()
+    cross_v.start()
+
     receive(0)
     rates = stress_rates([f[...] for f in av], lam[...], mu[...], velocity_faces(0))
     for i in range(6):
@@ -586,7 +590,7 @@
     cross_v.wait_recv()
     relay_v.start()
 
-    for name in ("peer", "slot", "own_s", "own_v"):
+    for name in ("peer", "slot"):
         loads[name].wait()
     pair_s.wait_recv()
     relay_s.wait_recv()
@@ -610,12 +614,6 @@
     for i in range(3, 6):
         a0[i] = as_[i][...]
 
-    receive(2)
-    rates = stress_rates([f[...] for f in av], lam[...], mu[...], velocity_faces(2))
-    for i in range(6):
-        as_[i][...] = a0[i] - rates[i]
-    send_stress(3, [f[...] for f in as_])
-
     forward_receive(0)
     rates = forward_step(0)
     pulse = hits[...] * t_wav[t_plan[0]]
@@ -626,6 +624,12 @@
     forward_edges(1)
     forward_faces(1)
 
+    receive(2)
+    rates = stress_rates([f[...] for f in av], lam[...], mu[...], velocity_faces(2))
+    for i in range(6):
+        as_[i][...] = a0[i] - rates[i]
+    send_stress(3, [f[...] for f in as_])
+
     def image(s, a):
         by_lambda = (s[0] + s[1] + s[2]) * (a[0] + a[1] + a[2])
         by_mu = s[0] * a[0] + s[1] * a[1] + s[2] * a[2] + 2.0 * (s[3] * a[3] + s[4] * a[4] + s[5] * a[5])
@@ -642,7 +646,7 @@
     for i in range(6):
         adj_out[3 + i] = as_[i][...]
     sent(3)
-    for copy in (cross_s, cross_v, pair_s, pair_v, relay_s, relay_v):
+    for copy in (cross_v, pair_s, pair_v, relay_s, relay_v):
         copy.wait_send()
 
     forward_receive(1)

time: 27.9 us -> 25.3 us (0.907)
  the two profiles are of different devices: /device:TPU:66 before, /device:TPU:34 now
where the time goes in v5:
time: 25.3 us; the launch traced here: 24.9 us
  Pallas kernels  24.3 us (96%)
  between operations  0.64 us (3%)
    pallas_call x1, Pallas kernels, on_device(): pl.pallas_call(functools.partial(kernel, sizes), out_shape=tuple((pltpu.V...  23.5 us
    pallas_call x1, Pallas kernels, on_device(): pl.pallas_call(write_out, out_shape=tuple((jax.ShapeDtypeStruct(shape, f3...  0.75 us

profile of v5, /device:TPU:34, one launch (start us, length us, event | category | flops | bytes accessed | tf_op | source)
XLA Modules:
  0.0 24.9 jit_solution(5073602409902179360)
XLA Ops:
  0.6 23.5 %window.1 = (f32[9,8,8,128]{3,2,1,0:T(8,128)S(1)}, f32[8,8,128]{2,1,0:T(8,128)S(1)}, f32[8,8,128]{2,1,0:T(8,128)S(1)}) custom-call(bf16[8,9,1,8,128]{4,3,2,1,0:T(8,128)(2,1)} %store.1, s32[1,1,4,8]{3,2,1,0:T(4,128)} %hpeer.1, s32[1,1,4,8]{3,2,1,0:T(4,128)} %hslot.1, f32[9,8,8,128]{3,2,1,0:T(8,128)} %adj_in.1, f32[8,8,128]{2,1,0:T(8,128)} %lam_in.1, ...), custom_call_target="tpu_custom_call" | custom-call | tf_op jit(solution)/shard_map/window/pallas_call | solution.py:714
  24.2 0.8 %write_out.1 = (f32[9,8,8,128]{3,2,1,0:T(8,128)}, f32[8,8,128]{2,1,0:T(8,128)}, f32[8,8,128]{2,1,0:T(8,128)}) custom-call(f32[9,8,8,128]{3,2,1,0:T(8,128)S(1)} %get-tuple-element.6.adj, f32[8,8,128]{2,1,0:T(8,128)S(1)} %get-tuple-element.7.il, f32[8,8,128]{2,1,0:T(8,128)S(1)} %get-tuple-element.8.im), custom_call_target="tpu_custom_call" | custom-call | tf_op jit(solution)/shard_map/write_out/pallas_call | solution.py:725

commit v6 on v4

--- a/solution.py
+++ b/solution.py
@@ -9,6 +9,7 @@
 
 MESH = pl.DeviceIdType.MESH
 STEPS = 2
+CAP = 5
 
 GREETED = ((1, 0, 0), (-1, 0, 0), (0, 1, 0), (0, -1, 0))
 
@@ -113,14 +114,20 @@
     t_src,
     t_wav,
     t_plan,
-    gath_s,
-    gath_v,
+    own_s,
+    own_v,
+    stage_s,
+    stage_v,
+    got_s,
+    got_v,
     fv,
     fs,
     adj,
     a1,
     a0,
     bx,
+    mx,
+    lx,
     hits,
     s_xl,
     s_xr,
@@ -146,6 +153,24 @@
     g_yr,
     g_zl,
     g_zr,
+    c_xl,
+    c_xr,
+    c_yl,
+    c_yr,
+    c_zl,
+    c_zr,
+    d_xl,
+    d_xr,
+    d_yl,
+    d_yr,
+    d_zl,
+    d_zr,
+    vxy_pm,
+    vxy_mp,
+    vxz_pm,
+    vxz_mp,
+    vyz_pm,
+    vyz_mp,
     exy_mm,
     exy_pp,
     exy_pm,
@@ -161,16 +186,17 @@
     in_sem,
     send_sem,
     recv_sem,
+    asend_sem,
+    arecv_sem,
     fsend_sem,
     frecv_sem,
     rs_send,
     rs_recv,
+    ready,
 ):
     count = dict(zip(("gx", "gy", "gz"), sizes))
     index = {axis: lax.axis_index(axis) for axis in ("gx", "gy", "gz")}
     gz = index["gz"]
-    partner = gz + 1 - 2 * lax.rem(gz, 2)
-    cross = lax.rem(gz + 2, 4)
 
     def exists(step):
         found = None
@@ -188,14 +214,14 @@
     def greet(where):
         pl.semaphore_signal(barrier, inc=1, device_id=where, device_id_type=MESH)
 
-    greeted = 3
+    around = jnp.int32(0)
     for step in GREETED:
 
         @pl.when(exists(step))
         def _():
             greet(at(step))
 
-        greeted = greeted + exists(step).astype(jnp.int32)
+        around = around + exists(step).astype(jnp.int32)
     for d in (1, 2, 3):
         greet({"gz": lax.rem(gz + d, 4)})
 
@@ -203,6 +229,10 @@
         return pltpu.make_async_copy(src, dst, in_sem.at[n])
 
     loads = dict(
+        peer=local(hpeer.at[0, 0], t_peer, 7),
+        slot=local(hslot.at[0, 0], t_slot, 8),
+        own_s=local(store.at[:, pl.ds(3, 6), 0], own_s, 9),
+        own_v=local(store.at[:, pl.ds(0, 3), 0], own_v, 10),
         adj=local(adj_in, adj, 0),
         lam=local(lam_in, params.at[0], 1),
         mu=local(mu_in, params.at[1], 1),
@@ -212,10 +242,6 @@
         plan=local(plan_in, t_plan, 4),
         wav=local(wav_in, t_wav, 5),
         src=local(src_in.at[0, 0, 0], t_src, 6),
-        peer=local(hpeer.at[0, 0], t_peer, 7),
-        slot=local(hslot.at[0, 0], t_slot, 8),
-        own_s=local(store.at[:, pl.ds(3, 6), 0], gath_s.at[pl.ds(gz * 8, 8)], 9),
-        own_v=local(store.at[:, pl.ds(0, 3), 0], gath_v.at[pl.ds(gz * 8, 8)], 10),
     )
     for copy in loads.values():
         copy.start()
@@ -236,48 +262,39 @@
             (eyz_mp, (0, 1, -1), f_zl.at[e, pl.ds(6, 1)]),
         )
 
+    adjoint_messages = (
+        (d_xl, (1, 0, 0), c_xr),
+        (d_xr, (-1, 0, 0), c_xl),
+        (d_yl, (0, 1, 0), c_yr),
+        (d_yr, (0, -1, 0), c_yl),
+        (d_zl, (0, 0, 1), c_zr),
+        (d_zr, (0, 0, -1), c_zl),
+        (vxy_pm, (-1, 1, 0), c_yr.at[0]),
+        (vxy_mp, (1, -1, 0), c_yl.at[0]),
+        (vxz_pm, (-1, 0, 1), c_zr.at[0]),
+        (vxz_mp, (1, 0, -1), c_zl.at[0]),
+        (vyz_pm, (0, -1, 1), c_zr.at[0]),
+        (vyz_mp, (0, 1, -1), c_zl.at[1]),
+    )
+
     def back(step):
         return tuple(-d for d in step)
 
     for step, refs in (
-        ((-1, 0, 0), (r_xl, g_xl)),
-        ((1, 0, 0), (r_xr, g_xr)),
-        ((0, -1, 0), (r_yl, g_yl)),
-        ((0, 1, 0), (r_yr, g_yr)),
-        ((0, 0, -1), (r_zl, g_zl)),
-        ((0, 0, 1), (r_zr, g_zr)),
+        ((-1, 0, 0), (r_xl, g_xl, d_xl)),
+        ((1, 0, 0), (r_xr, g_xr, d_xr)),
+        ((0, -1, 0), (r_yl, g_yl, d_yl)),
+        ((0, 1, 0), (r_yr, g_yr, d_yr)),
+        ((0, 0, -1), (r_zl, g_zl, d_zl)),
+        ((0, 0, 1), (r_zr, g_zr, d_zr)),
         *((back(step), (ref,)) for ref, step, _ in edges(0)),
+        *((back(step), (ref,)) for ref, step, _ in adjoint_messages[6:]),
     ):
 
         @pl.when(jnp.logical_not(exists(step)))
         def _():
             for ref in refs:
                 ref[...] = jnp.zeros(ref.shape, jnp.float32)
-
-    pl.semaphore_wait(barrier, greeted)
-
-    def remote(src, dst, n, where):
-        return pltpu.make_async_remote_copy(
-            src_ref=src,
-            dst_ref=dst,
-            send_sem=rs_send.at[n],
-            recv_sem=rs_recv.at[n],
-            device_id={"gz": where},
-            device_id_type=MESH,
-        )
-
-    mine, theirs = pl.ds(gz * 8, 8), pl.ds(cross * 8, 8)
-    st_s, st_v = store.at[:, pl.ds(3, 6), 0], store.at[:, pl.ds(0, 3), 0]
-    cross_s = remote(st_s, gath_s.at[mine], 0, cross)
-    cross_v = remote(st_v, gath_v.at[mine], 1, cross)
-    pair_s = remote(st_s, gath_s.at[mine], 2, partner)
-    pair_v = remote(st_v, gath_v.at[mine], 3, partner)
-    relay_s = remote(gath_s.at[theirs], gath_s.at[theirs], 4, partner)
-    relay_v = remote(gath_v.at[theirs], gath_v.at[theirs], 5, partner)
-    cross_s.start()
-    cross_v.start()
-    pair_s.start()
-    pair_v.start()
 
     lam, mu, buoy = params.at[0], params.at[1], params.at[2]
     av, as_ = [adj.at[i] for i in range(3)], [adj.at[3 + i] for i in range(6)]
@@ -307,7 +324,7 @@
         )
         return copy, exists(step), exists(back(step))
 
-    COUNTS = ((2, 3), (2, 1), (1, 2), (2, 1))
+    COUNTS = ((3, 5), (2, 1))
 
     def sent(r):
         for d in range(6):
@@ -317,44 +334,104 @@
             def _():
                 copy.wait_send()
 
-    def send_faces(r, up, down):
+    def fill_faces(r, up, down):
         (xu, yu, zu), (xd, yd, zd) = up, down
-        if r > 0:
-            sent(r - 1)
-
-        def start(d):
-            copy, goes, _ = face(r, d, COUNTS[r][d % 2])
-
-            @pl.when(goes)
-            def _():
-                copy.start()
-
         s_xr[r] = pack_columns(xu, 127)
         s_xl[r] = pack_columns(xd, 0)
-        start(0)
-        start(1)
         for i, f in enumerate(zu):
             s_zr[r, i] = f[7]
         for i, f in enumerate(zd):
             s_zl[r, i] = f[0]
-        start(4)
-        start(5)
         for i, f in enumerate(yu):
             s_yr[r, i] = f[:, 7:8, :]
         for i, f in enumerate(yd):
             s_yl[r, i] = f[:, 0:1, :]
-        start(2)
-        start(3)
+
+    def start_faces(r):
+        for d in (0, 1, 4, 5, 2, 3):
+            copy, goes, _ = face(r, d, COUNTS[r][d % 2])
+
+            @pl.when(goes)
+            def _():
+                copy.start()
+
+    def fill_velocity():
+        v, b, l, m = [f[...] for f in av], buoy[...], lam[...], mu[...]
+        more, most = (b, m), (b, l, m)
+        fill_faces(
+            0,
+            ((v[0], *more), (v[1], *more), (v[2], *more)),
+            ((v[1], v[2], *most), (v[0], v[2], *most), (v[0], v[1], *most)),
+        )
+
+    def send_velocity(r):
+        start_faces(r)
 
     def send_stress(r, s):
-        send_faces(r, ((s[3], s[4]), (s[3], s[5]), (s[4], s[5])), ((s[0],), (s[1],), (s[2],)))
-
-    def send_velocity(r, v, more=()):
-        send_faces(
-            r,
-            ((v[0], *more), (v[1], *more), (v[2], *more)),
-            ((v[1], v[2], *more), (v[0], v[2], *more), (v[0], v[1], *more)),
-        )
+        sent(r - 1)
+        fill_faces(r, ((s[3], s[4]), (s[3], s[5]), (s[4], s[5])), ((s[0],), (s[1],), (s[2],)))
+        start_faces(r)
+
+    for name in ("peer", "slot", "own_s"):
+        loads[name].wait()
+    slots = []
+    for d in range(4):
+        brick = lax.rem(gz + d, 4)
+        listed, shift = jnp.int32(0), jnp.int32(0)
+        for p in range(8):
+            held = t_peer[brick, p] == gz
+            listed = jnp.where(held, listed + lax.shift_left(t_slot[brick, p], shift), listed)
+            shift = jnp.where(held, shift + 3, shift)
+        slots.append([lax.bitwise_and(lax.shift_right_logical(listed, 3 * j), 7) for j in range(CAP)])
+
+    def stage(own, staged, got):
+        for d in (2, 1, 3, 0):
+            for j in range(CAP):
+                if d:
+                    staged[(d - 1) * CAP + j] = own[slots[d][j]]
+                else:
+                    got[3 * CAP + j] = own[slots[d][j]]
+
+    def restore(staged, got, n):
+        for d in (2, 1, 3):
+            rows = pl.ds((d - 1) * CAP, CAP)
+            pltpu.make_async_remote_copy(
+                src_ref=staged.at[rows],
+                dst_ref=got.at[rows],
+                send_sem=rs_send.at[n],
+                recv_sem=rs_recv.at[n],
+                device_id={"gz": lax.rem(gz + d, 4)},
+                device_id_type=MESH,
+            ).start()
+
+    def restored(got, n):
+        rows = got.at[pl.ds(0, 3 * CAP)]
+        pltpu.make_async_copy(rows, rows, rs_recv.at[n]).wait()
+
+    where_is, seen = [], jnp.int32(0)
+    for p in range(8):
+        holder = t_peer[gz, p]
+        at_digit = holder * 4
+        before = lax.bitwise_and(lax.shift_right_logical(seen, at_digit), 15)
+        where_is.append(lax.bitwise_and(gz - holder + 3, 3) * CAP + jnp.minimum(before, CAP - 1))
+        seen = seen + lax.shift_left(jnp.int32(1), at_digit)
+
+    stage(own_s, stage_s, got_s)
+    loads["adj"].wait()
+    pltpu.make_async_copy(params, params, in_sem.at[1]).wait()
+    fill_velocity()
+    pl.semaphore_wait(barrier, around + 3)
+    send_velocity(0)
+    restore(stage_s, got_s, 0)
+
+    for step in GREETED:
+
+        @pl.when(exists(step))
+        def _():
+            pl.semaphore_signal(ready, inc=1, device_id=at(step), device_id_type=MESH)
+
+    loads["own_v"].wait()
+    stage(own_v, stage_v, got_v)
 
     def receive(r):
         for d in range(6):
@@ -541,9 +618,128 @@
         fv[2, 7] = fv[2, 7] + buoy[7] * g_zr[e, 2]
         return stress_rates([fv[i] for i in range(3)], lam[...], mu[...], h)
 
-    loads["adj"].wait()
-    pltpu.make_async_copy(params, params, in_sem.at[1]).wait()
-    send_velocity(0, [f[...] for f in av], (buoy[...],))
+    def adjoint_message(n):
+        target, step, source = adjoint_messages[n]
+        copy = pltpu.make_async_remote_copy(
+            src_ref=source,
+            dst_ref=target,
+            send_sem=asend_sem.at[n],
+            recv_sem=arecv_sem.at[n],
+            device_id=at(step),
+            device_id_type=MESH,
+        )
+        return copy, exists(step), exists(back(step))
+
+    def adjoint_start(*which):
+        for n in which:
+            copy, goes, _ = adjoint_message(n)
+
+            @pl.when(goes)
+            def _():
+                copy.start()
+
+    def adjoint_sent():
+        for n in range(12):
+            copy, goes, _ = adjoint_message(n)
+
+            @pl.when(goes)
+            def _():
+                copy.wait_send()
+
+    def adjoint_receive():
+        for n in range(12):
+            copy, _, comes = adjoint_message(n)
+
+            @pl.when(comes)
+            def _():
+                copy.wait_recv()
+
+    def adjoint_send():
+        c_yr[0] = av[1][:, 7:8, :]
+        c_yl[0] = av[0][:, 0:1, :]
+        c_yl[1] = av[2][:, 0:1, :]
+        adjoint_start(6, 7)
+        c_zr[0] = av[2][7]
+        c_zl[0] = av[0][0]
+        c_zl[1] = av[1][0]
+        adjoint_start(8, 9, 10, 11)
+        v = [f[...] for f in av]
+        rates = stress_rates(v, lam[...], mu[...], Zeros())
+        s = [a0[i] - rates[i] for i in range(6)]
+        c_xr[...] = pack_columns((v[0], s[3], s[4]), 127)
+        c_xl[...] = pack_columns((v[1], v[2], s[0]), 0)
+        adjoint_start(0, 1)
+        c_zr[1] = s[4][7]
+        c_zr[2] = s[5][7]
+        c_zl[2] = s[2][0]
+        adjoint_start(4, 5)
+        c_yr[1] = s[3][:, 7:8, :]
+        c_yr[2] = s[5][:, 7:8, :]
+        c_yl[2] = s[1][:, 0:1, :]
+        adjoint_start(2, 3)
+
+    def adjoint_step():
+        v = [f[...] for f in av]
+        xl, xr = d_xl[...], d_xr[...]
+        lane2, row2 = iota2(1), iota2(0)
+        all3 = (8, 8, 128)
+        z1 = lax.broadcasted_iota(jnp.int32, (8, 1, 128), 0)
+        lane1 = lax.broadcasted_iota(jnp.int32, (8, 1, 128), 2)
+        h = {
+            ("xl", 0): unpack_columns(xl, 0, 0),
+            ("xr", 1): unpack_columns(xr, 0, 127),
+            ("xr", 2): unpack_columns(xr, 1, 127),
+            ("yl", 1): d_yl[0],
+            ("yr", 0): d_yr[0],
+            ("yr", 2): d_yr[1],
+            ("zl", 2): d_zl[0],
+            ("zr", 0): d_zr[0],
+            ("zr", 1): d_zr[1],
+        }
+        rates = stress_rates(v, lam[...], mu[...], h)
+        s = [a0[i] - rates[i] for i in range(6)]
+
+        xy_pm, xy_mp = pltpu.roll(vxy_pm[...], 127, 2), pltpu.roll(vxy_mp[...], 1, 2)
+        xz_pm, xz_mp = pltpu.roll(vxz_pm[...], 127, 1), pltpu.roll(vxz_mp[...], 1, 1)
+
+        def row(at_y, face):
+            return jnp.where(iota3(1) == at_y, jnp.broadcast_to(face, all3), 0.0)
+
+        def layer(at_z, tile):
+            return jnp.where(iota3(0) == at_z, tile[None], 0.0)
+
+        def y_layer(at_z, tile, at_y):
+            return jnp.where(z1 == at_z, jnp.broadcast_to(tile[at_y : at_y + 1, :][None], (8, 1, 128)), 0.0)
+
+        def y_edge(tile, at_y, from_y):
+            return jnp.where(row2 == at_y, jnp.broadcast_to(tile[from_y : from_y + 1, :], (8, 128)), 0.0)
+
+        both = lx[...] + 2.0 * mx[1]
+        g = {}
+        g["xl", 3] = unpack_columns(xl, 1, 0) - mx[0] * (v[1] + row(7, xy_mp))
+        g["xl", 4] = unpack_columns(xl, 2, 0) - mx[0] * (v[2] + layer(7, xz_mp))
+        g["xr", 0] = unpack_columns(xr, 2, 127) + both * v[0] + lx[...] * (row(0, xy_pm) + layer(0, xz_pm))
+        mu_m, lam_p, mu_p = r_yl[0, 2], r_yr[0, 3], r_yr[0, 4]
+        g["yl", 3] = d_yl[1] - mu_m * (v[0][:, 0:1, :] + jnp.where(lane1 == 127, xy_pm, 0.0))
+        g["yl", 5] = d_yl[2] - mu_m * (v[2][:, 0:1, :] + y_layer(7, vyz_mp[...], 7))
+        g["yr", 1] = (
+            d_yr[2]
+            + (lam_p + 2.0 * mu_p) * v[1][:, 7:8, :]
+            + lam_p * (jnp.where(lane1 == 0, xy_mp, 0.0) + y_layer(0, vyz_pm[...], 0))
+        )
+        mu_m, lam_p, mu_p = r_zl[0, 2], r_zr[0, 3], r_zr[0, 4]
+        g["zl", 4] = d_zl[1] - mu_m * (v[0][0] + jnp.where(lane2 == 127, xz_pm, 0.0))
+        g["zl", 5] = d_zl[2] - mu_m * (v[1][0] + y_edge(vyz_pm[...], 7, 0))
+        g["zr", 2] = (
+            d_zr[2]
+            + (lam_p + 2.0 * mu_p) * v[2][7]
+            + lam_p * (jnp.where(lane2 == 0, xz_mp, 0.0) + y_edge(vyz_mp[...], 0, 7))
+        )
+        for i in range(6):
+            adj_out[3 + i] = s[i]
+        rates = velocity_rates(s, buoy[...], g)
+        for i in range(3):
+            adj_out[i] = v[i] - rates[i]
 
     for name in ("rec", "traces", "plan"):
         loads[name].wait()
@@ -573,48 +769,38 @@
         counted = counted + jnp.where(flat == t_src[j], 1.0, 0.0)
     hits[...] = counted
 
+    restore(stage_v, got_v, 1)
+
+    restored(got_s, 0)
+    for p in range(8):
+        fs[:, p] = got_s[where_is[p]].astype(jnp.float32)
+    pl.semaphore_wait(ready, around)
+    forward_edges(0)
     receive(0)
     rates = stress_rates([f[...] for f in av], lam[...], mu[...], velocity_faces(0))
     for i in range(6):
         as_[i][...] = a1[i] - rates[i]
     send_stress(1, [f[...] for f in as_])
     bx[0] = unpack_columns(r_xl[0], 1, 0)
+    mx[0] = unpack_columns(r_xl[0], 2, 0)
     bx[1] = unpack_columns(r_xr[0], 2, 127)
-
-    cross_s.wait_recv()
-    relay_s.start()
-    cross_v.wait_recv()
-    relay_v.start()
-
-    for name in ("peer", "slot", "own_s", "own_v"):
-        loads[name].wait()
-    pair_s.wait_recv()
-    relay_s.wait_recv()
-    where_is = [t_peer[gz, p] * 8 + t_slot[gz, p] for p in range(8)]
+    lx[...] = unpack_columns(r_xr[0], 3, 127)
+    mx[1] = unpack_columns(r_xr[0], 4, 127)
+
+    restored(got_v, 1)
     for p in range(8):
-        fs[:, p] = gath_s[where_is[p]].astype(jnp.float32)
-    forward_edges(0)
-    pair_v.wait_recv()
-    relay_v.wait_recv()
-    for p in range(8):
-        fv[:, p] = gath_v[where_is[p]].astype(jnp.float32)
+        fv[:, p] = got_v[where_is[p]].astype(jnp.float32)
     forward_faces(0)
 
     receive(1)
     rates = velocity_rates([f[...] for f in as_], buoy[...], stress_faces(1))
     for i in range(3):
         av[i][...] = av[i][...] - rates[i]
-    send_velocity(2, [f[...] for f in av])
     for i in range(3):
         a0[i] = a0[i] + as_[i][...]
     for i in range(3, 6):
         a0[i] = as_[i][...]
-
-    receive(2)
-    rates = stress_rates([f[...] for f in av], lam[...], mu[...], velocity_faces(2))
-    for i in range(6):
-        as_[i][...] = a0[i] - rates[i]
-    send_stress(3, [f[...] for f in as_])
+    adjoint_send()
 
     forward_receive(0)
     rates = forward_step(0)
@@ -635,15 +821,12 @@
     il_out[...] = by_lambda
     im_out[...] = by_mu
 
-    receive(3)
-    rates = velocity_rates([f[...] for f in as_], buoy[...], stress_faces(3))
-    for i in range(3):
-        adj_out[i] = av[i][...] - rates[i]
-    for i in range(6):
-        adj_out[3 + i] = as_[i][...]
-    sent(3)
-    for copy in (cross_s, cross_v, pair_s, pair_v, relay_s, relay_v):
-        copy.wait_send()
+    adjoint_receive()
+    adjoint_step()
+    sent(1)
+    adjoint_sent()
+    for n, staged in enumerate((stage_s, stage_v)):
+        pltpu.make_async_copy(staged, staged, rs_send.at[n]).wait()
 
     forward_receive(1)
     rates = forward_step(1)
@@ -684,28 +867,37 @@
             pltpu.SMEM((nsrc,), i32),
             pltpu.SMEM((nt,), f32),
             pltpu.SMEM((STEPS,), i32),
-            vmem((32, 6, 8, 128), bf16),
-            vmem((32, 3, 8, 128), bf16),
+            vmem((8, 6, 8, 128), bf16),
+            vmem((8, 3, 8, 128), bf16),
+            vmem((3 * CAP, 6, 8, 128), bf16),
+            vmem((3 * CAP, 3, 8, 128), bf16),
+            vmem((4 * CAP, 6, 8, 128), bf16),
+            vmem((4 * CAP, 3, 8, 128), bf16),
             vmem((3,) + brick, f32),
             vmem((6,) + brick, f32),
             vmem((9,) + brick, f32),
             vmem((6,) + brick, f32),
             vmem((6,) + brick, f32),
             vmem((2,) + brick, f32),
+            vmem((2,) + brick, f32),
+            vmem(brick, f32),
             vmem(brick, f32),
         ]
         row, tile = (8, 1, 128), (8, 128)
         for _ in range(2):
-            scratch += [vmem((4,) + tile, f32)] * 2 + [vmem((4, 3) + row, f32)] * 2 + [vmem((4, 3) + tile, f32)] * 2
+            scratch += [vmem((2,) + tile, f32)] * 2 + [vmem((2, 5) + row, f32)] * 2 + [vmem((2, 5) + tile, f32)] * 2
         for down_y, down_z in ((5, 7), (3, 3)):
             received = down_y == 3
             scratch += [vmem((2,) + tile, f32)] * 2
             scratch += [vmem((2, 3 if received else 5) + row, f32), vmem((2, 3) + row, f32)]
             scratch += [vmem((2, 3 if received else 7) + tile, f32), vmem((2, 3) + tile, f32)]
+        for _ in range(2):
+            scratch += [vmem(tile, f32)] * 2 + [vmem((3,) + row, f32)] * 2 + [vmem((3,) + tile, f32)] * 2
+        scratch += [vmem(row, f32)] * 2 + [vmem(tile, f32)] * 4
         for shape in (row, tile, tile):
             scratch += [vmem((2, fields) + shape, f32) for fields in (1, 2, 1, 1)]
         dma = pltpu.SemaphoreType.DMA
-        scratch += [dma((11,)), dma((6,)), dma((2, 6)), dma((18,)), dma((2, 18)), dma((6,)), dma((6,))]
+        scratch += [dma((11,)), dma((6,)), dma((2, 6)), dma((12,)), dma((12,)), dma((18,)), dma((2, 18)), dma((2,)), dma((2,)), pltpu.SemaphoreType.REGULAR]
         shapes = ((9,) + brick, brick, brick)
         results = pl.pallas_call(
             functools.partial(kernel, sizes),

time: 27.9 us -> 23.5 us (0.84)
  the two profiles are of different devices: /device:TPU:66 before, /device:TPU:34 now
where the time goes in v6:
time: 23.5 us; the launch traced here: 23.4 us
  Pallas kernels  22.8 us (97%)
  between operations  0.64 us (3%)
    pallas_call x1, Pallas kernels, on_device(): pl.pallas_call(functools.partial(kernel, sizes), out_shape=tuple((pltpu.V...  22 us
    pallas_call x1, Pallas kernels, on_device(): pl.pallas_call(write_out, out_shape=tuple((jax.ShapeDtypeStruct(shape, f3...  0.75 us

profile of v6, /device:TPU:34, one launch (start us, length us, event | category | flops | bytes accessed | tf_op | source)
XLA Modules:
  0.0 23.4 jit_solution(12047062009741605513)
XLA Ops:
  0.6 22.0 %window.1 = (f32[9,8,8,128]{3,2,1,0:T(8,128)S(1)}, f32[8,8,128]{2,1,0:T(8,128)S(1)}, f32[8,8,128]{2,1,0:T(8,128)S(1)}) custom-call(bf16[8,9,1,8,128]{4,3,2,1,0:T(8,128)(2,1)} %store.1, s32[1,1,4,8]{3,2,1,0:T(4,128)} %hpeer.1, s32[1,1,4,8]{3,2,1,0:T(4,128)} %hslot.1, f32[9,8,8,128]{3,2,1,0:T(8,128)} %adj_in.1, f32[8,8,128]{2,1,0:T(8,128)} %lam_in.1, ...), custom_call_target="tpu_custom_call" | custom-call | tf_op jit(solution)/shard_map/window/pallas_call | solution.py:902
  22.7 0.8 %write_out.1 = (f32[9,8,8,128]{3,2,1,0:T(8,128)}, f32[8,8,128]{2,1,0:T(8,128)}, f32[8,8,128]{2,1,0:T(8,128)}) custom-call(f32[9,8,8,128]{3,2,1,0:T(8,128)S(1)} %get-tuple-element.6.adj, f32[8,8,128]{2,1,0:T(8,128)S(1)} %get-tuple-element.7.il, f32[8,8,128]{2,1,0:T(8,128)S(1)} %get-tuple-element.8.im), custom_call_target="tpu_custom_call" | custom-call | tf_op jit(solution)/shard_map/write_out/pallas_call | solution.py:913

commit v7 on v6

--- a/solution.py
+++ b/solution.py
@@ -87,6 +87,67 @@
         side = key[0]
         shape = (8, 1, 128) if side[0] == "y" else (8, 128)
         return jnp.zeros((8, 8, 128) if side[0] == "x" else shape, jnp.float32)
+
+
+class Part:
+    def __init__(self, kind, places):
+        self.kind, self.places = kind, places
+
+    def __getitem__(self, key):
+        e, i = key if isinstance(key, tuple) else (key, 0)
+        ref, first, _ = self.places[e]
+        return ref[first + i]
+
+    def at(self, e):
+        ref, first, count = self.places[e]
+        return ref.at[pl.ds(first, count)]
+
+
+class Exchange:
+    def __init__(self, e, buffers, spare, send, recv, messages, to, exists):
+        self.e, self.buffers, self.spare, self.send, self.recv = e, buffers, spare, send, recv
+        self.messages, self.to, self.exists = messages, to, exists
+
+    def prepare(self):
+        for part, step, _ in self.messages:
+            target = part.at(self.e)
+            _, first, count = part.places[self.e]
+            aside = self.spare[part.kind].at[pl.ds(first, count)]
+
+            @pl.when(jnp.logical_not(self.exists(step)))
+            def _():
+                zeros = self.spare[2 + part.kind].at[pl.ds(0, count)]
+                pltpu.make_async_copy(zeros, aside, self.send.at[part.kind]).start()
+
+            @pl.when(jnp.logical_not(self.exists(tuple(-d for d in step))))
+            def _():
+                zeros = self.spare[2 + part.kind].at[pl.ds(0, count)]
+                pltpu.make_async_copy(zeros, target, self.recv.at[part.kind]).start()
+
+    def start(self, *which):
+        for n in which:
+            part, step, source = self.messages[n]
+
+            @pl.when(self.exists(step))
+            def _():
+                pltpu.make_async_remote_copy(
+                    src_ref=source,
+                    dst_ref=part.at(self.e),
+                    send_sem=self.send.at[part.kind],
+                    recv_sem=self.recv.at[part.kind],
+                    device_id=self.to(step),
+                    device_id_type=MESH,
+                ).start()
+
+    def all_of(self, sems):
+        for kind, ref in enumerate(self.buffers):
+            pltpu.make_async_copy(ref, ref, sems.at[kind]).wait()
+
+    def sent(self):
+        self.all_of(self.send)
+
+    def receive(self):
+        self.all_of(self.recv)
 
 
 def kernel(
@@ -135,59 +196,43 @@
     s_yr,
     s_zl,
     s_zr,
-    r_xl,
-    r_xr,
-    r_yl,
-    r_yr,
-    r_zl,
-    r_zr,
+    r0_tiles,
+    r0_rows,
+    r1_tiles,
+    r1_rows,
     f_xl,
     f_xr,
     f_yl,
     f_yr,
     f_zl,
     f_zr,
-    g_xl,
-    g_xr,
-    g_yl,
-    g_yr,
-    g_zl,
-    g_zr,
+    g0_tiles,
+    g0_rows,
+    g1_tiles,
+    g1_rows,
     c_xl,
     c_xr,
     c_yl,
     c_yr,
     c_zl,
     c_zr,
-    d_xl,
-    d_xr,
-    d_yl,
-    d_yr,
-    d_zl,
-    d_zr,
-    vxy_pm,
-    vxy_mp,
-    vxz_pm,
-    vxz_mp,
-    vyz_pm,
-    vyz_mp,
-    exy_mm,
-    exy_pp,
-    exy_pm,
-    exy_mp,
-    exz_mm,
-    exz_pp,
-    exz_pm,
-    exz_mp,
-    eyz_mm,
-    eyz_pp,
-    eyz_pm,
-    eyz_mp,
+    d_tiles,
+    d_rows,
+    ar0_tiles,
+    ar0_rows,
+    ar1_tiles,
+    ar1_rows,
+    ad_tiles,
+    ad_rows,
+    ag0_tiles,
+    ag0_rows,
+    ag1_tiles,
+    ag1_rows,
+    no_tiles,
+    no_rows,
     in_sem,
     send_sem,
     recv_sem,
-    asend_sem,
-    arecv_sem,
     fsend_sem,
     frecv_sem,
     rs_send,
@@ -198,16 +243,18 @@
     index = {axis: lax.axis_index(axis) for axis in ("gx", "gy", "gz")}
     gz = index["gz"]
 
+    axes = ("gx", "gy", "gz")
+
     def exists(step):
         found = None
-        for axis, d in zip(("gx", "gy", "gz"), step):
+        for axis, d in zip(axes, step):
             if d:
                 here = index[axis] < count[axis] - 1 if d > 0 else index[axis] > 0
                 found = here if found is None else jnp.logical_and(found, here)
         return found
 
     def at(step):
-        return {axis: index[axis] + d for axis, d in zip(("gx", "gy", "gz"), step) if d}
+        return {axis: index[axis] + d for axis, d in zip(axes, step) if d}
 
     barrier = pltpu.get_barrier_semaphore()
 
@@ -246,98 +293,137 @@
     for copy in loads.values():
         copy.start()
 
-    def edges(e):
-        return (
-            (exy_mm, (1, 1, 0), f_yr.at[e, pl.ds(0, 1)]),
-            (exy_pp, (-1, -1, 0), f_yl.at[e, pl.ds(2, 2)]),
-            (exy_pm, (-1, 1, 0), f_yr.at[e, pl.ds(1, 1)]),
-            (exy_mp, (1, -1, 0), f_yl.at[e, pl.ds(4, 1)]),
-            (exz_mm, (1, 0, 1), f_zr.at[e, pl.ds(0, 1)]),
-            (exz_pp, (-1, 0, -1), f_zl.at[e, pl.ds(2, 2)]),
-            (exz_pm, (-1, 0, 1), f_zr.at[e, pl.ds(1, 1)]),
-            (exz_mp, (1, 0, -1), f_zl.at[e, pl.ds(6, 1)]),
-            (eyz_mm, (0, 1, 1), f_zr.at[e, pl.ds(1, 1)]),
-            (eyz_pp, (0, -1, -1), f_zl.at[e, pl.ds(4, 2)]),
-            (eyz_pm, (0, -1, 1), f_zr.at[e, pl.ds(0, 1)]),
-            (eyz_mp, (0, 1, -1), f_zl.at[e, pl.ds(6, 1)]),
-        )
-
-    adjoint_messages = (
-        (d_xl, (1, 0, 0), c_xr),
-        (d_xr, (-1, 0, 0), c_xl),
-        (d_yl, (0, 1, 0), c_yr),
-        (d_yr, (0, -1, 0), c_yl),
-        (d_zl, (0, 0, 1), c_zr),
-        (d_zr, (0, 0, -1), c_zl),
-        (vxy_pm, (-1, 1, 0), c_yr.at[0]),
-        (vxy_mp, (1, -1, 0), c_yl.at[0]),
-        (vxz_pm, (-1, 0, 1), c_zr.at[0]),
-        (vxz_mp, (1, 0, -1), c_zl.at[0]),
-        (vyz_pm, (0, -1, 1), c_zr.at[0]),
-        (vyz_mp, (0, 1, -1), c_zl.at[1]),
+    TILES, ROWS = 0, 1
+    first, second, forward0, forward1, last_one = (
+        (r0_tiles, r0_rows),
+        (r1_tiles, r1_rows),
+        (g0_tiles, g0_rows),
+        (g1_tiles, g1_rows),
+        (d_tiles, d_rows),
     )
 
-    def back(step):
-        return tuple(-d for d in step)
-
-    for step, refs in (
-        ((-1, 0, 0), (r_xl, g_xl, d_xl)),
-        ((1, 0, 0), (r_xr, g_xr, d_xr)),
-        ((0, -1, 0), (r_yl, g_yl, d_yl)),
-        ((0, 1, 0), (r_yr, g_yr, d_yr)),
-        ((0, 0, -1), (r_zl, g_zl, d_zl)),
-        ((0, 0, 1), (r_zr, g_zr, d_zr)),
-        *((back(step), (ref,)) for ref, step, _ in edges(0)),
-        *((back(step), (ref,)) for ref, step, _ in adjoint_messages[6:]),
-    ):
-
-        @pl.when(jnp.logical_not(exists(step)))
-        def _():
-            for ref in refs:
-                ref[...] = jnp.zeros(ref.shape, jnp.float32)
+    spares = [
+        (*aside, no_tiles, no_rows)
+        for aside in (
+            (ar0_tiles, ar0_rows),
+            (ar1_tiles, ar1_rows),
+            (ad_tiles, ad_rows),
+            (ag0_tiles, ag0_rows),
+            (ag1_tiles, ag1_rows),
+        )
+    ]
+
+    def part(kind, *places):
+        return Part(kind, [(buffers[kind], at_row, fields) for buffers, at_row, fields in places])
+
+    r_xl = part(TILES, (first, 0, 1), (second, 0, 1))
+    r_xr = part(TILES, (first, 1, 1), (second, 1, 1))
+    r_zl = part(TILES, (first, 2, 3), (second, 2, 2))
+    r_zr = part(TILES, (first, 5, 5), (second, 4, 1))
+    r_yl = part(ROWS, (first, 0, 3), (second, 0, 2))
+    r_yr = part(ROWS, (first, 3, 5), (second, 2, 1))
+
+    def adjoint_exchange(r):
+        up, down = ((3, 5), (2, 1))[r]
+        return Exchange(
+            r,
+            (first, second)[r],
+            spares[r],
+            send_sem.at[r],
+            recv_sem.at[r],
+            (
+                (r_xl, (1, 0, 0), s_xr.at[r]),
+                (r_xr, (-1, 0, 0), s_xl.at[r]),
+                (r_zl, (0, 0, 1), s_zr.at[r, pl.ds(0, up)]),
+                (r_zr, (0, 0, -1), s_zl.at[r, pl.ds(0, down)]),
+                (r_yl, (0, 1, 0), s_yr.at[r, pl.ds(0, up)]),
+                (r_yr, (0, -1, 0), s_yl.at[r, pl.ds(0, down)]),
+            ),
+            at,
+            exists,
+        )
+
+    def forward_part(kind, at_row, fields):
+        return part(kind, (forward0, at_row, fields), (forward1, at_row, fields))
+
+    g_xl, g_xr = forward_part(TILES, 0, 1), forward_part(TILES, 1, 1)
+    g_zl, g_zr = forward_part(TILES, 2, 3), forward_part(TILES, 5, 3)
+    exz_mm, exz_pp = forward_part(TILES, 8, 1), forward_part(TILES, 9, 2)
+    exz_pm, exz_mp = forward_part(TILES, 11, 1), forward_part(TILES, 12, 1)
+    eyz_mm, eyz_pp = forward_part(TILES, 13, 1), forward_part(TILES, 14, 2)
+    eyz_pm, eyz_mp = forward_part(TILES, 16, 1), forward_part(TILES, 17, 1)
+    g_yl, g_yr = forward_part(ROWS, 0, 3), forward_part(ROWS, 3, 3)
+    exy_mm, exy_pp = forward_part(ROWS, 6, 1), forward_part(ROWS, 7, 2)
+    exy_pm, exy_mp = forward_part(ROWS, 9, 1), forward_part(ROWS, 10, 1)
+
+    def forward_exchange(e):
+        return Exchange(
+            e,
+            (forward0, forward1)[e],
+            spares[3 + e],
+            fsend_sem.at[e],
+            frecv_sem.at[e],
+            (
+                (g_xl, (1, 0, 0), f_xr.at[e]),
+                (g_xr, (-1, 0, 0), f_xl.at[e]),
+                (g_yl, (0, 1, 0), f_yr.at[e, pl.ds(0, 3)]),
+                (g_yr, (0, -1, 0), f_yl.at[e, pl.ds(0, 3)]),
+                (g_zl, (0, 0, 1), f_zr.at[e, pl.ds(0, 3)]),
+                (g_zr, (0, 0, -1), f_zl.at[e, pl.ds(0, 3)]),
+                (exy_mm, (1, 1, 0), f_yr.at[e, pl.ds(0, 1)]),
+                (exy_pp, (-1, -1, 0), f_yl.at[e, pl.ds(2, 2)]),
+                (exy_pm, (-1, 1, 0), f_yr.at[e, pl.ds(1, 1)]),
+                (exy_mp, (1, -1, 0), f_yl.at[e, pl.ds(4, 1)]),
+                (exz_mm, (1, 0, 1), f_zr.at[e, pl.ds(0, 1)]),
+                (exz_pp, (-1, 0, -1), f_zl.at[e, pl.ds(2, 2)]),
+                (exz_pm, (-1, 0, 1), f_zr.at[e, pl.ds(1, 1)]),
+                (exz_mp, (1, 0, -1), f_zl.at[e, pl.ds(6, 1)]),
+                (eyz_mm, (0, 1, 1), f_zr.at[e, pl.ds(1, 1)]),
+                (eyz_pp, (0, -1, -1), f_zl.at[e, pl.ds(4, 2)]),
+                (eyz_pm, (0, -1, 1), f_zr.at[e, pl.ds(0, 1)]),
+                (eyz_mp, (0, 1, -1), f_zl.at[e, pl.ds(6, 1)]),
+            ),
+            at,
+            exists,
+        )
+
+    d_xl, d_xr = part(TILES, (last_one, 0, 1)), part(TILES, (last_one, 1, 1))
+    d_zl, d_zr = part(TILES, (last_one, 2, 3)), part(TILES, (last_one, 5, 3))
+    vxz_pm, vxz_mp = part(TILES, (last_one, 8, 1)), part(TILES, (last_one, 9, 1))
+    vyz_pm, vyz_mp = part(TILES, (last_one, 10, 1)), part(TILES, (last_one, 11, 1))
+    d_yl, d_yr = part(ROWS, (last_one, 0, 3)), part(ROWS, (last_one, 3, 3))
+    vxy_pm, vxy_mp = part(ROWS, (last_one, 6, 1)), part(ROWS, (last_one, 7, 1))
+    last_exchange = Exchange(
+        0,
+        last_one,
+        spares[2],
+        send_sem.at[2],
+        recv_sem.at[2],
+        (
+            (d_xl, (1, 0, 0), c_xr),
+            (d_xr, (-1, 0, 0), c_xl),
+            (d_yl, (0, 1, 0), c_yr),
+            (d_yr, (0, -1, 0), c_yl),
+            (d_zl, (0, 0, 1), c_zr),
+            (d_zr, (0, 0, -1), c_zl),
+            (vxy_pm, (-1, 1, 0), c_yr.at[pl.ds(0, 1)]),
+            (vxy_mp, (1, -1, 0), c_yl.at[pl.ds(0, 1)]),
+            (vxz_pm, (-1, 0, 1), c_zr.at[pl.ds(0, 1)]),
+            (vxz_mp, (1, 0, -1), c_zl.at[pl.ds(0, 1)]),
+            (vyz_pm, (0, -1, 1), c_zr.at[pl.ds(0, 1)]),
+            (vyz_mp, (0, 1, -1), c_zl.at[pl.ds(1, 1)]),
+        ),
+        at,
+        exists,
+    )
 
     lam, mu, buoy = params.at[0], params.at[1], params.at[2]
     av, as_ = [adj.at[i] for i in range(3)], [adj.at[3 + i] for i in range(6)]
 
-    ends = (
-        ((1, 0, 0), s_xr, r_xl),
-        ((-1, 0, 0), s_xl, r_xr),
-        ((0, 1, 0), s_yr, r_yl),
-        ((0, -1, 0), s_yl, r_yr),
-        ((0, 0, 1), s_zr, r_zl),
-        ((0, 0, -1), s_zl, r_zr),
-    )
-
-    def face(r, d, fields):
-        step, source, target = ends[d]
-        if d < 2:
-            src, dst = source.at[r], target.at[r]
-        else:
-            src, dst = source.at[r, pl.ds(0, fields)], target.at[r, pl.ds(0, fields)]
-        copy = pltpu.make_async_remote_copy(
-            src_ref=src,
-            dst_ref=dst,
-            send_sem=send_sem.at[d],
-            recv_sem=recv_sem.at[r % 2, d],
-            device_id=at(step),
-            device_id_type=MESH,
-        )
-        return copy, exists(step), exists(back(step))
-
-    COUNTS = ((3, 5), (2, 1))
-
-    def sent(r):
-        for d in range(6):
-            copy, goes, _ = face(r, d, COUNTS[r][d % 2])
-
-            @pl.when(goes)
-            def _():
-                copy.wait_send()
-
     def fill_faces(r, up, down):
         (xu, yu, zu), (xd, yd, zd) = up, down
-        s_xr[r] = pack_columns(xu, 127)
-        s_xl[r] = pack_columns(xd, 0)
+        s_xr[r, 0] = pack_columns(xu, 127)
+        s_xl[r, 0] = pack_columns(xd, 0)
         for i, f in enumerate(zu):
             s_zr[r, i] = f[7]
         for i, f in enumerate(zd):
@@ -347,14 +433,6 @@
         for i, f in enumerate(yd):
             s_yl[r, i] = f[:, 0:1, :]
 
-    def start_faces(r):
-        for d in (0, 1, 4, 5, 2, 3):
-            copy, goes, _ = face(r, d, COUNTS[r][d % 2])
-
-            @pl.when(goes)
-            def _():
-                copy.start()
-
     def fill_velocity():
         v, b, l, m = [f[...] for f in av], buoy[...], lam[...], mu[...]
         more, most = (b, m), (b, l, m)
@@ -364,13 +442,9 @@
             ((v[1], v[2], *most), (v[0], v[2], *most), (v[0], v[1], *most)),
         )
 
-    def send_velocity(r):
-        start_faces(r)
-
     def send_stress(r, s):
-        sent(r - 1)
         fill_faces(r, ((s[3], s[4]), (s[3], s[5]), (s[4], s[5])), ((s[0],), (s[1],), (s[2],)))
-        start_faces(r)
+        adjoint_exchange(r).start(*range(6))
 
     for name in ("peer", "slot", "own_s"):
         loads[name].wait()
@@ -421,7 +495,7 @@
     pltpu.make_async_copy(params, params, in_sem.at[1]).wait()
     fill_velocity()
     pl.semaphore_wait(barrier, around + 3)
-    send_velocity(0)
+    adjoint_exchange(0).start(*range(6))
     restore(stage_s, got_s, 0)
 
     for step in GREETED:
@@ -432,14 +506,6 @@
 
     loads["own_v"].wait()
     stage(own_v, stage_v, got_v)
-
-    def receive(r):
-        for d in range(6):
-            copy, _, comes = face(r, d, COUNTS[r][d % 2])
-
-            @pl.when(comes)
-            def _():
-                copy.wait_recv()
 
     def stress_faces(r):
         xl, xr = r_xl[r], r_xr[r]
@@ -469,88 +535,35 @@
             ("zr", 1): r_zr[r, 1],
         }
 
-    fends = (
-        (g_xl, (1, 0, 0), f_xr),
-        (g_xr, (-1, 0, 0), f_xl),
-        (g_yl, (0, 1, 0), f_yr),
-        (g_yr, (0, -1, 0), f_yl),
-        (g_zl, (0, 0, 1), f_zr),
-        (g_zr, (0, 0, -1), f_zl),
-    )
-
-    def message(e, n):
-        if n < 6:
-            target, step, source = fends[n]
-            src = source.at[e] if n < 2 else source.at[e, pl.ds(0, 3)]
-        else:
-            target, step, src = edges(e)[n - 6]
-        copy = pltpu.make_async_remote_copy(
-            src_ref=src,
-            dst_ref=target.at[e],
-            send_sem=fsend_sem.at[n],
-            recv_sem=frecv_sem.at[e, n],
-            device_id=at(step),
-            device_id_type=MESH,
-        )
-        return copy, exists(step), exists(back(step))
-
-    def forward_start(e, n):
-        copy, goes, _ = message(e, n)
-
-        @pl.when(goes)
-        def _():
-            copy.start()
-
-    def forward_sent(e):
-        for n in range(18):
-            copy, goes, _ = message(e, n)
-
-            @pl.when(goes)
-            def _():
-                copy.wait_send()
-
-    def forward_receive(e):
-        for n in range(18):
-            copy, _, comes = message(e, n)
-
-            @pl.when(comes)
-            def _():
-                copy.wait_recv()
-
     def forward_edges(e):
-        if e > 0:
-            forward_sent(e - 1)
+        exchange = forward_exchange(e)
         f_yr[e, 0] = fs[3, :, 7:8, :]
         f_yr[e, 1] = fs[5, :, 7:8, :]
         for i, f in ((2, 1), (3, 0), (4, 4)):
             f_yl[e, i] = fs[f, :, 0:1, :]
-        for n in (6, 7, 8, 9):
-            forward_start(e, n)
+        exchange.start(6, 7, 8, 9)
         f_zr[e, 0] = fs[4, 7]
         f_zr[e, 1] = fs[5, 7]
         for i, f in ((2, 2), (3, 0), (4, 2), (5, 1), (6, 3)):
             f_zl[e, i] = fs[f, 0]
-        for n in range(10, 18):
-            forward_start(e, n)
+        exchange.start(*range(10, 18))
 
     def forward_faces(e):
+        exchange = forward_exchange(e)
         rates = velocity_rates([fs[i] for i in range(6)], buoy[...], Zeros())
         for i in range(3):
             fv[i] = fv[i] + rates[i]
-        f_xr[e] = pack_columns((fs[3], fs[4], fv[0]), 127)
-        f_xl[e] = pack_columns((fs[0], fv[1], fv[2]), 0)
-        forward_start(e, 0)
-        forward_start(e, 1)
+        f_xr[e, 0] = pack_columns((fs[3], fs[4], fv[0]), 127)
+        f_xl[e, 0] = pack_columns((fs[0], fv[1], fv[2]), 0)
+        exchange.start(0, 1)
         f_zr[e, 2] = fv[2, 7]
         f_zl[e, 0] = fv[0, 0]
         f_zl[e, 1] = fv[1, 0]
-        forward_start(e, 4)
-        forward_start(e, 5)
+        exchange.start(4, 5)
         f_yr[e, 2] = fv[1, :, 7:8, :]
         f_yl[e, 0] = fv[0, :, 0:1, :]
         f_yl[e, 1] = fv[2, :, 0:1, :]
-        forward_start(e, 2)
-        forward_start(e, 3)
+        exchange.start(2, 3)
 
     def forward_step(e):
         xl, xr = g_xl[e], g_xr[e]
@@ -618,69 +631,33 @@
         fv[2, 7] = fv[2, 7] + buoy[7] * g_zr[e, 2]
         return stress_rates([fv[i] for i in range(3)], lam[...], mu[...], h)
 
-    def adjoint_message(n):
-        target, step, source = adjoint_messages[n]
-        copy = pltpu.make_async_remote_copy(
-            src_ref=source,
-            dst_ref=target,
-            send_sem=asend_sem.at[n],
-            recv_sem=arecv_sem.at[n],
-            device_id=at(step),
-            device_id_type=MESH,
-        )
-        return copy, exists(step), exists(back(step))
-
-    def adjoint_start(*which):
-        for n in which:
-            copy, goes, _ = adjoint_message(n)
-
-            @pl.when(goes)
-            def _():
-                copy.start()
-
-    def adjoint_sent():
-        for n in range(12):
-            copy, goes, _ = adjoint_message(n)
-
-            @pl.when(goes)
-            def _():
-                copy.wait_send()
-
-    def adjoint_receive():
-        for n in range(12):
-            copy, _, comes = adjoint_message(n)
-
-            @pl.when(comes)
-            def _():
-                copy.wait_recv()
-
     def adjoint_send():
         c_yr[0] = av[1][:, 7:8, :]
         c_yl[0] = av[0][:, 0:1, :]
         c_yl[1] = av[2][:, 0:1, :]
-        adjoint_start(6, 7)
+        last_exchange.start(6, 7)
         c_zr[0] = av[2][7]
         c_zl[0] = av[0][0]
         c_zl[1] = av[1][0]
-        adjoint_start(8, 9, 10, 11)
+        last_exchange.start(8, 9, 10, 11)
         v = [f[...] for f in av]
         rates = stress_rates(v, lam[...], mu[...], Zeros())
         s = [a0[i] - rates[i] for i in range(6)]
-        c_xr[...] = pack_columns((v[0], s[3], s[4]), 127)
-        c_xl[...] = pack_columns((v[1], v[2], s[0]), 0)
-        adjoint_start(0, 1)
+        c_xr[0] = pack_columns((v[0], s[3], s[4]), 127)
+        c_xl[0] = pack_columns((v[1], v[2], s[0]), 0)
+        last_exchange.start(0, 1)
         c_zr[1] = s[4][7]
         c_zr[2] = s[5][7]
         c_zl[2] = s[2][0]
-        adjoint_start(4, 5)
+        last_exchange.start(4, 5)
         c_yr[1] = s[3][:, 7:8, :]
         c_yr[2] = s[5][:, 7:8, :]
         c_yl[2] = s[1][:, 0:1, :]
-        adjoint_start(2, 3)
+        last_exchange.start(2, 3)
 
     def adjoint_step():
         v = [f[...] for f in av]
-        xl, xr = d_xl[...], d_xr[...]
+        xl, xr = d_xl[0], d_xr[0]
         lane2, row2 = iota2(1), iota2(0)
         all3 = (8, 8, 128)
         z1 = lax.broadcasted_iota(jnp.int32, (8, 1, 128), 0)
@@ -689,18 +666,18 @@
             ("xl", 0): unpack_columns(xl, 0, 0),
             ("xr", 1): unpack_columns(xr, 0, 127),
             ("xr", 2): unpack_columns(xr, 1, 127),
-            ("yl", 1): d_yl[0],
-            ("yr", 0): d_yr[0],
-            ("yr", 2): d_yr[1],
-            ("zl", 2): d_zl[0],
-            ("zr", 0): d_zr[0],
-            ("zr", 1): d_zr[1],
+            ("yl", 1): d_yl[0, 0],
+            ("yr", 0): d_yr[0, 0],
+            ("yr", 2): d_yr[0, 1],
+            ("zl", 2): d_zl[0, 0],
+            ("zr", 0): d_zr[0, 0],
+            ("zr", 1): d_zr[0, 1],
         }
         rates = stress_rates(v, lam[...], mu[...], h)
         s = [a0[i] - rates[i] for i in range(6)]
 
-        xy_pm, xy_mp = pltpu.roll(vxy_pm[...], 127, 2), pltpu.roll(vxy_mp[...], 1, 2)
-        xz_pm, xz_mp = pltpu.roll(vxz_pm[...], 127, 1), pltpu.roll(vxz_mp[...], 1, 1)
+        xy_pm, xy_mp = pltpu.roll(vxy_pm[0], 127, 2), pltpu.roll(vxy_mp[0], 1, 2)
+        xz_pm, xz_mp = pltpu.roll(vxz_pm[0], 127, 1), pltpu.roll(vxz_mp[0], 1, 1)
 
         def row(at_y, face):
             return jnp.where(iota3(1) == at_y, jnp.broadcast_to(face, all3), 0.0)
@@ -720,26 +697,33 @@
         g["xl", 4] = unpack_columns(xl, 2, 0) - mx[0] * (v[2] + layer(7, xz_mp))
         g["xr", 0] = unpack_columns(xr, 2, 127) + both * v[0] + lx[...] * (row(0, xy_pm) + layer(0, xz_pm))
         mu_m, lam_p, mu_p = r_yl[0, 2], r_yr[0, 3], r_yr[0, 4]
-        g["yl", 3] = d_yl[1] - mu_m * (v[0][:, 0:1, :] + jnp.where(lane1 == 127, xy_pm, 0.0))
-        g["yl", 5] = d_yl[2] - mu_m * (v[2][:, 0:1, :] + y_layer(7, vyz_mp[...], 7))
+        g["yl", 3] = d_yl[0, 1] - mu_m * (v[0][:, 0:1, :] + jnp.where(lane1 == 127, xy_pm, 0.0))
+        g["yl", 5] = d_yl[0, 2] - mu_m * (v[2][:, 0:1, :] + y_layer(7, vyz_mp[0], 7))
         g["yr", 1] = (
-            d_yr[2]
+            d_yr[0, 2]
             + (lam_p + 2.0 * mu_p) * v[1][:, 7:8, :]
-            + lam_p * (jnp.where(lane1 == 0, xy_mp, 0.0) + y_layer(0, vyz_pm[...], 0))
+            + lam_p * (jnp.where(lane1 == 0, xy_mp, 0.0) + y_layer(0, vyz_pm[0], 0))
         )
         mu_m, lam_p, mu_p = r_zl[0, 2], r_zr[0, 3], r_zr[0, 4]
-        g["zl", 4] = d_zl[1] - mu_m * (v[0][0] + jnp.where(lane2 == 127, xz_pm, 0.0))
-        g["zl", 5] = d_zl[2] - mu_m * (v[1][0] + y_edge(vyz_pm[...], 7, 0))
+        g["zl", 4] = d_zl[0, 1] - mu_m * (v[0][0] + jnp.where(lane2 == 127, xz_pm, 0.0))
+        g["zl", 5] = d_zl[0, 2] - mu_m * (v[1][0] + y_edge(vyz_pm[0], 7, 0))
         g["zr", 2] = (
-            d_zr[2]
+            d_zr[0, 2]
             + (lam_p + 2.0 * mu_p) * v[2][7]
-            + lam_p * (jnp.where(lane2 == 0, xz_mp, 0.0) + y_edge(vyz_mp[...], 0, 7))
+            + lam_p * (jnp.where(lane2 == 0, xz_mp, 0.0) + y_edge(vyz_mp[0], 0, 7))
         )
         for i in range(6):
             adj_out[3 + i] = s[i]
         rates = velocity_rates(s, buoy[...], g)
         for i in range(3):
             adj_out[i] = v[i] - rates[i]
+
+    restore(stage_v, got_v, 1)
+    no_tiles[...] = jnp.zeros(no_tiles.shape, jnp.float32)
+    no_rows[...] = jnp.zeros(no_rows.shape, jnp.float32)
+    exchanges = (adjoint_exchange(0), adjoint_exchange(1), last_exchange, forward_exchange(0), forward_exchange(1))
+    for exchange in exchanges:
+        exchange.prepare()
 
     for name in ("rec", "traces", "plan"):
         loads[name].wait()
@@ -769,14 +753,13 @@
         counted = counted + jnp.where(flat == t_src[j], 1.0, 0.0)
     hits[...] = counted
 
-    restore(stage_v, got_v, 1)
 
     restored(got_s, 0)
     for p in range(8):
         fs[:, p] = got_s[where_is[p]].astype(jnp.float32)
     pl.semaphore_wait(ready, around)
     forward_edges(0)
-    receive(0)
+    adjoint_exchange(0).receive()
     rates = stress_rates([f[...] for f in av], lam[...], mu[...], velocity_faces(0))
     for i in range(6):
         as_[i][...] = a1[i] - rates[i]
@@ -792,7 +775,7 @@
         fv[:, p] = got_v[where_is[p]].astype(jnp.float32)
     forward_faces(0)
 
-    receive(1)
+    adjoint_exchange(1).receive()
     rates = velocity_rates([f[...] for f in as_], buoy[...], stress_faces(1))
     for i in range(3):
         av[i][...] = av[i][...] - rates[i]
@@ -802,7 +785,7 @@
         a0[i] = as_[i][...]
     adjoint_send()
 
-    forward_receive(0)
+    forward_exchange(0).receive()
     rates = forward_step(0)
     pulse = hits[...] * t_wav[t_plan[0]]
     for i in range(3):
@@ -821,21 +804,21 @@
     il_out[...] = by_lambda
     im_out[...] = by_mu
 
-    adjoint_receive()
+    last_exchange.receive()
     adjoint_step()
-    sent(1)
-    adjoint_sent()
+    for exchange in exchanges[:4]:
+        exchange.sent()
     for n, staged in enumerate((stage_s, stage_v)):
         pltpu.make_async_copy(staged, staged, rs_send.at[n]).wait()
 
-    forward_receive(1)
+    forward_exchange(1).receive()
     rates = forward_step(1)
     pulse = hits[...] * t_wav[t_plan[1]]
     last = [fs[i] + rates[i] + pulse for i in range(3)] + [fs[i] + rates[i] for i in range(3, 6)]
     by_lambda, by_mu = image(last, a1)
     il_out[...] += by_lambda
     im_out[...] += by_mu
-    forward_sent(1)
+    forward_exchange(1).sent()
 
 
 def write_out(adj, il, im, adj_out, il_out, im_out, sem):
@@ -884,20 +867,17 @@
             vmem(brick, f32),
         ]
         row, tile = (8, 1, 128), (8, 128)
-        for _ in range(2):
-            scratch += [vmem((2,) + tile, f32)] * 2 + [vmem((2, 5) + row, f32)] * 2 + [vmem((2, 5) + tile, f32)] * 2
-        for down_y, down_z in ((5, 7), (3, 3)):
-            received = down_y == 3
-            scratch += [vmem((2,) + tile, f32)] * 2
-            scratch += [vmem((2, 3 if received else 5) + row, f32), vmem((2, 3) + row, f32)]
-            scratch += [vmem((2, 3 if received else 7) + tile, f32), vmem((2, 3) + tile, f32)]
-        for _ in range(2):
-            scratch += [vmem(tile, f32)] * 2 + [vmem((3,) + row, f32)] * 2 + [vmem((3,) + tile, f32)] * 2
-        scratch += [vmem(row, f32)] * 2 + [vmem(tile, f32)] * 4
-        for shape in (row, tile, tile):
-            scratch += [vmem((2, fields) + shape, f32) for fields in (1, 2, 1, 1)]
+        scratch += [vmem((2, 1) + tile, f32)] * 2 + [vmem((2, 5) + row, f32)] * 2 + [vmem((2, 5) + tile, f32)] * 2
+        scratch += [vmem((10,) + tile, f32), vmem((8,) + row, f32), vmem((5,) + tile, f32), vmem((3,) + row, f32)]
+        scratch += [vmem((2, 1) + tile, f32)] * 2 + [vmem((2, 5) + row, f32), vmem((2, 3) + row, f32)]
+        scratch += [vmem((2, 7) + tile, f32), vmem((2, 3) + tile, f32)]
+        scratch += [vmem((18,) + tile, f32), vmem((11,) + row, f32)] * 2
+        scratch += [vmem((1,) + tile, f32)] * 2 + [vmem((3,) + row, f32)] * 2 + [vmem((3,) + tile, f32)] * 2
+        scratch += [vmem((12,) + tile, f32), vmem((8,) + row, f32)]
+        for tiles, rows in ((10, 8), (5, 3), (12, 8), (18, 11), (18, 11), (5, 5)):
+            scratch += [vmem((tiles,) + tile, f32), vmem((rows,) + row, f32)]
         dma = pltpu.SemaphoreType.DMA
-        scratch += [dma((11,)), dma((6,)), dma((2, 6)), dma((12,)), dma((12,)), dma((18,)), dma((2, 18)), dma((2,)), dma((2,)), pltpu.SemaphoreType.REGULAR]
+        scratch += [dma((11,)), dma((3, 2)), dma((3, 2)), dma((2, 2)), dma((2, 2)), dma((2,)), dma((2,)), pltpu.SemaphoreType.REGULAR]
         shapes = ((9,) + brick, brick, brick)
         results = pl.pallas_call(
             functools.partial(kernel, sizes),

time: 23.5 us -> 22.8 us (0.970)
  Pallas kernels: 22.8 us -> 22 us
    pallas_call x1, Pallas kernels: 22 us -> 21.3 us  [on_device(): pl.pallas_call(functools.partial(kernel, sizes), out_shape=tuple((pltpu.V...]
where the time goes in v7:
time: 22.8 us; the launch traced here: 22.7 us
  Pallas kernels  22 us (96%)
  between operations  0.64 us (3%)
    pallas_call x1, Pallas kernels, on_device(): pl.pallas_call(functools.partial(kernel, sizes), out_shape=tuple((pltpu.V...  21.3 us
    pallas_call x1, Pallas kernels, on_device(): pl.pallas_call(write_out, out_shape=tuple((jax.ShapeDtypeStruct(shape, f3...  0.75 us

profile of v7, /device:TPU:34, one launch (start us, length us, event | category | flops | bytes accessed | tf_op | source)
XLA Modules:
  0.0 22.7 jit_solution(6873444022578426450)
XLA Ops:
  0.6 21.3 %window.1 = (f32[9,8,8,128]{3,2,1,0:T(8,128)S(1)}, f32[8,8,128]{2,1,0:T(8,128)S(1)}, f32[8,8,128]{2,1,0:T(8,128)S(1)}) custom-call(bf16[8,9,1,8,128]{4,3,2,1,0:T(8,128)(2,1)} %store.1, s32[1,1,4,8]{3,2,1,0:T(4,128)} %hpeer.1, s32[1,1,4,8]{3,2,1,0:T(4,128)} %hslot.1, f32[9,8,8,128]{3,2,1,0:T(8,128)} %adj_in.1, f32[8,8,128]{2,1,0:T(8,128)} %lam_in.1, ...), custom_call_target="tpu_custom_call" | custom-call | tf_op jit(solution)/shard_map/window/pallas_call | solution.py:882
  21.9 0.8 %write_out.1 = (f32[9,8,8,128]{3,2,1,0:T(8,128)}, f32[8,8,128]{2,1,0:T(8,128)}, f32[8,8,128]{2,1,0:T(8,128)}) custom-call(f32[9,8,8,128]{3,2,1,0:T(8,128)S(1)} %get-tuple-element.6.adj, f32[8,8,128]{2,1,0:T(8,128)S(1)} %get-tuple-element.7.il, f32[8,8,128]{2,1,0:T(8,128)S(1)} %get-tuple-element.8.im), custom_call_target="tpu_custom_call" | custom-call | tf_op jit(solution)/shard_map/write_out/pallas_call | solution.py:893

commit v8 on v7

--- a/solution.py
+++ b/solution.py
@@ -256,22 +256,6 @@
     def at(step):
         return {axis: index[axis] + d for axis, d in zip(axes, step) if d}
 
-    barrier = pltpu.get_barrier_semaphore()
-
-    def greet(where):
-        pl.semaphore_signal(barrier, inc=1, device_id=where, device_id_type=MESH)
-
-    around = jnp.int32(0)
-    for step in GREETED:
-
-        @pl.when(exists(step))
-        def _():
-            greet(at(step))
-
-        around = around + exists(step).astype(jnp.int32)
-    for d in (1, 2, 3):
-        greet({"gz": lax.rem(gz + d, 4)})
-
     def local(src, dst, n):
         return pltpu.make_async_copy(src, dst, in_sem.at[n])
 
@@ -279,8 +263,9 @@
         peer=local(hpeer.at[0, 0], t_peer, 7),
         slot=local(hslot.at[0, 0], t_slot, 8),
         own_s=local(store.at[:, pl.ds(3, 6), 0], own_s, 9),
+        av=local(adj_in.at[pl.ds(0, 3)], adj.at[pl.ds(0, 3)], 0),
         own_v=local(store.at[:, pl.ds(0, 3), 0], own_v, 10),
-        adj=local(adj_in, adj, 0),
+        as_=local(adj_in.at[pl.ds(3, 6)], adj.at[pl.ds(3, 6)], 11),
         lam=local(lam_in, params.at[0], 1),
         mu=local(mu_in, params.at[1], 1),
         buoy=local(buoy_in, params.at[2], 1),
@@ -290,8 +275,28 @@
         wav=local(wav_in, t_wav, 5),
         src=local(src_in.at[0, 0, 0], t_src, 6),
     )
-    for copy in loads.values():
-        copy.start()
+    for name in ("own_s", "peer", "slot"):
+        loads[name].start()
+
+    barrier = pltpu.get_barrier_semaphore()
+
+    def greet(where):
+        pl.semaphore_signal(barrier, inc=1, device_id=where, device_id_type=MESH)
+
+    around = jnp.int32(0)
+    for step in GREETED:
+
+        @pl.when(exists(step))
+        def _():
+            greet(at(step))
+
+        around = around + exists(step).astype(jnp.int32)
+    for d in (1, 2, 3):
+        greet({"gz": lax.rem(gz + d, 4)})
+
+    for name, copy in loads.items():
+        if name not in ("own_s", "peer", "slot"):
+            copy.start()
 
     TILES, ROWS = 0, 1
     first, second, forward0, forward1, last_one = (
@@ -318,13 +323,13 @@
 
     r_xl = part(TILES, (first, 0, 1), (second, 0, 1))
     r_xr = part(TILES, (first, 1, 1), (second, 1, 1))
-    r_zl = part(TILES, (first, 2, 3), (second, 2, 2))
-    r_zr = part(TILES, (first, 5, 5), (second, 4, 1))
-    r_yl = part(ROWS, (first, 0, 3), (second, 0, 2))
-    r_yr = part(ROWS, (first, 3, 5), (second, 2, 1))
+    r_zl = part(TILES, (first, 2, 1), (second, 2, 4))
+    r_zr = part(TILES, (first, 3, 2), (second, 6, 4))
+    r_yl = part(ROWS, (first, 0, 1), (second, 0, 4))
+    r_yr = part(ROWS, (first, 1, 2), (second, 4, 4))
 
     def adjoint_exchange(r):
-        up, down = ((3, 5), (2, 1))[r]
+        up, down = ((1, 2), (4, 4))[r]
         return Exchange(
             r,
             (first, second)[r],
@@ -434,16 +439,16 @@
             s_yl[r, i] = f[:, 0:1, :]
 
     def fill_velocity():
-        v, b, l, m = [f[...] for f in av], buoy[...], lam[...], mu[...]
-        more, most = (b, m), (b, l, m)
+        v = [f[...] for f in av]
+        fill_faces(0, ((v[0],), (v[1],), (v[2],)), ((v[1], v[2]), (v[0], v[2]), (v[0], v[1])))
+
+    def send_stress(r, s):
+        b, l, m = buoy[...], lam[...], mu[...]
         fill_faces(
-            0,
-            ((v[0], *more), (v[1], *more), (v[2], *more)),
-            ((v[1], v[2], *most), (v[0], v[2], *most), (v[0], v[1], *most)),
-        )
-
-    def send_stress(r, s):
-        fill_faces(r, ((s[3], s[4]), (s[3], s[5]), (s[4], s[5])), ((s[0],), (s[1],), (s[2],)))
+            r,
+            ((s[3], s[4], b, m), (s[3], s[5], b, m), (s[4], s[5], b, m)),
+            ((s[0], b, l, m), (s[1], b, l, m), (s[2], b, l, m)),
+        )
         adjoint_exchange(r).start(*range(6))
 
     for name in ("peer", "slot", "own_s"):
@@ -467,7 +472,8 @@
                     got[3 * CAP + j] = own[slots[d][j]]
 
     def restore(staged, got, n):
-        for d in (2, 1, 3):
+        odd = lax.rem(gz, 2)
+        for d in (2, 3 - 2 * odd, 1 + 2 * odd):
             rows = pl.ds((d - 1) * CAP, CAP)
             pltpu.make_async_remote_copy(
                 src_ref=staged.at[rows],
@@ -491,12 +497,12 @@
         seen = seen + lax.shift_left(jnp.int32(1), at_digit)
 
     stage(own_s, stage_s, got_s)
-    loads["adj"].wait()
-    pltpu.make_async_copy(params, params, in_sem.at[1]).wait()
+    loads["av"].wait()
     fill_velocity()
     pl.semaphore_wait(barrier, around + 3)
-    adjoint_exchange(0).start(*range(6))
+    adjoint_exchange(0).start(0, 1)
     restore(stage_s, got_s, 0)
+    adjoint_exchange(0).start(2, 3, 4, 5)
 
     for step in GREETED:
 
@@ -600,7 +606,7 @@
         def y_layer(at_z, tile, at_y):
             return jnp.where(z1 == at_z, jnp.broadcast_to(tile[at_y : at_y + 1, :][None], (8, 1, 128)), 0.0)
 
-        bym, byp = r_yl[0, 1], r_yr[0, 2]
+        bym, byp = r_yl[1, 2], r_yr[1, 1]
         h["yl", 1] = g_yl[e, 2] + bym * (
             fs[1, :, 0:1, :] - jnp.where(lane1 == 0, mm, 0.0) - y_layer(0, eyz_mm[e, 0], 7)
         )
@@ -614,7 +620,7 @@
         def y_edge(tile, at_y, from_y):
             return jnp.where(row2 == at_y, jnp.broadcast_to(tile[from_y : from_y + 1, :], (8, 128)), 0.0)
 
-        bzm, bzp = r_zl[0, 1], r_zr[0, 2]
+        bzm, bzp = r_zl[1, 2], r_zr[1, 1]
         h["zl", 2] = g_zl[e, 2] + bzm * (fs[2, 0] - jnp.where(lane2 == 0, zmm, 0.0) - y_edge(eyz_mm[e, 0], 0, 7))
         h["zr", 0] = g_zr[e, 0] + bzp * (
             jnp.where(lane2 == 127, zpp[1], 0.0) - fs[4, 7] - y_edge(eyz_mp[e, 0], 0, 7)
@@ -696,7 +702,7 @@
         g["xl", 3] = unpack_columns(xl, 1, 0) - mx[0] * (v[1] + row(7, xy_mp))
         g["xl", 4] = unpack_columns(xl, 2, 0) - mx[0] * (v[2] + layer(7, xz_mp))
         g["xr", 0] = unpack_columns(xr, 2, 127) + both * v[0] + lx[...] * (row(0, xy_pm) + layer(0, xz_pm))
-        mu_m, lam_p, mu_p = r_yl[0, 2], r_yr[0, 3], r_yr[0, 4]
+        mu_m, lam_p, mu_p = r_yl[1, 3], r_yr[1, 2], r_yr[1, 3]
         g["yl", 3] = d_yl[0, 1] - mu_m * (v[0][:, 0:1, :] + jnp.where(lane1 == 127, xy_pm, 0.0))
         g["yl", 5] = d_yl[0, 2] - mu_m * (v[2][:, 0:1, :] + y_layer(7, vyz_mp[0], 7))
         g["yr", 1] = (
@@ -704,7 +710,7 @@
             + (lam_p + 2.0 * mu_p) * v[1][:, 7:8, :]
             + lam_p * (jnp.where(lane1 == 0, xy_mp, 0.0) + y_layer(0, vyz_pm[0], 0))
         )
-        mu_m, lam_p, mu_p = r_zl[0, 2], r_zr[0, 3], r_zr[0, 4]
+        mu_m, lam_p, mu_p = r_zl[1, 3], r_zr[1, 2], r_zr[1, 3]
         g["zl", 4] = d_zl[0, 1] - mu_m * (v[0][0] + jnp.where(lane2 == 127, xz_pm, 0.0))
         g["zl", 5] = d_zl[0, 2] - mu_m * (v[1][0] + y_edge(vyz_pm[0], 7, 0))
         g["zr", 2] = (
@@ -725,8 +731,9 @@
     for exchange in exchanges:
         exchange.prepare()
 
-    for name in ("rec", "traces", "plan"):
+    for name in ("rec", "traces", "plan", "as_"):
         loads[name].wait()
+    pltpu.make_async_copy(params, params, in_sem.at[1]).wait()
     cells = rec[0]
     row_of, x_of = lax.shift_right_logical(cells, 7), lax.bitwise_and(cells, 127)
     rows = lax.broadcasted_iota(jnp.int32, (64, 64), 0)
@@ -764,11 +771,6 @@
     for i in range(6):
         as_[i][...] = a1[i] - rates[i]
     send_stress(1, [f[...] for f in as_])
-    bx[0] = unpack_columns(r_xl[0], 1, 0)
-    mx[0] = unpack_columns(r_xl[0], 2, 0)
-    bx[1] = unpack_columns(r_xr[0], 2, 127)
-    lx[...] = unpack_columns(r_xr[0], 3, 127)
-    mx[1] = unpack_columns(r_xr[0], 4, 127)
 
     restored(got_v, 1)
     for p in range(8):
@@ -784,6 +786,11 @@
     for i in range(3, 6):
         a0[i] = as_[i][...]
     adjoint_send()
+    bx[0] = unpack_columns(r_xl[1], 2, 0)
+    mx[0] = unpack_columns(r_xl[1], 3, 0)
+    bx[1] = unpack_columns(r_xr[1], 1, 127)
+    lx[...] = unpack_columns(r_xr[1], 2, 127)
+    mx[1] = unpack_columns(r_xr[1], 3, 127)
 
     forward_exchange(0).receive()
     rates = forward_step(0)
@@ -868,16 +875,16 @@
         ]
         row, tile = (8, 1, 128), (8, 128)
         scratch += [vmem((2, 1) + tile, f32)] * 2 + [vmem((2, 5) + row, f32)] * 2 + [vmem((2, 5) + tile, f32)] * 2
-        scratch += [vmem((10,) + tile, f32), vmem((8,) + row, f32), vmem((5,) + tile, f32), vmem((3,) + row, f32)]
+        scratch += [vmem((5,) + tile, f32), vmem((3,) + row, f32), vmem((10,) + tile, f32), vmem((8,) + row, f32)]
         scratch += [vmem((2, 1) + tile, f32)] * 2 + [vmem((2, 5) + row, f32), vmem((2, 3) + row, f32)]
         scratch += [vmem((2, 7) + tile, f32), vmem((2, 3) + tile, f32)]
         scratch += [vmem((18,) + tile, f32), vmem((11,) + row, f32)] * 2
         scratch += [vmem((1,) + tile, f32)] * 2 + [vmem((3,) + row, f32)] * 2 + [vmem((3,) + tile, f32)] * 2
         scratch += [vmem((12,) + tile, f32), vmem((8,) + row, f32)]
-        for tiles, rows in ((10, 8), (5, 3), (12, 8), (18, 11), (18, 11), (5, 5)):
+        for tiles, rows in ((5, 3), (10, 8), (12, 8), (18, 11), (18, 11), (5, 5)):
             scratch += [vmem((tiles,) + tile, f32), vmem((rows,) + row, f32)]
         dma = pltpu.SemaphoreType.DMA
-        scratch += [dma((11,)), dma((3, 2)), dma((3, 2)), dma((2, 2)), dma((2, 2)), dma((2,)), dma((2,)), pltpu.SemaphoreType.REGULAR]
+        scratch += [dma((12,)), dma((3, 2)), dma((3, 2)), dma((2, 2)), dma((2, 2)), dma((2,)), dma((2,)), pltpu.SemaphoreType.REGULAR]
         shapes = ((9,) + brick, brick, brick)
         results = pl.pallas_call(
             functools.partial(kernel, sizes),

time: 22.8 us -> 22.6 us (level)
  no operation moved by 1% of the time
where the time goes in v8:
time: 22.6 us; the launch traced here: 22.5 us
  Pallas kernels  21.9 us (97%)
  between operations  0.64 us (3%)
    pallas_call x1, Pallas kernels, on_device(): pl.pallas_call(functools.partial(kernel, sizes), out_shape=tuple((pltpu.V...  21.1 us
    pallas_call x1, Pallas kernels, on_device(): pl.pallas_call(write_out, out_shape=tuple((jax.ShapeDtypeStruct(shape, f3...  0.75 us

profile of v8, /device:TPU:34, one launch (start us, length us, event | category | flops | bytes accessed | tf_op | source)
XLA Modules:
  0.0 22.5 jit_solution(3053547198240654180)
XLA Ops:
  0.6 21.1 %window.1 = (f32[9,8,8,128]{3,2,1,0:T(8,128)S(1)}, f32[8,8,128]{2,1,0:T(8,128)S(1)}, f32[8,8,128]{2,1,0:T(8,128)S(1)}) custom-call(bf16[8,9,1,8,128]{4,3,2,1,0:T(8,128)(2,1)} %store.1, s32[1,1,4,8]{3,2,1,0:T(4,128)} %hpeer.1, s32[1,1,4,8]{3,2,1,0:T(4,128)} %hslot.1, f32[9,8,8,128]{3,2,1,0:T(8,128)} %adj_in.1, f32[8,8,128]{2,1,0:T(8,128)} %lam_in.1, ...), custom_call_target="tpu_custom_call" | custom-call | tf_op jit(solution)/shard_map/window/pallas_call | solution.py:889
  21.8 0.8 %write_out.1 = (f32[9,8,8,128]{3,2,1,0:T(8,128)}, f32[8,8,128]{2,1,0:T(8,128)}, f32[8,8,128]{2,1,0:T(8,128)}) custom-call(f32[9,8,8,128]{3,2,1,0:T(8,128)S(1)} %get-tuple-element.6.adj, f32[8,8,128]{2,1,0:T(8,128)S(1)} %get-tuple-element.7.il, f32[8,8,128]{2,1,0:T(8,128)S(1)} %get-tuple-element.8.im), custom_call_target="tpu_custom_call" | custom-call | tf_op jit(solution)/shard_map/write_out/pallas_call | solution.py:900

commit v9 on v8

--- a/solution.py
+++ b/solution.py
@@ -117,12 +117,12 @@
             @pl.when(jnp.logical_not(self.exists(step)))
             def _():
                 zeros = self.spare[2 + part.kind].at[pl.ds(0, count)]
-                pltpu.make_async_copy(zeros, aside, self.send.at[part.kind]).start()
+                pltpu.make_async_copy(zeros, aside, self.send).start()
 
             @pl.when(jnp.logical_not(self.exists(tuple(-d for d in step))))
             def _():
                 zeros = self.spare[2 + part.kind].at[pl.ds(0, count)]
-                pltpu.make_async_copy(zeros, target, self.recv.at[part.kind]).start()
+                pltpu.make_async_copy(zeros, target, self.recv).start()
 
     def start(self, *which):
         for n in which:
@@ -133,15 +133,16 @@
                 pltpu.make_async_remote_copy(
                     src_ref=source,
                     dst_ref=part.at(self.e),
-                    send_sem=self.send.at[part.kind],
-                    recv_sem=self.recv.at[part.kind],
+                    send_sem=self.send,
+                    recv_sem=self.recv,
                     device_id=self.to(step),
                     device_id_type=MESH,
                 ).start()
 
     def all_of(self, sems):
-        for kind, ref in enumerate(self.buffers):
-            pltpu.make_async_copy(ref, ref, sems.at[kind]).wait()
+        total = sum(ref.shape[0] for ref in self.buffers)
+        everything = self.spare[4].at[pl.ds(0, total)]
+        pltpu.make_async_copy(everything, everything, sems).wait()
 
     def sent(self):
         self.all_of(self.send)
@@ -230,6 +231,7 @@
     ag1_rows,
     no_tiles,
     no_rows,
+    meter,
     in_sem,
     send_sem,
     recv_sem,
@@ -308,7 +310,7 @@
     )
 
     spares = [
-        (*aside, no_tiles, no_rows)
+        (*aside, no_tiles, no_rows, meter)
         for aside in (
             (ar0_tiles, ar0_rows),
             (ar1_tiles, ar1_rows),
@@ -883,8 +885,9 @@
         scratch += [vmem((12,) + tile, f32), vmem((8,) + row, f32)]
         for tiles, rows in ((5, 3), (10, 8), (12, 8), (18, 11), (18, 11), (5, 5)):
             scratch += [vmem((tiles,) + tile, f32), vmem((rows,) + row, f32)]
+        scratch += [vmem((29,) + tile, f32)]
         dma = pltpu.SemaphoreType.DMA
-        scratch += [dma((12,)), dma((3, 2)), dma((3, 2)), dma((2, 2)), dma((2, 2)), dma((2,)), dma((2,)), pltpu.SemaphoreType.REGULAR]
+        scratch += [dma((12,)), dma((3,)), dma((3,)), dma((2,)), dma((2,)), dma((2,)), dma((2,)), pltpu.SemaphoreType.REGULAR]
         shapes = ((9,) + brick, brick, brick)
         results = pl.pallas_call(
             functools.partial(kernel, sizes),

time: 22.6 us -> 22.5 us (level)
  no operation moved by 1% of the time
where the time goes in v9:
time: 22.5 us; the launch traced here: 22.4 us
  Pallas kernels  21.8 us (97%)
  between operations  0.64 us (3%)
    pallas_call x1, Pallas kernels, on_device(): pl.pallas_call(functools.partial(kernel, sizes), out_shape=tuple((pltpu.V...  21.1 us
    pallas_call x1, Pallas kernels, on_device(): pl.pallas_call(write_out, out_shape=tuple((jax.ShapeDtypeStruct(shape, f3...  0.75 us

profile of v9, /device:TPU:34, one launch (start us, length us, event | category | flops | bytes accessed | tf_op | source)
XLA Modules:
  0.0 22.4 jit_solution(10240595923258329078)
XLA Ops:
  0.6 21.1 %window.1 = (f32[9,8,8,128]{3,2,1,0:T(8,128)S(1)}, f32[8,8,128]{2,1,0:T(8,128)S(1)}, f32[8,8,128]{2,1,0:T(8,128)S(1)}) custom-call(bf16[8,9,1,8,128]{4,3,2,1,0:T(8,128)(2,1)} %store.1, s32[1,1,4,8]{3,2,1,0:T(4,128)} %hpeer.1, s32[1,1,4,8]{3,2,1,0:T(4,128)} %hslot.1, f32[9,8,8,128]{3,2,1,0:T(8,128)} %adj_in.1, f32[8,8,128]{2,1,0:T(8,128)} %lam_in.1, ...), custom_call_target="tpu_custom_call" | custom-call | tf_op jit(solution)/shard_map/window/pallas_call | solution.py:892
  21.7 0.8 %write_out.1 = (f32[9,8,8,128]{3,2,1,0:T(8,128)}, f32[8,8,128]{2,1,0:T(8,128)}, f32[8,8,128]{2,1,0:T(8,128)}) custom-call(f32[9,8,8,128]{3,2,1,0:T(8,128)S(1)} %get-tuple-element.6.adj, f32[8,8,128]{2,1,0:T(8,128)S(1)} %get-tuple-element.7.il, f32[8,8,128]{2,1,0:T(8,128)S(1)} %get-tuple-element.8.im), custom_call_target="tpu_custom_call" | custom-call | tf_op jit(solution)/shard_map/write_out/pallas_call | solution.py:903

commit v10 on v9

--- a/solution.py
+++ b/solution.py
@@ -143,9 +143,6 @@
         total = sum(ref.shape[0] for ref in self.buffers)
         everything = self.spare[4].at[pl.ds(0, total)]
         pltpu.make_async_copy(everything, everything, sems).wait()
-
-    def sent(self):
-        self.all_of(self.send)
 
     def receive(self):
         self.all_of(self.recv)
@@ -235,7 +232,6 @@
     in_sem,
     send_sem,
     recv_sem,
-    fsend_sem,
     frecv_sem,
     rs_send,
     rs_recv,
@@ -336,7 +332,7 @@
             r,
             (first, second)[r],
             spares[r],
-            send_sem.at[r],
+            send_sem.at[0],
             recv_sem.at[r],
             (
                 (r_xl, (1, 0, 0), s_xr.at[r]),
@@ -368,7 +364,7 @@
             e,
             (forward0, forward1)[e],
             spares[3 + e],
-            fsend_sem.at[e],
+            send_sem.at[0],
             frecv_sem.at[e],
             (
                 (g_xl, (1, 0, 0), f_xr.at[e]),
@@ -404,7 +400,7 @@
         0,
         last_one,
         spares[2],
-        send_sem.at[2],
+        send_sem.at[0],
         recv_sem.at[2],
         (
             (d_xl, (1, 0, 0), c_xr),
@@ -815,8 +811,6 @@
 
     last_exchange.receive()
     adjoint_step()
-    for exchange in exchanges[:4]:
-        exchange.sent()
     for n, staged in enumerate((stage_s, stage_v)):
         pltpu.make_async_copy(staged, staged, rs_send.at[n]).wait()
 
@@ -827,7 +821,7 @@
     by_lambda, by_mu = image(last, a1)
     il_out[...] += by_lambda
     im_out[...] += by_mu
-    forward_exchange(1).sent()
+    pltpu.make_async_copy(meter, meter, send_sem.at[0]).wait()
 
 
 def write_out(adj, il, im, adj_out, il_out, im_out, sem):
@@ -885,9 +879,9 @@
         scratch += [vmem((12,) + tile, f32), vmem((8,) + row, f32)]
         for tiles, rows in ((5, 3), (10, 8), (12, 8), (18, 11), (18, 11), (5, 5)):
             scratch += [vmem((tiles,) + tile, f32), vmem((rows,) + row, f32)]
-        scratch += [vmem((29,) + tile, f32)]
+        scratch += [vmem((104,) + tile, f32)]
         dma = pltpu.SemaphoreType.DMA
-        scratch += [dma((12,)), dma((3,)), dma((3,)), dma((2,)), dma((2,)), dma((2,)), dma((2,)), pltpu.SemaphoreType.REGULAR]
+        scratch += [dma((12,)), dma((1,)), dma((3,)), dma((2,)), dma((2,)), dma((2,)), pltpu.SemaphoreType.REGULAR]
         shapes = ((9,) + brick, brick, brick)
         results = pl.pallas_call(
             functools.partial(kernel, sizes),

time: 22.5 us -> 22.5 us (level)
  no operation moved by 1% of the time
where the time goes in v10:
time: 22.5 us; the launch traced here: 22.4 us
  Pallas kernels  21.8 us (97%)
  between operations  0.64 us (3%)
    pallas_call x1, Pallas kernels, on_device(): pl.pallas_call(functools.partial(kernel, sizes), out_shape=tuple((pltpu.V...  21 us
    pallas_call x1, Pallas kernels, on_device(): pl.pallas_call(write_out, out_shape=tuple((jax.ShapeDtypeStruct(shape, f3...  0.75 us

profile of v10, /device:TPU:34, one launch (start us, length us, event | category | flops | bytes accessed | tf_op | source)
XLA Modules:
  0.0 22.4 jit_solution(5027894288805945950)
XLA Ops:
  0.6 21.0 %window.1 = (f32[9,8,8,128]{3,2,1,0:T(8,128)S(1)}, f32[8,8,128]{2,1,0:T(8,128)S(1)}, f32[8,8,128]{2,1,0:T(8,128)S(1)}) custom-call(bf16[8,9,1,8,128]{4,3,2,1,0:T(8,128)(2,1)} %store.1, s32[1,1,4,8]{3,2,1,0:T(4,128)} %hpeer.1, s32[1,1,4,8]{3,2,1,0:T(4,128)} %hslot.1, f32[9,8,8,128]{3,2,1,0:T(8,128)} %adj_in.1, f32[8,8,128]{2,1,0:T(8,128)} %lam_in.1, ...), custom_call_target="tpu_custom_call" | custom-call | tf_op jit(solution)/shard_map/window/pallas_call | solution.py:886
  21.7 0.8 %write_out.1 = (f32[9,8,8,128]{3,2,1,0:T(8,128)}, f32[8,8,128]{2,1,0:T(8,128)}, f32[8,8,128]{2,1,0:T(8,128)}) custom-call(f32[9,8,8,128]{3,2,1,0:T(8,128)S(1)} %get-tuple-element.6.adj, f32[8,8,128]{2,1,0:T(8,128)S(1)} %get-tuple-element.7.il, f32[8,8,128]{2,1,0:T(8,128)S(1)} %get-tuple-element.8.im), custom_call_target="tpu_custom_call" | custom-call | tf_op jit(solution)/shard_map/write_out/pallas_call | solution.py:897
